TPU v7x, 128 devices: a whole 4x4x4 slice. The times are simulated.
128 devices in a mesh: slab: 32 (over x, z, y_hi), dp: 4 (over y_lo, core).
Axes of the slice: x: 4, y: 4 (y_hi: 2, y_lo: 2; y = y_hi * 2 + y_lo), z: 4, core: 2. Of those that a mesh axis runs over, the one named last changes fastest.
Arguments:
- field: bfloat16 [4, 64, 32, 64, 512], P('dp', 'slab'), may hold values from -6 to 6
- cotangent: bfloat16 [4, 64, 32, 64, 512], P('dp', 'slab'), may hold values from -6 to 6
- spectral_weight: bfloat16 [96, 16, 16, 32, 64], P('slab'), may hold values from -9 to 9
- point_weight: bfloat16 [32, 32], replicated, may hold values from -1 to 1
- bias_term: float32 [32], replicated, may hold values from -3 to 3
Outputs:
- layer_out: bfloat16 [4, 64, 32, 64, 512], P('dp', 'slab')
- field_grad: bfloat16 [4, 64, 32, 64, 512], P('dp', 'slab')
- weight_grad: float32 [96, 16, 16, 32, 64], P('slab')
All inputs are finite; a program needn't handle non-finite values.
Results may differ from a plain program's by a relative error of at most 0.018.
Values may be sent and summed in bfloat16 or wider, within the bound.
No kernel may reach another device: no remote copies, remote signals or barrier semaphores. Data moves between devices by JAX's collectives and lax.ppermute only.
A program may use at most 128 MiB of HBM per device.

v0:
```python
import math
from functools import partial

import jax
import jax.numpy as jnp
import numpy as np
from jax import lax
from jax.experimental import pallas as pl
from jax.experimental.pallas import tpu as pltpu
from jax.sharding import PartitionSpec as P

X = 64
Y = 64
Z = 32
T_SIZE = 16
ZT = Z * T_SIZE
C = 32
MX = 16
MY = 16
MZ = 12
MT = 8
NQ = 3
ND = 32
SCALE = 1.0 / (X * Y * Z * T_SIZE)
BF = jnp.bfloat16
F32 = jnp.float32


def signed(modes):
    i = np.arange(modes)
    return np.where(i < modes // 2, i, i - modes)


def inner_np():
    q = np.arange(MZ * MT)
    place = np.arange(ZT)
    kz = (signed(MZ)[q // MT] % Z)[:, None]
    kt = (q % MT)[:, None]
    counts = kz * (place // T_SIZE)[None] % Z * T_SIZE + kt * (place % T_SIZE)[None] % T_SIZE * Z
    angle = 2.0 * math.pi / ZT * (counts % ZT)
    return np.stack([np.cos(angle), -np.sin(angle)]).astype(np.float32)


def complex_np(modes, length):
    k = (signed(modes) % length)[:, None]
    angle = 2.0 * math.pi / length * (k * np.arange(length)[None] % length)
    c, s = np.cos(angle), np.sin(angle)
    return np.stack([np.stack([c, s], 1), np.stack([-s, c], 1)]).astype(np.float32)


def tables():
    inner = inner_np()
    mid = complex_np(MY, Y)
    out = complex_np(MX, X)
    by_owner = inner.reshape(2, ND, NQ, ZT).transpose(0, 2, 1, 3)
    ana_in = by_owner.reshape(192, ZT)
    syn_in = np.zeros((2, 128, ZT), np.float32)
    syn_in[:, :96] = by_owner.reshape(2, 96, ZT)
    syn_in = syn_in.reshape(256, ZT)
    eye8 = np.eye(8, dtype=np.float32)
    ana_mid = np.einsum("rkpy,cd->pcyrkd", mid, eye8).reshape(2, 512, 256)
    syn_mid = np.einsum("pkry,cd->rcypkd", mid, eye8).reshape(1024, 256)
    eye4 = np.eye(4, dtype=np.float32)
    ana_out = np.einsum("rkpsi,gh->grkspih", out.reshape(2, MX, 2, ND, 2), eye4).reshape(128, 512)
    syn_out = out.reshape(2, MX, 2, ND, 2).transpose(2, 4, 3, 0, 1)
    fwd_out = np.repeat(syn_out.reshape(128, 32), 16, axis=1)
    bwd_out = np.repeat(syn_out.reshape(128, 32), 8, axis=1)
    perm = np.zeros((4, MY, 8, MY, 4, 8), np.float32)
    for g in range(4):
        for k in range(MY):
            for c in range(8):
                perm[g, k, c, k, g, c] = 1.0
    perm = perm.reshape(512, 512)
    spread = np.zeros((2, 2, 4, 8, 4, MY, 8), np.float32)
    for g in range(4):
        for c in range(8):
            spread[0, 0, g, c, g, :, c] = 1.0
            spread[1, 1, g, c, g, :, c] = 1.0
    spread = spread.reshape(2, 64, 512)
    fold = np.zeros((2, 8, C, 128), np.float32)
    for o in range(C):
        fold[0, :, o, o] = 1.0
        fold[0, :, o, 96 + o] = -1.0
        fold[1, :, o, 32 + o] = 1.0
        fold[1, :, o, 64 + o] = 1.0
    fold = fold.reshape(2, 256, 128)
    t = dict(
        ana_in=ana_in, syn_in=syn_in, ana_mid=ana_mid, syn_mid=syn_mid, ana_out=ana_out,
        fwd_out=fwd_out, bwd_out=bwd_out, perm=perm, spread=spread, fold=fold,
    )
    return {k: jnp.asarray(v, BF) for k, v in t.items()}


def dot(a, b):
    return lax.dot_general(a, b, (((1,), (0,)), ((), ())), preferred_element_type=F32)


def dot_t(a, b):
    return lax.dot_general(a, b, (((1,), (1,)), ((), ())), preferred_element_type=F32)


def analyse_rows(rows, slot, ana_in, ana_mid, work):
    first = dot_t(ana_in[...], rows).astype(BF)
    second = dot(first[:96], ana_mid[0]) + dot(first[96:], ana_mid[1])
    for qi in range(NQ):
        for r in range(2):
            work[qi, pl.ds(r * 8 + slot, ND, stride=16), :] = second[
                qi * 32 : qi * 32 + 32, r * 128 : r * 128 + 128
            ]


def flush(work, out):
    for qi in range(NQ):
        out[:, qi * 16 : qi * 16 + 16, :] = work[qi].reshape(ND, 16, 128).astype(BF)


def analyse_body(v, ana_in, ana_mid, out, work):
    step = pl.program_id(0)
    analyse_rows(v[...], step, ana_in, ana_mid, work)

    @pl.when(step == 7)
    def _():
        flush(work, out)


def whole(shape):
    return pl.BlockSpec(shape, lambda i: (0,) * len(shape))


def rows_spec():
    return pl.BlockSpec((512, ZT), lambda i: (i, 0))


def analyse(values, t):
    return pl.pallas_call(
        analyse_body,
        grid=(8,),
        in_specs=[rows_spec(), whole((192, ZT)), whole((2, 512, 256))],
        out_specs=whole((ND, 48, 128)),
        out_shape=jax.ShapeDtypeStruct((ND, 48, 128), BF),
        scratch_shapes=[pltpu.VMEM((NQ, 512, 128), F32)],
        name="analyse",
    )(values, t["ana_in"], t["ana_mid"])


def spectrum_rows(got, ana_out, perm, scale):
    parts = dot(ana_out[...], got[...].reshape(512, 128))
    if scale is not None:
        parts = parts * scale
    parts = parts.astype(BF)
    joined = jnp.concatenate([parts[g * 32 : g * 32 + 32] for g in range(4)], axis=1)
    return dot(joined, perm[...])


def mode_mask():
    lane = lax.broadcasted_iota(jnp.int32, (8, 256), 1) // 32
    return lane == lax.broadcasted_iota(jnp.int32, (8, 256), 0)


def scatter_owner(synth, work, out):
    for r in range(2):
        for xi in range(2):
            for g in range(4):
                at = (r * 2 + xi) * 32
                work[pl.ds(r * 8 + xi * 4 + g, ND, stride=16), :] = synth[
                    at : at + 32, g * 128 : g * 128 + 128
                ]
    out[...] = work[...].reshape(ND, 16, 128).astype(BF)


def mix_forward_body(got, w, ana_out, perm, spread, fwd_out, out, spec, srow, mixed, work):
    rows = spectrum_rows(got, ana_out, perm, None)
    spec[...] = rows.astype(BF)
    srow[...] = rows
    mask = mode_mask()
    for kx in range(MX):
        for h in range(2):
            lanes = slice(h * 256, h * 256 + 256)
            real = jnp.where(mask, jnp.broadcast_to(srow[kx : kx + 1, lanes], (8, 256)), 0.0)
            imag = jnp.where(mask, jnp.broadcast_to(srow[16 + kx : 17 + kx, lanes], (8, 256)), 0.0)
            left = jnp.concatenate([real, imag], axis=0).astype(BF)
            at = (kx * 2 + h) * 256
            both = dot(left, w[at : at + 256, :])
            low = both[8:16]
            turned = jnp.concatenate([-low[:, 32:], low[:, :32]], axis=1)
            mixed[kx * 16 + h * 8 : kx * 16 + h * 8 + 8, :] = both[:8] + turned
    values = mixed[...].astype(BF)
    row_ky = lax.broadcasted_iota(jnp.int32, (256, 512), 0) % 16
    lane_ky = lax.broadcasted_iota(jnp.int32, (256, 512), 1) // 8 % 16
    same = row_ky == lane_ky
    wide = [jnp.where(same, dot(values, spread[p]), 0.0).astype(BF) for p in range(2)]
    synth = dot(fwd_out[...], jnp.concatenate(wide, axis=0))
    scatter_owner(synth, work, out)


def squeezed(shape):
    return pl.BlockSpec((None,) + shape, lambda i: (i,) + (0,) * len(shape))


def slot_spec():
    return pl.BlockSpec((ND, 16, 128), lambda i: (0, i, 0))


def mix_forward(got, weights, t):
    return pl.pallas_call(
        mix_forward_body,
        grid=(NQ,),
        in_specs=[
            slot_spec(), squeezed((8192, 64)), whole((128, 512)), whole((512, 512)),
            whole((2, 64, 512)), whole((128, 512)),
        ],
        out_specs=[slot_spec(), squeezed((32, 512))],
        out_shape=[
            jax.ShapeDtypeStruct((ND, 48, 128), BF),
            jax.ShapeDtypeStruct((NQ, 32, 512), BF),
        ],
        scratch_shapes=[
            pltpu.VMEM((32, 512), F32), pltpu.VMEM((256, 64), F32), pltpu.VMEM((512, 128), F32),
        ],
        name="mix_forward",
    )(got, weights, t["ana_out"], t["perm"], t["spread"], t["fwd_out"])


def mix_backward_body(
    got, w, ana_out, perm, fold, bwd_out, out, spec, srow, pair, masked, work
):
    rows = spectrum_rows(got, ana_out, perm, SCALE)
    spec[...] = rows.astype(BF)
    srow[...] = rows
    mask = mode_mask()
    for h in range(2):
        total = None
        for part in range(2):
            lanes = slice(h * 256, h * 256 + 256)
            tall = [
                jnp.where(mask, jnp.broadcast_to(srow[k : k + 1, lanes], (8, 256)), 0.0)
                for k in range(part * 16, part * 16 + 16)
            ]
            one = dot(jnp.concatenate(tall, axis=0).astype(BF), fold[part])
            total = one if total is None else total + one
        pair[h] = total
    for kx in range(MX):
        for h in range(2):
            both = pair[h, kx * 8 : kx * 8 + 8, :]
            left = jnp.concatenate([both[:, :64], both[:, 64:]], axis=0).astype(BF)
            at = (kx * 2 + h) * 256
            full = dot_t(left, w[at : at + 256, :])
            masked[h, kx * 8 : kx * 8 + 8, :] = jnp.where(mask, full[:8], 0.0)
            masked[h, 128 + kx * 8 : 136 + kx * 8, :] = jnp.where(mask, full[8:], 0.0)
    synth = [dot(bwd_out[...], masked[h].astype(BF)).astype(BF) for h in range(2)]
    turned = dot_t(jnp.concatenate(synth, axis=1), perm[...])
    scatter_owner(turned, work, out)


def mix_backward(got, weights, t):
    return pl.pallas_call(
        mix_backward_body,
        grid=(NQ,),
        in_specs=[
            slot_spec(), squeezed((8192, 64)), whole((128, 512)), whole((512, 512)),
            whole((2, 256, 128)), whole((128, 256)),
        ],
        out_specs=[slot_spec(), squeezed((32, 512))],
        out_shape=[
            jax.ShapeDtypeStruct((ND, 48, 128), BF),
            jax.ShapeDtypeStruct((NQ, 32, 512), BF),
        ],
        scratch_shapes=[
            pltpu.VMEM((32, 512), F32), pltpu.VMEM((2, 128, 128), F32),
            pltpu.VMEM((2, 256, 256), F32), pltpu.VMEM((512, 128), F32),
        ],
        name="mix_backward",
    )(got, weights, t["ana_out"], t["perm"], t["fold"], t["bwd_out"])


def unpack(got, have):
    for qi in range(NQ):
        have[qi] = got[:, qi * 16 : qi * 16 + 16, :].reshape(512, 128).astype(F32)


def synthesise_rows(slot, have, syn_mid, syn_in):
    parts = []
    for p in range(2):
        pieces = [have[qi, pl.ds(p * 8 + slot, ND, stride=16), :] for qi in range(NQ)]
        pieces.append(jnp.zeros((ND, 128), F32))
        parts.append(jnp.concatenate(pieces, axis=0).astype(BF))
    both = jnp.concatenate(parts, axis=1)
    tall = dot_t(syn_mid[...], both).astype(BF)
    return dot(jnp.concatenate([tall[:512], tall[512:]], axis=1), syn_in[...])


ROOT = math.sqrt(2.0 / math.pi)
CHUNK = 32


def activate_body(
    got, lin, cot, syn_mid, syn_in, ana_in, ana_mid, act, grad, out, have, spectral, work
):
    step = pl.program_id(0)

    @pl.when(step == 0)
    def _():
        unpack(got, have)

    spectral[...] = synthesise_rows(step, have, syn_mid, syn_in)

    def chunk(i, carry):
        at = pl.ds(pl.multiple_of(i * CHUNK, CHUNK), CHUNK)
        v = spectral[at, :] * SCALE + lin[at, :]
        square = v * v
        half = 0.5 + 0.5 * jnp.tanh(v * (ROOT + (ROOT * 0.044715) * square))
        value = v * half
        slope = half + (value - value * half) * (2.0 * ROOT + (6.0 * ROOT * 0.044715) * square)
        act[at, :] = value.astype(BF)
        grad[at, :] = (cot[at, :].astype(F32) * slope).astype(BF)
        return carry

    lax.fori_loop(0, 512 // CHUNK, chunk, 0)
    analyse_rows(grad[...], step, ana_in, ana_mid, work)

    @pl.when(step == 7)
    def _():
        flush(work, out)


def activate(got, lin, cot, t):
    return pl.pallas_call(
        activate_body,
        grid=(8,),
        in_specs=[
            whole((ND, 48, 128)), rows_spec(), rows_spec(), whole((1024, 256)), whole((256, ZT)),
            whole((192, ZT)), whole((2, 512, 256)),
        ],
        out_specs=[rows_spec(), rows_spec(), whole((ND, 48, 128))],
        out_shape=[
            jax.ShapeDtypeStruct((4096, ZT), BF),
            jax.ShapeDtypeStruct((4096, ZT), BF),
            jax.ShapeDtypeStruct((ND, 48, 128), BF),
        ],
        scratch_shapes=[
            pltpu.VMEM((NQ, 512, 128), F32), pltpu.VMEM((512, ZT), F32), pltpu.VMEM((NQ, 512, 128), F32),
        ],
        name="activate",
    )(got, lin, cot, t["syn_mid"], t["syn_in"], t["ana_in"], t["ana_mid"])


def finish_body(got, lin, syn_mid, syn_in, out, have):
    step = pl.program_id(0)

    @pl.when(step == 0)
    def _():
        unpack(got, have)

    out[...] = (synthesise_rows(step, have, syn_mid, syn_in) + lin[...]).astype(BF)


def finish(got, lin, t):
    return pl.pallas_call(
        finish_body,
        grid=(8,),
        in_specs=[whole((ND, 48, 128)), rows_spec(), whole((1024, 256)), whole((256, ZT))],
        out_specs=rows_spec(),
        out_shape=jax.ShapeDtypeStruct((4096, ZT), BF),
        scratch_shapes=[pltpu.VMEM((NQ, 512, 128), F32)],
        name="finish",
    )(got, lin, t["syn_mid"], t["syn_in"])


def linear_body(v, kron, bias, out):
    out[...] = (dot(kron[...], v[...].reshape(256, ZT)) + bias[...]).reshape(C, 8, ZT)


def linear(values, matrix, bias):
    block = pl.BlockSpec((None, C, 8, ZT), lambda i: (i // 8, 0, i % 8, 0))
    eye = jnp.eye(8, dtype=F32)
    kron = (matrix.astype(F32)[:, None, :, None] * eye[None, :, None, :]).reshape(256, 256)
    return pl.pallas_call(
        linear_body,
        grid=(16,),
        in_specs=[block, whole((256, 256)), whole((256, 1))],
        out_specs=block,
        out_shape=jax.ShapeDtypeStruct((2, C, Y, ZT), F32),
        name="linear",
    )(values, kron.astype(BF), jnp.repeat(bias, 8)[:, None])


def weight_body(*refs):
    specs, grads = refs[:4], refs[4:8]
    fold, out, srow, grow = refs[8:]
    group = pl.program_id(0) % 4

    @pl.when(group == 0)
    def _():
        for s in range(4):
            srow[s] = specs[s][...].astype(F32)
            grow[s] = grads[s][...].astype(F32)

    mask = mode_mask()
    low = lax.broadcasted_iota(jnp.int32, (32, 128), 1) < 64
    blank = jnp.zeros((64, 128), F32)

    def tall(ref, s, p, j, h):
        row = ref[s, pl.ds(p * 16 + group * 4 + j, 1), h * 256 : h * 256 + 256]
        return jnp.where(mask, jnp.broadcast_to(row, (8, 256)), 0.0)

    for h in range(2):
        left = [tall(srow, s, p, j, h) for j in range(4) for p in range(2) for s in range(4)]
        left = jnp.concatenate(left, axis=0).astype(BF)
        pair = None
        for p in range(2):
            rows = [tall(grow, s, p, j, h) for j in range(4) for s in range(4)]
            one = dot(jnp.concatenate(rows, axis=0).astype(BF), fold[p])
            pair = one if pair is None else pair + one
        blocks = []
        for j in range(4):
            here = pair[j * 32 : j * 32 + 32]
            there = jnp.concatenate([here[:, 64:], here[:, :64]], axis=1)
            if j % 2 == 0:
                first, second = jnp.where(low, here, 0.0), jnp.where(low, there, 0.0)
            else:
                first, second = jnp.where(low, 0.0, there), jnp.where(low, 0.0, here)
            piece = jnp.concatenate([first, second], axis=0)
            blocks.append(jnp.concatenate([piece, blank] if j < 2 else [blank, piece], axis=1))
        right = jnp.concatenate(blocks, axis=0).astype(BF)
        grad = lax.dot_general(left, right, (((0,), (0,)), ((), ())), preferred_element_type=F32)
        for j in range(4):
            at = (j * 2 + h) * 256
            out[at : at + 256, :] = grad[:, j * 64 : j * 64 + 64]


def weight_gradient(specs, grads, t):
    rows = pl.BlockSpec((None, 32, 512), lambda i: (i // 4, 0, 0))
    return pl.pallas_call(
        weight_body,
        grid=(NQ * 4,),
        in_specs=[rows] * 8 + [whole((2, 256, 128))],
        out_specs=pl.BlockSpec((None, 2048, 64), lambda i: (i // 4, i % 4, 0)),
        out_shape=jax.ShapeDtypeStruct((NQ, 8192, 64), F32),
        scratch_shapes=[pltpu.VMEM((4, 32, 512), F32), pltpu.VMEM((4, 32, 512), F32)],
        name="weight_gradient",
    )(*specs, *grads, t["fold"])


def exchange(values):
    return lax.all_to_all(values, "slab", split_axis=0, concat_axis=0, tiled=True)


def everyone(values):
    pieces = [values]
    for k in range(1, 4):
        pieces.append(lax.ppermute(values, "dp", [(i, i ^ k) for i in range(4)]))
    return pieces


def per_device(field, cotangent, spectral_weight, point_weight, bias_term):
    t = tables()
    rows = field.reshape(4096, ZT)
    weights = spectral_weight.reshape(NQ, 8192, 64)
    sent = exchange(analyse(rows, t))
    lin = linear(field[0], point_weight, bias_term)
    back, spec = mix_forward(sent, weights, t)
    got = exchange(back)
    specs = everyone(spec)
    act, grad_pre, out = activate(got, lin.reshape(4096, ZT), cotangent.reshape(4096, ZT), t)
    sent = exchange(out)
    lin = linear(grad_pre.reshape(2, C, Y, ZT), point_weight.T, jnp.zeros_like(bias_term))
    back, grad_spec = mix_backward(sent, weights, t)
    got = exchange(back)
    grads = everyone(grad_spec)
    weight_grad = weight_gradient(specs, grads, t).reshape(NQ, MX, MY, C, 2 * C)
    total = finish(got, lin.reshape(4096, ZT), t)
    shape = (1, 2, C, Y, ZT)
    return act.reshape(shape), total.reshape(shape), weight_grad


def solution(mesh):
    placed = (
        P("dp", "slab", None, None, None),
        P("dp", "slab", None, None, None),
        P("slab", None, None, None, None),
        P(),
        P(),
    )
    return jax.shard_map(
        per_device,
        mesh=mesh,
        in_specs=placed,
        out_specs=(
            P("dp", "slab", None, None, None),
            P("dp", "slab", None, None, None),
            P("slab", None, None, None, None),
        ),
        check_vma=False,
    )
```

profile of v0, /device:TPU:0, one launch (start us, length us, event | category | flops | bytes accessed | tf_op | source)
XLA Modules:
  0.0 166.1 jit_solution(14093138858855961147)
XLA Ops:
  0.6 8.3 %analyse.1 = bf16[32,48,128]{2,1,0:T(8,128)(2,1)} custom-call(bf16[4096,512]{1,0:T(8,128)(2,1)} %bitcast.20, bf16[192,512]{1,0:T(8,128)(2,1)} %constant.22.clone.ana_in, bf16[2,512,256]{2,1,0:T(8,128)(2,1)} %constant.24.clone.ana_mid), custom_call_target="tpu_custom_call" | custom-call | tf_op jit(solution)/shard_map/analyse/pallas_call | solution.py:135
  9.0 10.9 %all-to-all-start = ((bf16[32,48,128]{2,1,0:T(8,128)(2,1)}), bf16[32,48,128]{2,1,0:T(8,128)(2,1)S(1)}, u32[]{:S(2)}, u32[]{:S(2)}) async-start(bf16[32,48,128]{2,1,0:T(8,128)(2,1)} %analyse.1), calls=%async_computation | async-start | bytes 786432 | tf_op jit(solution)/shard_map/all_to_all | solution.py:445
  19.9 12.2 %all-to-all-done.got = bf16[32,48,128]{2,1,0:T(8,128)(2,1)S(1)} async-done(((bf16[32,48,128]{2,1,0:T(8,128)(2,1)}), bf16[32,48,128]{2,1,0:T(8,128)(2,1)S(1)}, u32[]{:S(2)}, u32[]{:S(2)}) %all-to-all-start) | async-done | bytes 393248 | tf_op jit(solution)/shard_map/all_to_all | solution.py:445
  32.1 0.7 copy-done.2
  32.8 6.7 %mix_forward.1 = (bf16[32,48,128]{2,1,0:T(8,128)(2,1)}, bf16[3,32,512]{2,1,0:T(8,128)(2,1)}) custom-call(bf16[32,48,128]{2,1,0:T(8,128)(2,1)} %copy-done.2, bf16[3,8192,64]{2,1,0:T(8,128)(2,1)} %bitcast.18, bf16[128,512]{1,0:T(8,128)(2,1)} %constant.26.clone.ana_out, bf16[512,512]{1,0:T(8,128)(2,1)} %constant.29.clone.perm, ...), custom_call_target="tpu_custom_call" | custom-call | tf_op jit(solution)/shard_map/mix_forward/pallas_call | solution.py:205
  39.5 3.9 %all-to-all-start.1 = ((bf16[32,48,128]{2,1,0:T(8,128)(2,1)}), bf16[32,48,128]{2,1,0:T(8,128)(2,1)S(1)}, u32[]{:S(2)}, u32[]{:S(2)}) async-start(bf16[32,48,128]{2,1,0:T(8,128)(2,1)} %get-tuple-element.10), calls=%async_computation.1 | async-start | bytes 786432 | tf_op jit(solution)/shard_map/all_to_all | solution.py:445
  43.5 0.7 broadcast_in_dim_reshape.8.bias
  44.3 2.0 %multiply_convert_fusion = (bf16[32,8,32,8]{3,2,1,0:T(8,128)(2,1)S(1)}, bf16[32,8,32,8]{3,2,1,0:T(8,128)(2,1)}) fusion(f32[32,32]{1,0:T(8,128)S(1)} %copy.20, f32[8,8]{1,0:T(8,128)S(1)} %fusion, f32[32,32]{1,0:T(8,128)S(1)} %get-tuple-element.18), kind=kLoop, calls=%fused_computation | loop fusion | flops 262144 | bytes 270592 | tf_op jit(solution)/shard_map/convert_element_type | solution.py:384
  46.3 4.7 %convert_element_type.32.kron = bf16[256,256]{1,0:T(8,128)(2,1)} reshape(bf16[32,8,32,8]{3,2,1,0:T(8,128)(2,1)} %get-tuple-element.20) | data formatting | bytes 262144 | tf_op jit(solution)/shard_map/convert_element_type | solution.py:384
  51.0 12.5 %linear.2 = f32[2,32,64,512]{3,2,1,0:T(8,128)} custom-call(bf16[2,32,64,512]{3,2,1,0:T(8,128)(2,1)} %bitcast.21, bf16[256,256]{1,0:T(8,128)(2,1)} %convert_element_type.32.kron, f32[256,1]{1,0:T(8,128)} %broadcast_in_dim_reshape.8.bias), custom_call_target="tpu_custom_call" | custom-call | tf_op jit(solution)/shard_map/linear/pallas_call | solution.py:377
  63.5 0.8 copy-done.1
  64.2 19.5 %activate.1 = (bf16[4096,512]{1,0:T(8,128)(2,1)}, bf16[4096,512]{1,0:T(8,128)(2,1)}, bf16[32,48,128]{2,1,0:T(8,128)(2,1)}) custom-call(bf16[32,48,128]{2,1,0:T(8,128)(2,1)} %copy-done.1, f32[4096,512]{1,0:T(8,128)} %bitcast.16, bf16[4096,512]{1,0:T(8,128)(2,1)} %bitcast.23, bf16[1024,256]{1,0:T(8,128)(2,1)} %constant.25.clone.syn_mid, ...), custom_call_target="tpu_custom_call" | custom-call | tf_op jit(solution)/shard_map/activate/pallas_call | solution.py:327
  83.8 21.4 %all_to_all.20.got = bf16[32,48,128]{2,1,0:T(8,128)(2,1)} all-to-all(bf16[32,48,128]{2,1,0:T(8,128)(2,1)} %get-tuple-element.12), channel_id=1, replica_groups=mesh['slab'=32,'dp'=4] {'slab'}, dimensions={0} | all-to-all | bytes 786432 | tf_op jit(solution)/shard_map/all_to_all | solution.py:445
  105.2 7.5 %mix_backward.1 = (bf16[32,48,128]{2,1,0:T(8,128)(2,1)}, bf16[3,32,512]{2,1,0:T(8,128)(2,1)}) custom-call(bf16[32,48,128]{2,1,0:T(8,128)(2,1)} %all_to_all.20.got, bf16[3,8192,64]{2,1,0:T(8,128)(2,1)} %bitcast.19, bf16[128,512]{1,0:T(8,128)(2,1)} %constant.26.clone.ana_out, bf16[512,512]{1,0:T(8,128)(2,1)} %constant.29.clone.perm, ...), custom_call_target="tpu_custom_call" | custom-call | tf_op jit(solution)/shard_map/mix_backward/pallas_call | solution.py:256
  112.6 3.9 %all-to-all-start.3 = ((bf16[32,48,128]{2,1,0:T(8,128)(2,1)}), bf16[32,48,128]{2,1,0:T(8,128)(2,1)S(1)}, u32[]{:S(2)}, u32[]{:S(2)}) async-start(bf16[32,48,128]{2,1,0:T(8,128)(2,1)} %get-tuple-element.13), calls=%async_computation.3 | async-start | bytes 786432 | tf_op jit(solution)/shard_map/all_to_all | solution.py:445
  116.6 0.8 collective-permute-start.1
  117.4 1.1 collective-permute-start
  118.8 1.3 collective-permute-start.4
  120.1 3.0 %collective-permute-done.2.refs_3_ = bf16[3,32,512]{2,1,0:T(8,128)(2,1)S(1)} collective-permute-done((bf16[3,32,512]{2,1,0:T(8,128)(2,1)S(1)}, bf16[3,32,512]{2,1,0:T(8,128)(2,1)S(1)}, u32[]{:S(2)}, u32[]{:S(2)}) %collective-permute-start.2) | collective-permute-done | bytes 98336 | tf_op jit(solution)/shard_map/ppermute | solution.py:451
  123.3 3.5 %convert_element_type.36.kron = bf16[256,256]{1,0:T(8,128)(2,1)} reshape(bf16[32,8,32,8]{3,2,1,0:T(8,128)(2,1)S(1)} %get-tuple-element.19) | data formatting | bytes 262144 | tf_op jit(solution)/shard_map/convert_element_type | solution.py:384
  127.4 12.5 %linear.3 = f32[2,32,64,512]{3,2,1,0:T(8,128)} custom-call(bf16[2,32,64,512]{3,2,1,0:T(8,128)(2,1)} %bitcast.24, bf16[256,256]{1,0:T(8,128)(2,1)} %convert_element_type.36.kron, f32[256,1]{1,0:T(8,128)} %broadcast_in_dim_reshape.7.bias), custom_call_target="tpu_custom_call" | custom-call | tf_op jit(solution)/shard_map/linear/pallas_call | solution.py:377
  141.4 13.6 %weight_gradient.1 = f32[3,8192,64]{2,1,0:T(8,128)} custom-call(bf16[3,32,512]{2,1,0:T(8,128)(2,1)} %get-tuple-element.15.refs_0_, bf16[3,32,512]{2,1,0:T(8,128)(2,1)} %copy-done.6, bf16[3,32,512]{2,1,0:T(8,128)(2,1)} %copy-done.5, bf16[3,32,512]{2,1,0:T(8,128)(2,1)} %copy-done.4, bf16[3,32,512]{2,1,0:T(8,128)(2,1)} %get-tuple-element.16.refs_4_, ...), custom_call_target="tpu_custom_call" | custom-call | tf_op jit(solution)/shard_map/weight_gradient/pallas_call | solution.py:433
  155.0 0.7 copy-done
  155.8 10.3 %finish.1 = bf16[4096,512]{1,0:T(8,128)(2,1)} custom-call(bf16[32,48,128]{2,1,0:T(8,128)(2,1)} %copy-done, f32[4096,512]{1,0:T(8,128)} %bitcast.17, bf16[1024,256]{1,0:T(8,128)(2,1)} %constant.25.clone.syn_mid, bf16[256,512]{1,0:T(8,128)(2,1)} %constant.23.clone.syn_in), custom_call_target="tpu_custom_call" | custom-call | tf_op jit(solution)/shard_map/finish/pallas_call | solution.py:358
  (36 shorter events, 2.8 us)
Async XLA Ops:
  0.6 19.3 %copy-start.10 = (bf16[32,32]{1,0:T(8,128)(2,1)S(1)}, bf16[32,32]{1,0:T(8,128)(2,1)}, u32[]{:S(2)}) copy-start(bf16[32,32]{1,0:T(8,128)(2,1)} %param.18) | copy-start | bytes 6148
  9.0 23.1 %all-to-all-start = ((bf16[32,48,128]{2,1,0:T(8,128)(2,1)}), bf16[32,48,128]{2,1,0:T(8,128)(2,1)S(1)}, u32[]{:S(2)}, u32[]{:S(2)}) async-start(bf16[32,48,128]{2,1,0:T(8,128)(2,1)} %analyse.1), calls=%async_computation | async-start | bytes 786432 | tf_op jit(solution)/shard_map/all_to_all | solution.py:445
  32.1 0.7 copy-start.2
  32.8 10.6 %copy-start.11 = (f32[32]{0:T(128)S(1)}, f32[32]{0:T(128)}, u32[]{:S(2)}) copy-start(f32[32]{0:T(128)} %param.19) | copy-start | bytes 388
  39.5 24.0 %all-to-all-start.1 = ((bf16[32,48,128]{2,1,0:T(8,128)(2,1)}), bf16[32,48,128]{2,1,0:T(8,128)(2,1)S(1)}, u32[]{:S(2)}, u32[]{:S(2)}) async-start(bf16[32,48,128]{2,1,0:T(8,128)(2,1)} %get-tuple-element.10), calls=%async_computation.1 | async-start | bytes 786432 | tf_op jit(solution)/shard_map/all_to_all | solution.py:445
  63.5 0.8 copy-start.1
  105.2 11.4 %copy-start.3 = (bf16[3,32,512]{2,1,0:T(8,128)(2,1)S(1)}, bf16[3,32,512]{2,1,0:T(8,128)(2,1)}, u32[]{:S(2)}) copy-start(bf16[3,32,512]{2,1,0:T(8,128)(2,1)} %get-tuple-element.15.refs_0_) | copy-start | bytes 294916
  112.6 42.4 %all-to-all-start.3 = ((bf16[32,48,128]{2,1,0:T(8,128)(2,1)}), bf16[32,48,128]{2,1,0:T(8,128)(2,1)S(1)}, u32[]{:S(2)}, u32[]{:S(2)}) async-start(bf16[32,48,128]{2,1,0:T(8,128)(2,1)} %get-tuple-element.13), calls=%async_computation.3 | async-start | bytes 786432 | tf_op jit(solution)/shard_map/all_to_all | solution.py:445
  116.5 6.6 %collective-permute-start.2 = (bf16[3,32,512]{2,1,0:T(8,128)(2,1)S(1)}, bf16[3,32,512]{2,1,0:T(8,128)(2,1)S(1)}, u32[]{:S(2)}, u32[]{:S(2)}) collective-permute-start(bf16[3,32,512]{2,1,0:T(8,128)(2,1)S(1)} %copy-done.3), channel_id=1, source_target_pairs={{0,3},{1,2},{2,1},{3,0},{4,7},{5,6},{6,5},{7,4},{8,11},{9,10},{10,... | collective-permute-start | bytes 294920 | tf_op jit(solution)/shard_map/ppermute | solution.py:451
  116.6 23.4 %collective-permute-start.1 = (bf16[3,32,512]{2,1,0:T(8,128)(2,1)S(1)}, bf16[3,32,512]{2,1,0:T(8,128)(2,1)S(1)}, u32[]{:S(2)}, u32[]{:S(2)}) collective-permute-start(bf16[3,32,512]{2,1,0:T(8,128)(2,1)S(1)} %copy-done.3), channel_id=1, source_target_pairs={{0,2},{1,3},{2,0},{3,1},{4,6},{5,7},{6,4},{7,5},{8,10},{9,11},{10,... | collective-permute-start | bytes 294920 | tf_op jit(solution)/shard_map/ppermute | solution.py:451
  117.4 22.6 %collective-permute-start = (bf16[3,32,512]{2,1,0:T(8,128)(2,1)S(1)}, bf16[3,32,512]{2,1,0:T(8,128)(2,1)S(1)}, u32[]{:S(2)}, u32[]{:S(2)}) collective-permute-start(bf16[3,32,512]{2,1,0:T(8,128)(2,1)S(1)} %copy-done.3), channel_id=1, source_target_pairs={{0,1},{1,0},{2,3},{3,2},{4,5},{5,4},{6,7},{7,6},{8,9},{9,8},{10,11... | collective-permute-start | bytes 294920 | tf_op jit(solution)/shard_map/ppermute | solution.py:451
  118.5 21.6 %collective-permute-start.5 = (bf16[3,32,512]{2,1,0:T(8,128)(2,1)}, bf16[3,32,512]{2,1,0:T(8,128)(2,1)S(1)}, u32[]{:S(2)}, u32[]{:S(2)}) collective-permute-start(bf16[3,32,512]{2,1,0:T(8,128)(2,1)} %get-tuple-element.16.refs_4_), channel_id=1, source_target_pairs={{0,3},{1,2},{2,1},{3,0},{4,7},{5,6},{6,5},{7,4},{8,11},{9,10},{10,... | collective-permute-start | bytes 294920 | tf_op jit(solution)/shard_map/ppermute | solution.py:451
  118.8 21.2 %collective-permute-start.4 = (bf16[3,32,512]{2,1,0:T(8,128)(2,1)}, bf16[3,32,512]{2,1,0:T(8,128)(2,1)S(1)}, u32[]{:S(2)}, u32[]{:S(2)}) collective-permute-start(bf16[3,32,512]{2,1,0:T(8,128)(2,1)} %get-tuple-element.16.refs_4_), channel_id=1, source_target_pairs={{0,2},{1,3},{2,0},{3,1},{4,6},{5,7},{6,4},{7,5},{8,10},{9,11},{10,... | collective-permute-start | bytes 294920 | tf_op jit(solution)/shard_map/ppermute | solution.py:451
  123.1 16.9 %copy-start.4 = (bf16[3,32,512]{2,1,0:T(8,128)(2,1)}, bf16[3,32,512]{2,1,0:T(8,128)(2,1)S(1)}, u32[]{:S(2)}) copy-start(bf16[3,32,512]{2,1,0:T(8,128)(2,1)S(1)} %collective-permute-done.2.refs_3_) | copy-start | bytes 294916
  123.1 16.9 %collective-permute-start.3 = (bf16[3,32,512]{2,1,0:T(8,128)(2,1)}, bf16[3,32,512]{2,1,0:T(8,128)(2,1)S(1)}, u32[]{:S(2)}, u32[]{:S(2)}) collective-permute-start(bf16[3,32,512]{2,1,0:T(8,128)(2,1)} %get-tuple-element.16.refs_4_), channel_id=1, source_target_pairs={{0,1},{1,0},{2,3},{3,2},{4,5},{5,4},{6,7},{7,6},{8,9},{9,8},{10,11... | collective-permute-start | bytes 294920 | tf_op jit(solution)/shard_map/ppermute | solution.py:451
  140.0 0.6 copy-start.5
  140.0 0.7 copy-start.6
  140.0 0.7 copy-start.7
  140.1 0.7 copy-start.8
  140.7 0.6 copy-start.9
  155.0 0.8 copy-start
where the time goes:
time: 169 us; the launch traced here: 166 us
  Pallas kernels  91 us (54%)
  starting transfers between devices  22.4 us (13%)
  blocking collectives  21.4 us (13%)
  waiting for transfers between devices  15.2 us (9%)
  local copies, waits for them, and re-layouts  13.3 us (8%)
  other arithmetic  2.03 us (1%)
    pallas_call x2, Pallas kernels, linear(): pl.pallas_call(linear_body, grid=(16,), in_specs=[block, whole((256, 256)...  25 us
    all_to_all x1, blocking collectives, exchange(): lax.all_to_all(values, 'slab', split_axis=0, concat_axis=0, tiled=True)  21.4 us
    pallas_call x1, Pallas kernels, activate(): pl.pallas_call(activate_body, grid=(8,), in_specs=[whole((ND, 48, 128)),...  19.5 us
    all_to_all x3, starting transfers between devices, exchange(): lax.all_to_all(values, 'slab', split_axis=0, concat_axis=0, tiled=True)  18.7 us
    pallas_call x1, Pallas kernels, weight_gradient(): pl.pallas_call(weight_body, grid=(NQ * 4,), in_specs=[rows] * 8 + [whole(...  13.6 us
    all_to_all x3, waiting for transfers between devices, exchange(): lax.all_to_all(values, 'slab', split_axis=0, concat_axis=0, tiled=True)  12.2 us
    pallas_call x1, Pallas kernels, finish(): pl.pallas_call(finish_body, grid=(8,), in_specs=[whole((ND, 48, 128)), ro...  10.3 us
    pallas_call x1, Pallas kernels, analyse(): pl.pallas_call(analyse_body, grid=(8,), in_specs=[rows_spec(), whole((192...  8.34 us
  transfers between devices with their start and end apart: 9, of which 2 were waited for; matrix products, arithmetic and copies ran while one was open for 7% of the time, Pallas kernels for 23%

commit v1 on v0

--- a/solution.py
+++ b/solution.py
@@ -52,14 +52,10 @@
     inner = inner_np()
     mid = complex_np(MY, Y)
     out = complex_np(MX, X)
-    by_owner = inner.reshape(2, ND, NQ, ZT).transpose(0, 2, 1, 3)
-    ana_in = by_owner.reshape(192, ZT)
-    syn_in = np.zeros((2, 128, ZT), np.float32)
-    syn_in[:, :96] = by_owner.reshape(2, 96, ZT)
-    syn_in = syn_in.reshape(256, ZT)
-    eye8 = np.eye(8, dtype=np.float32)
-    ana_mid = np.einsum("rkpy,cd->pcyrkd", mid, eye8).reshape(2, 512, 256)
-    syn_mid = np.einsum("pkry,cd->rcypkd", mid, eye8).reshape(1024, 256)
+    depth = np.zeros((2, 128, ZT), np.float32)
+    depth[:, :96] = inner.reshape(2, ND, NQ, ZT).transpose(0, 2, 1, 3).reshape(2, 96, ZT)
+    depth = depth.reshape(256, ZT)
+    middle = np.einsum("rkpy,cd->pcyrkd", mid, np.eye(8, dtype=np.float32)).reshape(1024, 256)
     eye4 = np.eye(4, dtype=np.float32)
     ana_out = np.einsum("rkpsi,gh->grkspih", out.reshape(2, MX, 2, ND, 2), eye4).reshape(128, 512)
     syn_out = out.reshape(2, MX, 2, ND, 2).transpose(2, 4, 3, 0, 1)
@@ -85,8 +81,8 @@
         fold[1, :, o, 64 + o] = 1.0
     fold = fold.reshape(2, 256, 128)
     t = dict(
-        ana_in=ana_in, syn_in=syn_in, ana_mid=ana_mid, syn_mid=syn_mid, ana_out=ana_out,
-        fwd_out=fwd_out, bwd_out=bwd_out, perm=perm, spread=spread, fold=fold,
+        depth=depth, middle=middle, ana_out=ana_out, fwd_out=fwd_out * SCALE, bwd_out=bwd_out,
+        perm=perm, spread=spread, fold=fold,
     )
     return {k: jnp.asarray(v, BF) for k, v in t.items()}
 
@@ -99,48 +95,67 @@
     return lax.dot_general(a, b, (((1,), (1,)), ((), ())), preferred_element_type=F32)
 
 
-def analyse_rows(rows, slot, ana_in, ana_mid, work):
-    first = dot_t(ana_in[...], rows).astype(BF)
-    second = dot(first[:96], ana_mid[0]) + dot(first[96:], ana_mid[1])
-    for qi in range(NQ):
-        for r in range(2):
-            work[qi, pl.ds(r * 8 + slot, ND, stride=16), :] = second[
-                qi * 32 : qi * 32 + 32, r * 128 : r * 128 + 128
-            ]
-
-
-def flush(work, out):
+def owner_table(depth):
+    return jnp.concatenate([depth[0:96, :], depth[128:224, :]], axis=0)
+
+
+def analyse_rows(rows, slot, table, first):
+    part = dot_t(table, rows).astype(BF)
+    at = pl.ds(slot * 96, 96) if isinstance(slot, int) else pl.ds(pl.multiple_of(slot * 96, 32), 96)
+    first[at, 0:512] = part[:96]
+    first[at, 512:1024] = part[96:]
+
+
+def by_owner(first, middle, out, work):
+    second = dot(first[...], middle[...])
+    for slot in range(8):
+        for qi in range(NQ):
+            for r in range(2):
+                at = slot * 96 + qi * 32
+                work[qi, pl.ds(r * 8 + slot, ND, stride=16), :] = second[
+                    at : at + 32, r * 128 : r * 128 + 128
+                ]
     for qi in range(NQ):
         out[:, qi * 16 : qi * 16 + 16, :] = work[qi].reshape(ND, 16, 128).astype(BF)
 
 
-def analyse_body(v, ana_in, ana_mid, out, work):
-    step = pl.program_id(0)
-    analyse_rows(v[...], step, ana_in, ana_mid, work)
-
-    @pl.when(step == 7)
-    def _():
-        flush(work, out)
+def chunk_copy(src, dst, sem, k):
+    at = pl.ds(k * 512, 512)
+    return pltpu.make_async_copy(src.at[at], dst.at[at], sem.at[k])
+
+
+def analyse_body(v, depth, middle, out, have, first, work, sem):
+    for k in range(8):
+        chunk_copy(v, have, sem, k).start()
+    table = owner_table(depth)
+    for k in range(8):
+        chunk_copy(v, have, sem, k).wait()
+        analyse_rows(have[k * 512 : k * 512 + 512, :], k, table, first)
+    by_owner(first, middle, out, work)
 
 
 def whole(shape):
     return pl.BlockSpec(shape, lambda i: (0,) * len(shape))
 
 
-def rows_spec():
-    return pl.BlockSpec((512, ZT), lambda i: (i, 0))
+HBM = pl.BlockSpec(memory_space=pl.ANY)
+VM = pl.BlockSpec(memory_space=pltpu.VMEM)
+GRID_ROWS = jax.ShapeDtypeStruct((4096, ZT), BF)
+SENT = jax.ShapeDtypeStruct((ND, 48, 128), BF)
 
 
 def analyse(values, t):
     return pl.pallas_call(
         analyse_body,
-        grid=(8,),
-        in_specs=[rows_spec(), whole((192, ZT)), whole((2, 512, 256))],
-        out_specs=whole((ND, 48, 128)),
-        out_shape=jax.ShapeDtypeStruct((ND, 48, 128), BF),
-        scratch_shapes=[pltpu.VMEM((NQ, 512, 128), F32)],
+        in_specs=[HBM, VM, VM],
+        out_specs=VM,
+        out_shape=SENT,
+        scratch_shapes=[
+            pltpu.VMEM((4096, ZT), BF), pltpu.VMEM((768, 1024), BF),
+            pltpu.VMEM((NQ, 512, 128), F32), pltpu.SemaphoreType.DMA((8,)),
+        ],
         name="analyse",
-    )(values, t["ana_in"], t["ana_mid"])
+    )(values, t["depth"], t["middle"])
 
 
 def spectrum_rows(got, ana_out, perm, scale):
@@ -273,170 +288,227 @@
     )(got, weights, t["ana_out"], t["perm"], t["fold"], t["bwd_out"])
 
 
-def unpack(got, have):
+def unpack(got, have, turned, middle, tall):
     for qi in range(NQ):
         have[qi] = got[:, qi * 16 : qi * 16 + 16, :].reshape(512, 128).astype(F32)
-
-
-def synthesise_rows(slot, have, syn_mid, syn_in):
-    parts = []
-    for p in range(2):
-        pieces = [have[qi, pl.ds(p * 8 + slot, ND, stride=16), :] for qi in range(NQ)]
-        pieces.append(jnp.zeros((ND, 128), F32))
-        parts.append(jnp.concatenate(pieces, axis=0).astype(BF))
-    both = jnp.concatenate(parts, axis=1)
-    tall = dot_t(syn_mid[...], both).astype(BF)
-    return dot(jnp.concatenate([tall[:512], tall[512:]], axis=1), syn_in[...])
+    for slot in range(8):
+        for p in range(2):
+            pieces = [have[qi, pl.ds(p * 8 + slot, ND, stride=16), :] for qi in range(NQ)]
+            pieces.append(jnp.zeros((ND, 128), F32))
+            turned[slot * 128 : slot * 128 + 128, p * 128 : p * 128 + 128] = jnp.concatenate(
+                pieces, axis=0
+            ).astype(BF)
+    for r in range(2):
+        block = dot_t(middle[r * 512 : r * 512 + 512, :], turned[...]).astype(BF)
+        for slot in range(8):
+            tall[slot * 512 : slot * 512 + 512, r * 128 : r * 128 + 128] = block[
+                :, slot * 128 : slot * 128 + 128
+            ]
 
 
 ROOT = math.sqrt(2.0 / math.pi)
-CHUNK = 32
+CHUNK = 128
 
 
 def activate_body(
-    got, lin, cot, syn_mid, syn_in, ana_in, ana_mid, act, grad, out, have, spectral, work
+    got, lin, cot, depth, middle, act, grad, out, lin_v, cot_v, act_v, grad_v, have, turned, tall,
+    first, work, sems,
 ):
-    step = pl.program_id(0)
-
-    @pl.when(step == 0)
-    def _():
-        unpack(got, have)
-
-    spectral[...] = synthesise_rows(step, have, syn_mid, syn_in)
-
-    def chunk(i, carry):
-        at = pl.ds(pl.multiple_of(i * CHUNK, CHUNK), CHUNK)
-        v = spectral[at, :] * SCALE + lin[at, :]
-        square = v * v
-        half = 0.5 + 0.5 * jnp.tanh(v * (ROOT + (ROOT * 0.044715) * square))
-        value = v * half
-        slope = half + (value - value * half) * (2.0 * ROOT + (6.0 * ROOT * 0.044715) * square)
-        act[at, :] = value.astype(BF)
-        grad[at, :] = (cot[at, :].astype(F32) * slope).astype(BF)
+    for k in range(8):
+        chunk_copy(lin, lin_v, sems.at[0], k).start()
+        chunk_copy(cot, cot_v, sems.at[1], k).start()
+    unpack(got, have, turned, middle, tall)
+
+    def step(k, carry):
+        chunk_copy(lin, lin_v, sems.at[0], k).wait()
+        chunk_copy(cot, cot_v, sems.at[1], k).wait()
+        for j in range(512 // CHUNK):
+            at = pl.ds(pl.multiple_of(k * 512 + j * CHUNK, CHUNK), CHUNK)
+            v = dot(tall[at, :], depth[...]) + lin_v[at, :].astype(F32)
+            square = v * v
+            half = 0.5 + 0.5 * jnp.tanh(v * (ROOT + (ROOT * 0.044715) * square))
+            value = v * half
+            slope = half + (value - value * half) * (2.0 * ROOT + (6.0 * ROOT * 0.044715) * square)
+            act_v[at, :] = value.astype(BF)
+            grad_v[at, :] = (cot_v[at, :].astype(F32) * slope).astype(BF)
+        chunk_copy(act_v, act, sems.at[2], k).start()
+        chunk_copy(grad_v, grad, sems.at[3], k).start()
+        rows = grad_v[pl.ds(pl.multiple_of(k * 512, 512), 512), :]
+        analyse_rows(rows, k, owner_table(depth), first)
         return carry
 
-    lax.fori_loop(0, 512 // CHUNK, chunk, 0)
-    analyse_rows(grad[...], step, ana_in, ana_mid, work)
-
-    @pl.when(step == 7)
-    def _():
-        flush(work, out)
+    lax.fori_loop(0, 8, step, 0)
+    by_owner(first, middle, out, work)
+    for k in range(8):
+        chunk_copy(act_v, act, sems.at[2], k).wait()
+        chunk_copy(grad_v, grad, sems.at[3], k).wait()
+
+
+SYNTH_SCRATCH = [
+    pltpu.VMEM((NQ, 512, 128), F32), pltpu.VMEM((1024, 256), BF), pltpu.VMEM((4096, 256), BF),
+]
 
 
 def activate(got, lin, cot, t):
     return pl.pallas_call(
         activate_body,
-        grid=(8,),
-        in_specs=[
-            whole((ND, 48, 128)), rows_spec(), rows_spec(), whole((1024, 256)), whole((256, ZT)),
-            whole((192, ZT)), whole((2, 512, 256)),
-        ],
-        out_specs=[rows_spec(), rows_spec(), whole((ND, 48, 128))],
-        out_shape=[
-            jax.ShapeDtypeStruct((4096, ZT), BF),
-            jax.ShapeDtypeStruct((4096, ZT), BF),
-            jax.ShapeDtypeStruct((ND, 48, 128), BF),
-        ],
+        in_specs=[VM, HBM, HBM, VM, VM],
+        out_specs=[HBM, HBM, VM],
+        out_shape=[GRID_ROWS, GRID_ROWS, SENT],
+        scratch_shapes=[pltpu.VMEM((4096, ZT), BF)] * 4
+        + SYNTH_SCRATCH
+        + [
+            pltpu.VMEM((768, 1024), BF), pltpu.VMEM((NQ, 512, 128), F32),
+            pltpu.SemaphoreType.DMA((4, 8)),
+        ],
+        name="activate",
+    )(got, lin, cot, t["depth"], t["middle"])
+
+
+def finish_body(got, lin, depth, middle, out, lin_v, out_v, have, turned, tall, sems):
+    for k in range(8):
+        chunk_copy(lin, lin_v, sems.at[0], k).start()
+    unpack(got, have, turned, middle, tall)
+
+    def step(k, carry):
+        chunk_copy(lin, lin_v, sems.at[0], k).wait()
+        at = pl.ds(pl.multiple_of(k * 512, 512), 512)
+        out_v[at, :] = (dot(tall[at, :], depth[...]) + lin_v[at, :].astype(F32)).astype(BF)
+        chunk_copy(out_v, out, sems.at[1], k).start()
+        return carry
+
+    lax.fori_loop(0, 8, step, 0)
+    for k in range(8):
+        chunk_copy(out_v, out, sems.at[1], k).wait()
+
+
+def finish(got, lin, t):
+    return pl.pallas_call(
+        finish_body,
+        in_specs=[VM, HBM, VM, VM],
+        out_specs=HBM,
+        out_shape=GRID_ROWS,
+        scratch_shapes=[pltpu.VMEM((4096, ZT), BF)] * 2
+        + SYNTH_SCRATCH
+        + [pltpu.SemaphoreType.DMA((2, 8))],
+        name="finish",
+    )(got, lin, t["depth"], t["middle"])
+
+
+def linear_body(turn, v, matrix, bias, out, have, made, kron, sems):
+    for k in range(8):
+        chunk_copy(v, have, sems.at[0], k).start()
+    rows = lax.broadcasted_iota(jnp.int32, (512, C), 0) // 16
+    pick = jnp.where(rows == lax.broadcasted_iota(jnp.int32, (512, C), 1), 1.0, 0.0).astype(BF)
+    if turn:
+        wide = lax.dot_general(matrix[...], pick, (((0,), (1,)), ((), ())), preferred_element_type=F32)
+    else:
+        wide = dot_t(matrix[...], pick)
+    tall = dot(pick, wide.astype(BF))
+    row = lax.broadcasted_iota(jnp.int32, (512, 512), 0) % 16
+    col = lax.broadcasted_iota(jnp.int32, (512, 512), 1) % 16
+    kron[...] = jnp.where(row == col, tall, 0.0).astype(BF)
+    for x in range(2):
+        for k in range(4):
+            chunk_copy(v, have, sems.at[0], x * 4 + k).wait()
+        grid = have.at[pl.ds(x * 2048, 2048)].reshape(C, Y, ZT)
+        done = made.at[pl.ds(x * 2048, 2048)].reshape(C, Y, ZT)
+        for g in range(4):
+            cells = grid[:, g * 16 : g * 16 + 16, :].reshape(512, ZT)
+            result = dot(kron[...], cells)
+            for c in range(C):
+                one = result[c * 16 : c * 16 + 16]
+                if bias is not None:
+                    one = one + bias[c]
+                done[c, g * 16 : g * 16 + 16, :] = one.astype(BF)
+        for k in range(4):
+            chunk_copy(made, out, sems.at[1], x * 4 + k).start()
+    for k in range(8):
+        chunk_copy(made, out, sems.at[1], k).wait()
+
+
+def linear(values, matrix, bias, turn):
+    if bias is None:
+        body = lambda v, m, *rest: linear_body(turn, v, m, None, *rest)
+        more = []
+    else:
+        body = partial(linear_body, turn)
+        more = [bias]
+    return pl.pallas_call(
+        body,
+        in_specs=[HBM, VM] + [pl.BlockSpec(memory_space=pltpu.SMEM)] * len(more),
+        out_specs=HBM,
+        out_shape=GRID_ROWS,
         scratch_shapes=[
-            pltpu.VMEM((NQ, 512, 128), F32), pltpu.VMEM((512, ZT), F32), pltpu.VMEM((NQ, 512, 128), F32),
-        ],
-        name="activate",
-    )(got, lin, cot, t["syn_mid"], t["syn_in"], t["ana_in"], t["ana_mid"])
-
-
-def finish_body(got, lin, syn_mid, syn_in, out, have):
-    step = pl.program_id(0)
-
-    @pl.when(step == 0)
-    def _():
-        unpack(got, have)
-
-    out[...] = (synthesise_rows(step, have, syn_mid, syn_in) + lin[...]).astype(BF)
-
-
-def finish(got, lin, t):
-    return pl.pallas_call(
-        finish_body,
-        grid=(8,),
-        in_specs=[whole((ND, 48, 128)), rows_spec(), whole((1024, 256)), whole((256, ZT))],
-        out_specs=rows_spec(),
-        out_shape=jax.ShapeDtypeStruct((4096, ZT), BF),
-        scratch_shapes=[pltpu.VMEM((NQ, 512, 128), F32)],
-        name="finish",
-    )(got, lin, t["syn_mid"], t["syn_in"])
-
-
-def linear_body(v, kron, bias, out):
-    out[...] = (dot(kron[...], v[...].reshape(256, ZT)) + bias[...]).reshape(C, 8, ZT)
-
-
-def linear(values, matrix, bias):
-    block = pl.BlockSpec((None, C, 8, ZT), lambda i: (i // 8, 0, i % 8, 0))
-    eye = jnp.eye(8, dtype=F32)
-    kron = (matrix.astype(F32)[:, None, :, None] * eye[None, :, None, :]).reshape(256, 256)
-    return pl.pallas_call(
-        linear_body,
-        grid=(16,),
-        in_specs=[block, whole((256, 256)), whole((256, 1))],
-        out_specs=block,
-        out_shape=jax.ShapeDtypeStruct((2, C, Y, ZT), F32),
+            pltpu.VMEM((4096, ZT), BF), pltpu.VMEM((4096, ZT), BF), pltpu.VMEM((512, 512), BF),
+            pltpu.SemaphoreType.DMA((2, 8)),
+        ],
         name="linear",
-    )(values, kron.astype(BF), jnp.repeat(bias, 8)[:, None])
+    )(values, matrix, *more)
 
 
 def weight_body(*refs):
     specs, grads = refs[:4], refs[4:8]
-    fold, out, srow, grow = refs[8:]
-    group = pl.program_id(0) % 4
-
-    @pl.when(group == 0)
-    def _():
-        for s in range(4):
-            srow[s] = specs[s][...].astype(F32)
-            grow[s] = grads[s][...].astype(F32)
+    fold, out, srow, grow, made, sem = refs[8:]
+    for s in range(4):
+        srow[s] = specs[s][...].astype(F32)
+        grow[s] = grads[s][...].astype(F32)
 
     mask = mode_mask()
     low = lax.broadcasted_iota(jnp.int32, (32, 128), 1) < 64
     blank = jnp.zeros((64, 128), F32)
 
-    def tall(ref, s, p, j, h):
-        row = ref[s, pl.ds(p * 16 + group * 4 + j, 1), h * 256 : h * 256 + 256]
+    def tall(ref, qi, group, s, p, j, h):
+        row = ref[s, qi, pl.ds(p * 16 + group * 4 + j, 1), h * 256 : h * 256 + 256]
         return jnp.where(mask, jnp.broadcast_to(row, (8, 256)), 0.0)
 
-    for h in range(2):
-        left = [tall(srow, s, p, j, h) for j in range(4) for p in range(2) for s in range(4)]
-        left = jnp.concatenate(left, axis=0).astype(BF)
-        pair = None
-        for p in range(2):
-            rows = [tall(grow, s, p, j, h) for j in range(4) for s in range(4)]
-            one = dot(jnp.concatenate(rows, axis=0).astype(BF), fold[p])
-            pair = one if pair is None else pair + one
-        blocks = []
-        for j in range(4):
-            here = pair[j * 32 : j * 32 + 32]
-            there = jnp.concatenate([here[:, 64:], here[:, :64]], axis=1)
-            if j % 2 == 0:
-                first, second = jnp.where(low, here, 0.0), jnp.where(low, there, 0.0)
-            else:
-                first, second = jnp.where(low, 0.0, there), jnp.where(low, 0.0, here)
-            piece = jnp.concatenate([first, second], axis=0)
-            blocks.append(jnp.concatenate([piece, blank] if j < 2 else [blank, piece], axis=1))
-        right = jnp.concatenate(blocks, axis=0).astype(BF)
-        grad = lax.dot_general(left, right, (((0,), (0,)), ((), ())), preferred_element_type=F32)
-        for j in range(4):
-            at = (j * 2 + h) * 256
-            out[at : at + 256, :] = grad[:, j * 64 : j * 64 + 64]
+    def copy_out(i):
+        at = pl.ds(pl.multiple_of(i * 2048, 2048), 2048)
+        return pltpu.make_async_copy(made.at[at], out.at[at], sem.at[i])
+
+    def step(i, carry):
+        qi, group = i // 4, i % 4
+        for h in range(2):
+            left = [
+                tall(srow, qi, group, s, p, j, h) for j in range(4) for p in range(2) for s in range(4)
+            ]
+            left = jnp.concatenate(left, axis=0).astype(BF)
+            pair = None
+            for p in range(2):
+                rows = [tall(grow, qi, group, s, p, j, h) for j in range(4) for s in range(4)]
+                one = dot(jnp.concatenate(rows, axis=0).astype(BF), fold[p])
+                pair = one if pair is None else pair + one
+            blocks = []
+            for j in range(4):
+                here = pair[j * 32 : j * 32 + 32]
+                there = jnp.concatenate([here[:, 64:], here[:, :64]], axis=1)
+                if j % 2 == 0:
+                    one, two = jnp.where(low, here, 0.0), jnp.where(low, there, 0.0)
+                else:
+                    one, two = jnp.where(low, 0.0, there), jnp.where(low, 0.0, here)
+                piece = jnp.concatenate([one, two], axis=0)
+                blocks.append(jnp.concatenate([piece, blank] if j < 2 else [blank, piece], axis=1))
+            right = jnp.concatenate(blocks, axis=0).astype(BF)
+            grad = lax.dot_general(left, right, (((0,), (0,)), ((), ())), preferred_element_type=F32)
+            for j in range(4):
+                at = pl.ds(pl.multiple_of(i * 2048 + (j * 2 + h) * 256, 256), 256)
+                made[at, :] = grad[:, j * 64 : j * 64 + 64]
+        copy_out(i).start()
+        return carry
+
+    lax.fori_loop(0, NQ * 4, step, 0)
+    for i in range(NQ * 4):
+        copy_out(i).wait()
 
 
 def weight_gradient(specs, grads, t):
-    rows = pl.BlockSpec((None, 32, 512), lambda i: (i // 4, 0, 0))
     return pl.pallas_call(
         weight_body,
-        grid=(NQ * 4,),
-        in_specs=[rows] * 8 + [whole((2, 256, 128))],
-        out_specs=pl.BlockSpec((None, 2048, 64), lambda i: (i // 4, i % 4, 0)),
-        out_shape=jax.ShapeDtypeStruct((NQ, 8192, 64), F32),
-        scratch_shapes=[pltpu.VMEM((4, 32, 512), F32), pltpu.VMEM((4, 32, 512), F32)],
+        in_specs=[VM] * 9,
+        out_specs=HBM,
+        out_shape=jax.ShapeDtypeStruct((NQ * 8192, 64), F32),
+        scratch_shapes=[pltpu.VMEM((4, NQ, 32, 512), F32), pltpu.VMEM((4, NQ, 32, 512), F32)]
+        + [pltpu.VMEM((NQ * 8192, 64), F32), pltpu.SemaphoreType.DMA((NQ * 4,))],
         name="weight_gradient",
     )(*specs, *grads, t["fold"])
 
@@ -457,18 +529,21 @@
     rows = field.reshape(4096, ZT)
     weights = spectral_weight.reshape(NQ, 8192, 64)
     sent = exchange(analyse(rows, t))
-    lin = linear(field[0], point_weight, bias_term)
+    lin = linear(rows, point_weight, bias_term, False)
+    sent, lin = lax.optimization_barrier((sent, lin))
     back, spec = mix_forward(sent, weights, t)
     got = exchange(back)
     specs = everyone(spec)
-    act, grad_pre, out = activate(got, lin.reshape(4096, ZT), cotangent.reshape(4096, ZT), t)
+    act, grad_pre, out = activate(got, lin, cotangent.reshape(4096, ZT), t)
     sent = exchange(out)
-    lin = linear(grad_pre.reshape(2, C, Y, ZT), point_weight.T, jnp.zeros_like(bias_term))
+    lin = linear(grad_pre, point_weight, None, True)
+    sent, lin = lax.optimization_barrier((sent, lin))
     back, grad_spec = mix_backward(sent, weights, t)
     got = exchange(back)
     grads = everyone(grad_spec)
     weight_grad = weight_gradient(specs, grads, t).reshape(NQ, MX, MY, C, 2 * C)
-    total = finish(got, lin.reshape(4096, ZT), t)
+    got, weight_grad = lax.optimization_barrier((got, weight_grad))
+    total = finish(got, lin, t)
     shape = (1, 2, C, Y, ZT)
     return act.reshape(shape), total.reshape(shape), weight_grad
 

time: 169 us -> 130 us (0.77)
  Pallas kernels: 91 us -> 64.5 us
  local copies, waits for them, and re-layouts: 13.3 us -> 3.5 us
  waiting for transfers between devices: 15.2 us -> 20.5 us
  blocking collectives: 21.4 us -> 16.1 us
  other arithmetic: 2.03 us -> 0 us
    pallas_call x6, Pallas kernels: 76.8 us -> 50.4 us  [the longest x1 13.4 us: activate(): pl.pallas_call(activate_body, in_specs=[VM, HBM, HBM, VM, VM], out_specs=...]
    convert_element_type x3 -> x0, local copies, waits for them, and re-layouts: 8.23 us -> none  [the longest x2 8.16 us: linear(): kron.astype(BF)]
    ppermute x6, waiting for transfers between devices: 3.06 us -> 9.35 us  [everyone(): pieces.append(lax.ppermute(values, 'dp', [(i, i ^ k) for i in range(4)]))]
    all_to_all x1, blocking collectives: 21.4 us -> 16.1 us  [exchange(): lax.all_to_all(values, 'slab', split_axis=0, concat_axis=0, tiled=True)]
    convert_element_type x3 -> x0, other arithmetic: 2.03 us -> none  [the longest x1 2.02 us: linear(): kron.astype(BF)]
    unnamed x24 -> x20, local copies, waits for them, and re-layouts: 3.56 us -> 3.5 us
  transfers between devices with their start and end apart: 9 -> 9, of which waited for: 2 -> 6; matrix products, arithmetic and copies ran while one was open for 7% -> 0% of each run, Pallas kernels for 23% -> 20%
where the time goes in v1:
time: 130 us; the launch traced here: 128 us
  Pallas kernels  64.5 us (50%)
  starting transfers between devices  22.9 us (18%)
  waiting for transfers between devices  20.5 us (16%)
  blocking collectives  16.1 us (12%)
  local copies, waits for them, and re-layouts  3.5 us (3%)
    all_to_all x3, starting transfers between devices, exchange(): lax.all_to_all(values, 'slab', split_axis=0, concat_axis=0, tiled=True)  19.3 us
    all_to_all x1, blocking collectives, exchange(): lax.all_to_all(values, 'slab', split_axis=0, concat_axis=0, tiled=True)  16.1 us
    pallas_call x1, Pallas kernels, activate(): pl.pallas_call(activate_body, in_specs=[VM, HBM, HBM, VM, VM], out_specs=...  13.4 us
    pallas_call x1, Pallas kernels, weight_gradient(): pl.pallas_call(weight_body, in_specs=[VM] * 9, out_specs=HBM, out_shape=j...  12.7 us
    pallas_call x2, Pallas kernels, linear(): pl.pallas_call(body, in_specs=[HBM, VM] + [pl.BlockSpec(memory_space=pltp...  12.5 us
    all_to_all x3, waiting for transfers between devices, exchange(): lax.all_to_all(values, 'slab', split_axis=0, concat_axis=0, tiled=True)  11.2 us
    ppermute x6, waiting for transfers between devices, everyone(): pieces.append(lax.ppermute(values, 'dp', [(i, i ^ k) for i in range(4)]))  9.35 us
    pallas_call x1, Pallas kernels, mix_backward(): pl.pallas_call(mix_backward_body, grid=(NQ,), in_specs=[slot_spec(), sque...  7.43 us
  transfers between devices with their start and end apart: 9, of which 6 were waited for; matrix products, arithmetic and copies ran while one was open for 0% of the time, Pallas kernels for 20%

profile of v1, /device:TPU:0, one launch (start us, length us, event | category | flops | bytes accessed | tf_op | source)
XLA Modules:
  0.0 128.4 jit_solution(6110616965584971974)
XLA Ops:
  0.6 6.2 %analyse.1 = bf16[32,48,128]{2,1,0:T(8,128)(2,1)} custom-call(bf16[4096,512]{1,0:T(8,128)(2,1)} %bitcast.8, bf16[256,512]{1,0:T(8,128)(2,1)} %constant.16.clone.depth, bf16[1024,256]{1,0:T(8,128)(2,1)} %constant.17.clone.middle), custom_call_target="tpu_custom_call" | custom-call | tf_op jit(solution)/shard_map/analyse/pallas_call | solution.py:148
  6.8 10.9 %all-to-all-start = ((bf16[32,48,128]{2,1,0:T(8,128)(2,1)}), bf16[32,48,128]{2,1,0:T(8,128)(2,1)S(1)}, u32[]{:S(2)}, u32[]{:S(2)}) async-start(bf16[32,48,128]{2,1,0:T(8,128)(2,1)} %analyse.1), calls=%async_computation | async-start | bytes 786432 | tf_op jit(solution)/shard_map/all_to_all | solution.py:517
  17.7 6.3 %linear.2.lin = bf16[4096,512]{1,0:T(8,128)(2,1)} custom-call(bf16[4096,512]{1,0:T(8,128)(2,1)} %bitcast.9, bf16[32,32]{1,0:T(8,128)(2,1)} %m.1, f32[32]{0:T(128)} %bias.1), custom_call_target="tpu_custom_call" | custom-call | tf_op jit(solution)/shard_map/linear/pallas_call | solution.py:437
  24.0 5.9 %all-to-all-done.got = bf16[32,48,128]{2,1,0:T(8,128)(2,1)S(1)} async-done(((bf16[32,48,128]{2,1,0:T(8,128)(2,1)}), bf16[32,48,128]{2,1,0:T(8,128)(2,1)S(1)}, u32[]{:S(2)}, u32[]{:S(2)}) %all-to-all-start) | async-done | bytes 393248 | tf_op jit(solution)/shard_map/all_to_all | solution.py:517
  29.9 0.7 copy-done.2
  30.7 6.6 %mix_forward.1 = (bf16[32,48,128]{2,1,0:T(8,128)(2,1)}, bf16[3,32,512]{2,1,0:T(8,128)(2,1)}) custom-call(bf16[32,48,128]{2,1,0:T(8,128)(2,1)} %copy-done.2, bf16[3,8192,64]{2,1,0:T(8,128)(2,1)} %bitcast.6, bf16[128,512]{1,0:T(8,128)(2,1)} %constant.18.clone.ana_out, bf16[512,512]{1,0:T(8,128)(2,1)} %constant.21.clone.perm, ...), custom_call_target="tpu_custom_call" | custom-call | tf_op jit(solution)/shard_map/mix_forward/pallas_call | solution.py:220
  37.3 16.1 %all_to_all.20.got = bf16[32,48,128]{2,1,0:T(8,128)(2,1)} all-to-all(bf16[32,48,128]{2,1,0:T(8,128)(2,1)} %get-tuple-element.17), channel_id=1, replica_groups=mesh['slab'=32,'dp'=4] {'slab'}, dimensions={0} | all-to-all | bytes 786432 | tf_op jit(solution)/shard_map/all_to_all | solution.py:517
  53.4 13.4 %activate.1 = (bf16[4096,512]{1,0:T(8,128)(2,1)}, bf16[4096,512]{1,0:T(8,128)(2,1)}, bf16[32,48,128]{2,1,0:T(8,128)(2,1)}) custom-call(bf16[32,48,128]{2,1,0:T(8,128)(2,1)} %all_to_all.20.got, bf16[4096,512]{1,0:T(8,128)(2,1)} %linear.2.lin, bf16[4096,512]{1,0:T(8,128)(2,1)} %bitcast.11, bf16[256,512]{1,0:T(8,128)(2,1)} %constant.16.clone.depth, ...), custom_call_target="tpu_custom_call" | custom-call | tf_op jit(solution)/shard_map/activate/pallas_call | solution.py:353
  66.8 3.9 %all-to-all-start.2 = ((bf16[32,48,128]{2,1,0:T(8,128)(2,1)}), bf16[32,48,128]{2,1,0:T(8,128)(2,1)S(1)}, u32[]{:S(2)}, u32[]{:S(2)}) async-start(bf16[32,48,128]{2,1,0:T(8,128)(2,1)} %get-tuple-element.20), calls=%async_computation.2 | async-start | bytes 786432 | tf_op jit(solution)/shard_map/all_to_all | solution.py:517
  70.7 6.2 %linear.3.lin = bf16[4096,512]{1,0:T(8,128)(2,1)} custom-call(bf16[4096,512]{1,0:T(8,128)(2,1)} %get-tuple-element.21.v, bf16[32,32]{1,0:T(8,128)(2,1)} %m.1), custom_call_target="tpu_custom_call" | custom-call | tf_op jit(solution)/shard_map/linear/pallas_call | solution.py:437
  76.9 5.3 %all-to-all-done.2.got = bf16[32,48,128]{2,1,0:T(8,128)(2,1)S(1)} async-done(((bf16[32,48,128]{2,1,0:T(8,128)(2,1)}), bf16[32,48,128]{2,1,0:T(8,128)(2,1)S(1)}, u32[]{:S(2)}, u32[]{:S(2)}) %all-to-all-start.2) | async-done | bytes 393248 | tf_op jit(solution)/shard_map/all_to_all | solution.py:517
  82.2 0.7 copy-done.1
  83.0 7.4 %mix_backward.1 = (bf16[32,48,128]{2,1,0:T(8,128)(2,1)}, bf16[3,32,512]{2,1,0:T(8,128)(2,1)}) custom-call(bf16[32,48,128]{2,1,0:T(8,128)(2,1)} %copy-done.1, bf16[3,8192,64]{2,1,0:T(8,128)(2,1)} %bitcast.7, bf16[128,512]{1,0:T(8,128)(2,1)} %constant.18.clone.ana_out, bf16[512,512]{1,0:T(8,128)(2,1)} %constant.21.clone.perm, ...), custom_call_target="tpu_custom_call" | custom-call | tf_op jit(solution)/shard_map/mix_backward/pallas_call | solution.py:271
  90.4 4.5 %all-to-all-start.3 = ((bf16[32,48,128]{2,1,0:T(8,128)(2,1)}), bf16[32,48,128]{2,1,0:T(8,128)(2,1)S(1)}, u32[]{:S(2)}, u32[]{:S(2)}) async-start(bf16[32,48,128]{2,1,0:T(8,128)(2,1)} %get-tuple-element.23), calls=%async_computation.3 | async-start | bytes 786432 | tf_op jit(solution)/shard_map/all_to_all | solution.py:517
  95.0 0.8 collective-permute-start.1
  95.8 1.1 collective-permute-start
  97.2 1.3 collective-permute-start.4
  98.5 3.0 %collective-permute-done.2.refs_3_ = bf16[3,32,512]{2,1,0:T(8,128)(2,1)S(1)} collective-permute-done((bf16[3,32,512]{2,1,0:T(8,128)(2,1)S(1)}, bf16[3,32,512]{2,1,0:T(8,128)(2,1)S(1)}, u32[]{:S(2)}, u32[]{:S(2)}) %collective-permute-start.2) | collective-permute-done | bytes 98336 | tf_op jit(solution)/shard_map/ppermute | solution.py:523
  101.6 2.1 %collective-permute-done.1.refs_2_ = bf16[3,32,512]{2,1,0:T(8,128)(2,1)S(1)} collective-permute-done((bf16[3,32,512]{2,1,0:T(8,128)(2,1)S(1)}, bf16[3,32,512]{2,1,0:T(8,128)(2,1)S(1)}, u32[]{:S(2)}, u32[]{:S(2)}) %collective-permute-start.1) | collective-permute-done | bytes 98336 | tf_op jit(solution)/shard_map/ppermute | solution.py:523
  103.7 2.2 %collective-permute-done.5.refs_7_ = bf16[3,32,512]{2,1,0:T(8,128)(2,1)S(1)} collective-permute-done((bf16[3,32,512]{2,1,0:T(8,128)(2,1)}, bf16[3,32,512]{2,1,0:T(8,128)(2,1)S(1)}, u32[]{:S(2)}, u32[]{:S(2)}) %collective-permute-start.5) | collective-permute-done | bytes 98336 | tf_op jit(solution)/shard_map/ppermute | solution.py:523
  105.9 2.0 %collective-permute-done.4.refs_6_ = bf16[3,32,512]{2,1,0:T(8,128)(2,1)S(1)} collective-permute-done((bf16[3,32,512]{2,1,0:T(8,128)(2,1)}, bf16[3,32,512]{2,1,0:T(8,128)(2,1)S(1)}, u32[]{:S(2)}, u32[]{:S(2)}) %collective-permute-start.4) | collective-permute-done | bytes 98336 | tf_op jit(solution)/shard_map/ppermute | solution.py:523
  109.1 12.7 %weight_gradient.1 = f32[24576,64]{1,0:T(8,128)} custom-call(bf16[3,32,512]{2,1,0:T(8,128)(2,1)} %get-tuple-element.24.refs_0_, bf16[3,32,512]{2,1,0:T(8,128)(2,1)} %copy-done.6, bf16[3,32,512]{2,1,0:T(8,128)(2,1)} %copy-done.5, bf16[3,32,512]{2,1,0:T(8,128)(2,1)} %copy-done.4, bf16[3,32,512]{2,1,0:T(8,128)(2,1)} %get-tuple-element.25.refs_4_, ...), custom_call_target="tpu_custom_call" | custom-call | tf_op jit(solution)/shard_map/weight_gradient/pallas_call | solution.py:505
  121.9 0.7 copy-done
  122.7 5.6 %finish.1 = bf16[4096,512]{1,0:T(8,128)(2,1)} custom-call(bf16[32,48,128]{2,1,0:T(8,128)(2,1)} %copy-done, bf16[4096,512]{1,0:T(8,128)(2,1)} %linear.3.lin, bf16[256,512]{1,0:T(8,128)(2,1)} %constant.16.clone.depth, bf16[1024,256]{1,0:T(8,128)(2,1)} %constant.17.clone.middle), custom_call_target="tpu_custom_call" | custom-call | tf_op jit(solution)/shard_map/finish/pallas_call | solution.py:386
  (23 shorter events, 1.7 us)
Async XLA Ops:
  6.8 23.1 %all-to-all-start = ((bf16[32,48,128]{2,1,0:T(8,128)(2,1)}), bf16[32,48,128]{2,1,0:T(8,128)(2,1)S(1)}, u32[]{:S(2)}, u32[]{:S(2)}) async-start(bf16[32,48,128]{2,1,0:T(8,128)(2,1)} %analyse.1), calls=%async_computation | async-start | bytes 786432 | tf_op jit(solution)/shard_map/all_to_all | solution.py:517
  29.9 0.7 copy-start.2
  66.8 15.4 %all-to-all-start.2 = ((bf16[32,48,128]{2,1,0:T(8,128)(2,1)}), bf16[32,48,128]{2,1,0:T(8,128)(2,1)S(1)}, u32[]{:S(2)}, u32[]{:S(2)}) async-start(bf16[32,48,128]{2,1,0:T(8,128)(2,1)} %get-tuple-element.20), calls=%async_computation.2 | async-start | bytes 786432 | tf_op jit(solution)/shard_map/all_to_all | solution.py:517
  76.9 18.0 %copy-start.3 = (bf16[3,32,512]{2,1,0:T(8,128)(2,1)S(1)}, bf16[3,32,512]{2,1,0:T(8,128)(2,1)}, u32[]{:S(2)}) copy-start(bf16[3,32,512]{2,1,0:T(8,128)(2,1)} %get-tuple-element.24.refs_0_) | copy-start | bytes 294916
  82.2 0.7 copy-start.1
  90.4 31.5 %all-to-all-start.3 = ((bf16[32,48,128]{2,1,0:T(8,128)(2,1)}), bf16[32,48,128]{2,1,0:T(8,128)(2,1)S(1)}, u32[]{:S(2)}, u32[]{:S(2)}) async-start(bf16[32,48,128]{2,1,0:T(8,128)(2,1)} %get-tuple-element.23), calls=%async_computation.3 | async-start | bytes 786432 | tf_op jit(solution)/shard_map/all_to_all | solution.py:517
  94.9 6.6 %collective-permute-start.2 = (bf16[3,32,512]{2,1,0:T(8,128)(2,1)S(1)}, bf16[3,32,512]{2,1,0:T(8,128)(2,1)S(1)}, u32[]{:S(2)}, u32[]{:S(2)}) collective-permute-start(bf16[3,32,512]{2,1,0:T(8,128)(2,1)S(1)} %copy-done.3), channel_id=1, source_target_pairs={{0,3},{1,2},{2,1},{3,0},{4,7},{5,6},{6,5},{7,4},{8,11},{9,10},{10,... | collective-permute-start | bytes 294920 | tf_op jit(solution)/shard_map/ppermute | solution.py:523
  95.0 8.6 %collective-permute-start.1 = (bf16[3,32,512]{2,1,0:T(8,128)(2,1)S(1)}, bf16[3,32,512]{2,1,0:T(8,128)(2,1)S(1)}, u32[]{:S(2)}, u32[]{:S(2)}) collective-permute-start(bf16[3,32,512]{2,1,0:T(8,128)(2,1)S(1)} %copy-done.3), channel_id=1, source_target_pairs={{0,2},{1,3},{2,0},{3,1},{4,6},{5,7},{6,4},{7,5},{8,10},{9,11},{10,... | collective-permute-start | bytes 294920 | tf_op jit(solution)/shard_map/ppermute | solution.py:523
  95.8 7.9 %collective-permute-start = (bf16[3,32,512]{2,1,0:T(8,128)(2,1)S(1)}, bf16[3,32,512]{2,1,0:T(8,128)(2,1)S(1)}, u32[]{:S(2)}, u32[]{:S(2)}) collective-permute-start(bf16[3,32,512]{2,1,0:T(8,128)(2,1)S(1)} %copy-done.3), channel_id=1, source_target_pairs={{0,1},{1,0},{2,3},{3,2},{4,5},{5,4},{6,7},{7,6},{8,9},{9,8},{10,11... | collective-permute-start | bytes 294920 | tf_op jit(solution)/shard_map/ppermute | solution.py:523
  96.9 9.0 %collective-permute-start.5 = (bf16[3,32,512]{2,1,0:T(8,128)(2,1)}, bf16[3,32,512]{2,1,0:T(8,128)(2,1)S(1)}, u32[]{:S(2)}, u32[]{:S(2)}) collective-permute-start(bf16[3,32,512]{2,1,0:T(8,128)(2,1)} %get-tuple-element.25.refs_4_), channel_id=1, source_target_pairs={{0,3},{1,2},{2,1},{3,0},{4,7},{5,6},{6,5},{7,4},{8,11},{9,10},{10,... | collective-permute-start | bytes 294920 | tf_op jit(solution)/shard_map/ppermute | solution.py:523
  97.2 10.6 %collective-permute-start.4 = (bf16[3,32,512]{2,1,0:T(8,128)(2,1)}, bf16[3,32,512]{2,1,0:T(8,128)(2,1)S(1)}, u32[]{:S(2)}, u32[]{:S(2)}) collective-permute-start(bf16[3,32,512]{2,1,0:T(8,128)(2,1)} %get-tuple-element.25.refs_4_), channel_id=1, source_target_pairs={{0,2},{1,3},{2,0},{3,1},{4,6},{5,7},{6,4},{7,5},{8,10},{9,11},{10,... | collective-permute-start | bytes 294920 | tf_op jit(solution)/shard_map/ppermute | solution.py:523
  101.6 6.3 %copy-start.4 = (bf16[3,32,512]{2,1,0:T(8,128)(2,1)}, bf16[3,32,512]{2,1,0:T(8,128)(2,1)S(1)}, u32[]{:S(2)}) copy-start(bf16[3,32,512]{2,1,0:T(8,128)(2,1)S(1)} %collective-permute-done.2.refs_3_) | copy-start | bytes 294916
  101.6 6.3 %collective-permute-start.3 = (bf16[3,32,512]{2,1,0:T(8,128)(2,1)}, bf16[3,32,512]{2,1,0:T(8,128)(2,1)S(1)}, u32[]{:S(2)}, u32[]{:S(2)}) collective-permute-start(bf16[3,32,512]{2,1,0:T(8,128)(2,1)} %get-tuple-element.25.refs_4_), channel_id=1, source_target_pairs={{0,1},{1,0},{2,3},{3,2},{4,5},{5,4},{6,7},{7,6},{8,9},{9,8},{10,11... | collective-permute-start | bytes 294920 | tf_op jit(solution)/shard_map/ppermute | solution.py:523
  103.7 4.2 %copy-start.5 = (bf16[3,32,512]{2,1,0:T(8,128)(2,1)}, bf16[3,32,512]{2,1,0:T(8,128)(2,1)S(1)}, u32[]{:S(2)}) copy-start(bf16[3,32,512]{2,1,0:T(8,128)(2,1)S(1)} %collective-permute-done.1.refs_2_) | copy-start | bytes 294916
  103.7 4.2 %copy-start.6 = (bf16[3,32,512]{2,1,0:T(8,128)(2,1)}, bf16[3,32,512]{2,1,0:T(8,128)(2,1)S(1)}, u32[]{:S(2)}) copy-start(bf16[3,32,512]{2,1,0:T(8,128)(2,1)S(1)} %collective-permute-done.refs_1_) | copy-start | bytes 294916
  105.9 2.0 %copy-start.7 = (bf16[3,32,512]{2,1,0:T(8,128)(2,1)}, bf16[3,32,512]{2,1,0:T(8,128)(2,1)S(1)}, u32[]{:S(2)}) copy-start(bf16[3,32,512]{2,1,0:T(8,128)(2,1)S(1)} %collective-permute-done.5.refs_7_) | copy-start | bytes 294916
  107.9 0.6 copy-start.8
  108.5 0.6 copy-start.9
  121.9 0.8 copy-start

commit v2 on v1

--- a/solution.py
+++ b/solution.py
@@ -61,12 +61,6 @@
     syn_out = out.reshape(2, MX, 2, ND, 2).transpose(2, 4, 3, 0, 1)
     fwd_out = np.repeat(syn_out.reshape(128, 32), 16, axis=1)
     bwd_out = np.repeat(syn_out.reshape(128, 32), 8, axis=1)
-    perm = np.zeros((4, MY, 8, MY, 4, 8), np.float32)
-    for g in range(4):
-        for k in range(MY):
-            for c in range(8):
-                perm[g, k, c, k, g, c] = 1.0
-    perm = perm.reshape(512, 512)
     spread = np.zeros((2, 2, 4, 8, 4, MY, 8), np.float32)
     for g in range(4):
         for c in range(8):
@@ -79,10 +73,10 @@
         fold[0, :, o, 96 + o] = -1.0
         fold[1, :, o, 32 + o] = 1.0
         fold[1, :, o, 64 + o] = 1.0
-    fold = fold.reshape(2, 256, 128)
+    fold = fold.reshape(512, 128)
     t = dict(
         depth=depth, middle=middle, ana_out=ana_out, fwd_out=fwd_out * SCALE, bwd_out=bwd_out,
-        perm=perm, spread=spread, fold=fold,
+        spread=spread, fold=fold,
     )
     return {k: jnp.asarray(v, BF) for k, v in t.items()}
 
@@ -138,7 +132,7 @@
     return pl.BlockSpec(shape, lambda i: (0,) * len(shape))
 
 
-HBM = pl.BlockSpec(memory_space=pl.ANY)
+HBM = pl.BlockSpec(memory_space=pltpu.HBM)
 VM = pl.BlockSpec(memory_space=pltpu.VMEM)
 GRID_ROWS = jax.ShapeDtypeStruct((4096, ZT), BF)
 SENT = jax.ShapeDtypeStruct((ND, 48, 128), BF)
@@ -155,16 +149,28 @@
             pltpu.VMEM((NQ, 512, 128), F32), pltpu.SemaphoreType.DMA((8,)),
         ],
         name="analyse",
+        compiler_params=pltpu.CompilerParams(vmem_limit_bytes=52 << 20),
     )(values, t["depth"], t["middle"])
 
 
+def channel_order(perm):
+    row = lax.broadcasted_iota(jnp.int32, (512, 512), 0)
+    col = lax.broadcasted_iota(jnp.int32, (512, 512), 1)
+    place = row // 8 % 16 * 32 + row // 128 * 8 + row % 8
+    perm[...] = jnp.where(place == col, 1.0, 0.0).astype(BF)
+
+
 def spectrum_rows(got, ana_out, perm, scale):
-    parts = dot(ana_out[...], got[...].reshape(512, 128))
+    tall = [got[:, q * 16 : q * 16 + 16, :].reshape(512, 128) for q in range(NQ)]
+    parts = dot(ana_out[...], jnp.concatenate(tall, axis=1))
     if scale is not None:
         parts = parts * scale
     parts = parts.astype(BF)
-    joined = jnp.concatenate([parts[g * 32 : g * 32 + 32] for g in range(4)], axis=1)
-    return dot(joined, perm[...])
+    rows = [
+        jnp.concatenate([parts[g * 32 : g * 32 + 32, q * 128 : q * 128 + 128] for g in range(4)], axis=1)
+        for q in range(NQ)
+    ]
+    return dot(jnp.concatenate(rows, axis=0), perm[...])
 
 
 def mode_mask():
@@ -172,120 +178,128 @@
     return lane == lax.broadcasted_iota(jnp.int32, (8, 256), 0)
 
 
-def scatter_owner(synth, work, out):
+def scatter_owner(synth, q, work, out):
     for r in range(2):
         for xi in range(2):
             for g in range(4):
                 at = (r * 2 + xi) * 32
-                work[pl.ds(r * 8 + xi * 4 + g, ND, stride=16), :] = synth[
+                work[q, pl.ds(r * 8 + xi * 4 + g, ND, stride=16), :] = synth[
                     at : at + 32, g * 128 : g * 128 + 128
                 ]
-    out[...] = work[...].reshape(ND, 16, 128).astype(BF)
-
-
-def mix_forward_body(got, w, ana_out, perm, spread, fwd_out, out, spec, srow, mixed, work):
+    out[:, q * 16 : q * 16 + 16, :] = work[q].reshape(ND, 16, 128).astype(BF)
+
+
+def weight_copy(w, have, sem, q):
+    return pltpu.make_async_copy(w.at[q], have.at[q], sem.at[q])
+
+
+def mix_forward_body(
+    got, w, ana_out, spread, fwd_out, out, spec, have, srow, mixed, work, perm, sem
+):
+    for q in range(NQ):
+        weight_copy(w, have, sem, q).start()
+    channel_order(perm)
     rows = spectrum_rows(got, ana_out, perm, None)
-    spec[...] = rows.astype(BF)
     srow[...] = rows
+    for q in range(NQ):
+        spec[q] = rows[q * 32 : q * 32 + 32].astype(BF)
     mask = mode_mask()
-    for kx in range(MX):
-        for h in range(2):
-            lanes = slice(h * 256, h * 256 + 256)
-            real = jnp.where(mask, jnp.broadcast_to(srow[kx : kx + 1, lanes], (8, 256)), 0.0)
-            imag = jnp.where(mask, jnp.broadcast_to(srow[16 + kx : 17 + kx, lanes], (8, 256)), 0.0)
-            left = jnp.concatenate([real, imag], axis=0).astype(BF)
-            at = (kx * 2 + h) * 256
-            both = dot(left, w[at : at + 256, :])
-            low = both[8:16]
-            turned = jnp.concatenate([-low[:, 32:], low[:, :32]], axis=1)
-            mixed[kx * 16 + h * 8 : kx * 16 + h * 8 + 8, :] = both[:8] + turned
-    values = mixed[...].astype(BF)
     row_ky = lax.broadcasted_iota(jnp.int32, (256, 512), 0) % 16
     lane_ky = lax.broadcasted_iota(jnp.int32, (256, 512), 1) // 8 % 16
     same = row_ky == lane_ky
-    wide = [jnp.where(same, dot(values, spread[p]), 0.0).astype(BF) for p in range(2)]
-    synth = dot(fwd_out[...], jnp.concatenate(wide, axis=0))
-    scatter_owner(synth, work, out)
-
-
-def squeezed(shape):
-    return pl.BlockSpec((None,) + shape, lambda i: (i,) + (0,) * len(shape))
-
-
-def slot_spec():
-    return pl.BlockSpec((ND, 16, 128), lambda i: (0, i, 0))
+    for q in range(NQ):
+        weight_copy(w, have, sem, q).wait()
+        for kx in range(MX):
+            for h in range(2):
+                lanes = slice(h * 256, h * 256 + 256)
+                at = q * 32 + kx
+                real = jnp.where(mask, jnp.broadcast_to(srow[at : at + 1, lanes], (8, 256)), 0.0)
+                at = at + 16
+                imag = jnp.where(mask, jnp.broadcast_to(srow[at : at + 1, lanes], (8, 256)), 0.0)
+                left = jnp.concatenate([real, imag], axis=0).astype(BF)
+                at = (kx * 2 + h) * 256
+                both = dot(left, have[q, at : at + 256, :])
+                low = both[8:16]
+                turned = jnp.concatenate([-low[:, 32:], low[:, :32]], axis=1)
+                at = kx * 16 + h * 8
+                mixed[q, at : at + 8, :] = both[:8] + turned
+        values = mixed[q].astype(BF)
+        wide = [jnp.where(same, dot(values, spread[p]), 0.0).astype(BF) for p in range(2)]
+        synth = dot(fwd_out[...], jnp.concatenate(wide, axis=0))
+        scatter_owner(synth, q, work, out)
+
+
+SPECTRUM = jax.ShapeDtypeStruct((NQ, 32, 512), BF)
 
 
 def mix_forward(got, weights, t):
     return pl.pallas_call(
         mix_forward_body,
-        grid=(NQ,),
-        in_specs=[
-            slot_spec(), squeezed((8192, 64)), whole((128, 512)), whole((512, 512)),
-            whole((2, 64, 512)), whole((128, 512)),
-        ],
-        out_specs=[slot_spec(), squeezed((32, 512))],
-        out_shape=[
-            jax.ShapeDtypeStruct((ND, 48, 128), BF),
-            jax.ShapeDtypeStruct((NQ, 32, 512), BF),
-        ],
+        in_specs=[VM, HBM, VM, VM, VM],
+        out_specs=[VM, VM],
+        out_shape=[SENT, SPECTRUM],
         scratch_shapes=[
-            pltpu.VMEM((32, 512), F32), pltpu.VMEM((256, 64), F32), pltpu.VMEM((512, 128), F32),
+            pltpu.VMEM((NQ, 8192, 64), BF), pltpu.VMEM((96, 512), F32), pltpu.VMEM((NQ, 256, 64), F32),
+            pltpu.VMEM((NQ, 512, 128), F32), pltpu.VMEM((512, 512), BF),
+            pltpu.SemaphoreType.DMA((NQ,)),
         ],
         name="mix_forward",
-    )(got, weights, t["ana_out"], t["perm"], t["spread"], t["fwd_out"])
+        compiler_params=pltpu.CompilerParams(vmem_limit_bytes=52 << 20),
+    )(got, weights, t["ana_out"], t["spread"], t["fwd_out"])
 
 
 def mix_backward_body(
-    got, w, ana_out, perm, fold, bwd_out, out, spec, srow, pair, masked, work
+    got, w, ana_out, fold, bwd_out, out, spec, have, srow, pair, masked, work, perm, sem
 ):
+    for q in range(NQ):
+        weight_copy(w, have, sem, q).start()
+    channel_order(perm)
     rows = spectrum_rows(got, ana_out, perm, SCALE)
-    spec[...] = rows.astype(BF)
     srow[...] = rows
+    for q in range(NQ):
+        spec[q] = rows[q * 32 : q * 32 + 32].astype(BF)
     mask = mode_mask()
     for h in range(2):
-        total = None
+        lanes = slice(h * 256, h * 256 + 256)
+        sides = []
         for part in range(2):
-            lanes = slice(h * 256, h * 256 + 256)
             tall = [
                 jnp.where(mask, jnp.broadcast_to(srow[k : k + 1, lanes], (8, 256)), 0.0)
-                for k in range(part * 16, part * 16 + 16)
+                for q in range(NQ)
+                for k in range(q * 32 + part * 16, q * 32 + part * 16 + 16)
             ]
-            one = dot(jnp.concatenate(tall, axis=0).astype(BF), fold[part])
-            total = one if total is None else total + one
-        pair[h] = total
-    for kx in range(MX):
-        for h in range(2):
-            both = pair[h, kx * 8 : kx * 8 + 8, :]
-            left = jnp.concatenate([both[:, :64], both[:, 64:]], axis=0).astype(BF)
-            at = (kx * 2 + h) * 256
-            full = dot_t(left, w[at : at + 256, :])
-            masked[h, kx * 8 : kx * 8 + 8, :] = jnp.where(mask, full[:8], 0.0)
-            masked[h, 128 + kx * 8 : 136 + kx * 8, :] = jnp.where(mask, full[8:], 0.0)
-    synth = [dot(bwd_out[...], masked[h].astype(BF)).astype(BF) for h in range(2)]
-    turned = dot_t(jnp.concatenate(synth, axis=1), perm[...])
-    scatter_owner(turned, work, out)
+            sides.append(jnp.concatenate(tall, axis=0).astype(BF))
+        pair[h] = dot(jnp.concatenate(sides, axis=1), fold[...])
+    for q in range(NQ):
+        weight_copy(w, have, sem, q).wait()
+        for kx in range(MX):
+            for h in range(2):
+                at = q * 128 + kx * 8
+                both = pair[h, at : at + 8, :]
+                left = jnp.concatenate([both[:, :64], both[:, 64:]], axis=0).astype(BF)
+                at = (kx * 2 + h) * 256
+                full = dot_t(left, have[q, at : at + 256, :])
+                masked[q, h, kx * 8 : kx * 8 + 8, :] = jnp.where(mask, full[:8], 0.0)
+                masked[q, h, 128 + kx * 8 : 136 + kx * 8, :] = jnp.where(mask, full[8:], 0.0)
+        synth = [dot(bwd_out[...], masked[q, h].astype(BF)).astype(BF) for h in range(2)]
+        turned = dot_t(jnp.concatenate(synth, axis=1), perm[...])
+        scatter_owner(turned, q, work, out)
 
 
 def mix_backward(got, weights, t):
     return pl.pallas_call(
         mix_backward_body,
-        grid=(NQ,),
-        in_specs=[
-            slot_spec(), squeezed((8192, 64)), whole((128, 512)), whole((512, 512)),
-            whole((2, 256, 128)), whole((128, 256)),
-        ],
-        out_specs=[slot_spec(), squeezed((32, 512))],
-        out_shape=[
-            jax.ShapeDtypeStruct((ND, 48, 128), BF),
-            jax.ShapeDtypeStruct((NQ, 32, 512), BF),
-        ],
+        in_specs=[VM, HBM, VM, VM, VM],
+        out_specs=[VM, VM],
+        out_shape=[SENT, SPECTRUM],
         scratch_shapes=[
-            pltpu.VMEM((32, 512), F32), pltpu.VMEM((2, 128, 128), F32),
-            pltpu.VMEM((2, 256, 256), F32), pltpu.VMEM((512, 128), F32),
+            pltpu.VMEM((NQ, 8192, 64), BF), pltpu.VMEM((96, 512), F32), pltpu.VMEM((2, 384, 128), F32),
+            pltpu.VMEM((NQ, 2, 256, 256), F32), pltpu.VMEM((NQ, 512, 128), F32),
+            pltpu.VMEM((512, 512), BF), pltpu.SemaphoreType.DMA((NQ,)),
         ],
         name="mix_backward",
-    )(got, weights, t["ana_out"], t["perm"], t["fold"], t["bwd_out"])
+        compiler_params=pltpu.CompilerParams(vmem_limit_bytes=52 << 20),
+    )(got, weights, t["ana_out"], t["fold"], t["bwd_out"])
 
 
 def unpack(got, have, turned, middle, tall):
@@ -307,7 +321,7 @@
 
 
 ROOT = math.sqrt(2.0 / math.pi)
-CHUNK = 128
+CHUNK = 512
 
 
 def activate_body(
@@ -362,6 +376,7 @@
             pltpu.SemaphoreType.DMA((4, 8)),
         ],
         name="activate",
+        compiler_params=pltpu.CompilerParams(vmem_limit_bytes=52 << 20),
     )(got, lin, cot, t["depth"], t["middle"])
 
 
@@ -392,6 +407,7 @@
         + SYNTH_SCRATCH
         + [pltpu.SemaphoreType.DMA((2, 8))],
         name="finish",
+        compiler_params=pltpu.CompilerParams(vmem_limit_bytes=52 << 20),
     )(got, lin, t["depth"], t["middle"])
 
 
@@ -444,72 +460,81 @@
             pltpu.SemaphoreType.DMA((2, 8)),
         ],
         name="linear",
+        compiler_params=pltpu.CompilerParams(vmem_limit_bytes=52 << 20),
     )(values, matrix, *more)
 
 
 def weight_body(*refs):
-    specs, grads = refs[:4], refs[4:8]
-    fold, out, srow, grow, made, sem = refs[8:]
-    for s in range(4):
-        srow[s] = specs[s][...].astype(F32)
-        grow[s] = grads[s][...].astype(F32)
+    specs, grads = refs[:2], refs[2:4]
+    fold, out, srow, grow, made, sem = refs[4:]
+    for i in range(2):
+        srow[i * 2 : i * 2 + 2] = specs[i][...].astype(F32)
+        grow[i * 2 : i * 2 + 2] = grads[i][...].astype(F32)
 
     mask = mode_mask()
     low = lax.broadcasted_iota(jnp.int32, (32, 128), 1) < 64
     blank = jnp.zeros((64, 128), F32)
 
-    def tall(ref, qi, group, s, p, j, h):
-        row = ref[s, qi, pl.ds(p * 16 + group * 4 + j, 1), h * 256 : h * 256 + 256]
+    def tall(ref, q, s, k, h):
+        row = ref[s, q, k : k + 1, h * 256 : h * 256 + 256]
         return jnp.where(mask, jnp.broadcast_to(row, (8, 256)), 0.0)
 
-    def copy_out(i):
-        at = pl.ds(pl.multiple_of(i * 2048, 2048), 2048)
-        return pltpu.make_async_copy(made.at[at], out.at[at], sem.at[i])
-
-    def step(i, carry):
-        qi, group = i // 4, i % 4
+    def copy_out(q):
+        return pltpu.make_async_copy(made.at[q], out.at[q], sem.at[q])
+
+    def step(q, carry):
         for h in range(2):
-            left = [
-                tall(srow, qi, group, s, p, j, h) for j in range(4) for p in range(2) for s in range(4)
+            sides = [
+                jnp.concatenate(
+                    [tall(grow, q, s, p * 16 + kx, h) for kx in range(MX) for s in range(4)], axis=0
+                ).astype(BF)
+                for p in range(2)
             ]
-            left = jnp.concatenate(left, axis=0).astype(BF)
-            pair = None
-            for p in range(2):
-                rows = [tall(grow, qi, group, s, p, j, h) for j in range(4) for s in range(4)]
-                one = dot(jnp.concatenate(rows, axis=0).astype(BF), fold[p])
-                pair = one if pair is None else pair + one
-            blocks = []
-            for j in range(4):
-                here = pair[j * 32 : j * 32 + 32]
-                there = jnp.concatenate([here[:, 64:], here[:, :64]], axis=1)
-                if j % 2 == 0:
-                    one, two = jnp.where(low, here, 0.0), jnp.where(low, there, 0.0)
-                else:
-                    one, two = jnp.where(low, 0.0, there), jnp.where(low, 0.0, here)
-                piece = jnp.concatenate([one, two], axis=0)
-                blocks.append(jnp.concatenate([piece, blank] if j < 2 else [blank, piece], axis=1))
-            right = jnp.concatenate(blocks, axis=0).astype(BF)
-            grad = lax.dot_general(left, right, (((0,), (0,)), ((), ())), preferred_element_type=F32)
-            for j in range(4):
-                at = pl.ds(pl.multiple_of(i * 2048 + (j * 2 + h) * 256, 256), 256)
-                made[at, :] = grad[:, j * 64 : j * 64 + 64]
-        copy_out(i).start()
+            pair = dot(jnp.concatenate(sides, axis=1), fold[...])
+            for group in range(4):
+                left = [
+                    tall(srow, q, s, p * 16 + group * 4 + j, h)
+                    for j in range(4)
+                    for p in range(2)
+                    for s in range(4)
+                ]
+                left = jnp.concatenate(left, axis=0).astype(BF)
+                blocks = []
+                for j in range(4):
+                    at = (group * 4 + j) * 32
+                    here = pair[at : at + 32]
+                    there = jnp.concatenate([here[:, 64:], here[:, :64]], axis=1)
+                    if j % 2 == 0:
+                        one, two = jnp.where(low, here, 0.0), jnp.where(low, there, 0.0)
+                    else:
+                        one, two = jnp.where(low, 0.0, there), jnp.where(low, 0.0, here)
+                    piece = jnp.concatenate([one, two], axis=0)
+                    blocks.append(jnp.concatenate([piece, blank] if j < 2 else [blank, piece], axis=1))
+                right = jnp.concatenate(blocks, axis=0).astype(BF)
+                grad = lax.dot_general(
+                    left, right, (((0,), (0,)), ((), ())), preferred_element_type=F32
+                )
+                for j in range(4):
+                    at = group * 2048 + (j * 2 + h) * 256
+                    made[q, at : at + 256, :] = grad[:, j * 64 : j * 64 + 64]
+        copy_out(q).start()
         return carry
 
-    lax.fori_loop(0, NQ * 4, step, 0)
-    for i in range(NQ * 4):
-        copy_out(i).wait()
+    lax.fori_loop(0, NQ, step, 0)
+    for q in range(NQ):
+        copy_out(q).wait()
 
 
 def weight_gradient(specs, grads, t):
     return pl.pallas_call(
         weight_body,
-        in_specs=[VM] * 9,
+        in_specs=[VM] * 5,
         out_specs=HBM,
-        out_shape=jax.ShapeDtypeStruct((NQ * 8192, 64), F32),
+        out_shape=jax.ShapeDtypeStruct((NQ, 8192, 64), F32),
         scratch_shapes=[pltpu.VMEM((4, NQ, 32, 512), F32), pltpu.VMEM((4, NQ, 32, 512), F32)]
-        + [pltpu.VMEM((NQ * 8192, 64), F32), pltpu.SemaphoreType.DMA((NQ * 4,))],
+        + [pltpu.VMEM((NQ, 8192, 64), F32), pltpu.SemaphoreType.DMA((NQ,))],
         name="weight_gradient",
+        compiler_params=pltpu.CompilerParams(vmem_limit_bytes=52 << 20),
     )(*specs, *grads, t["fold"])
 
 
@@ -518,10 +543,10 @@
 
 
 def everyone(values):
-    pieces = [values]
-    for k in range(1, 4):
-        pieces.append(lax.ppermute(values, "dp", [(i, i ^ k) for i in range(4)]))
-    return pieces
+    far = lax.ppermute(values, "dp", [(i, i ^ 2) for i in range(4)])
+    both = jnp.stack([values, far])
+    near = lax.ppermute(both, "dp", [(i, i ^ 1) for i in range(4)])
+    return both, near
 
 
 def per_device(field, cotangent, spectral_weight, point_weight, bias_term):
@@ -534,6 +559,7 @@
     back, spec = mix_forward(sent, weights, t)
     got = exchange(back)
     specs = everyone(spec)
+    got, specs = lax.optimization_barrier((got, specs))
     act, grad_pre, out = activate(got, lin, cotangent.reshape(4096, ZT), t)
     sent = exchange(out)
     lin = linear(grad_pre, point_weight, None, True)

time: 130 us -> 109 us (0.84)
  blocking collectives: 16.1 us -> 0 us
  Pallas kernels: 64.5 us -> 51.1 us
  waiting for transfers between devices: 20.5 us -> 28.6 us
  starting transfers between devices: 22.9 us -> 25.6 us
  local copies, waits for them, and re-layouts: 3.5 us -> 2.05 us
    all_to_all x1 -> x0, blocking collectives: 16.1 us -> none  [exchange(): lax.all_to_all(values, 'slab', split_axis=0, concat_axis=0, tiled=True)]
    all_to_all x3 -> x4, waiting for transfers between devices: 11.2 us -> 25.7 us  [exchange(): lax.all_to_all(values, 'slab', split_axis=0, concat_axis=0, tiled=True)]
    pallas_call x3, Pallas kernels: 26.8 us -> 17.4 us  [the longest x1 6.19 us: mix_backward(): pl.pallas_call(mix_backward_body, in_specs=[VM, HBM, VM, VM, VM], out_spe...]
    ppermute x6 -> x4, waiting for transfers between devices: 9.35 us -> 2.86 us  [the longest x2 2.86 us: everyone(): near = lax.ppermute(both, 'dp', [(i, i ^ 1) for i in range(4)])]
    all_to_all x3 -> x4, starting transfers between devices: 19.3 us -> 23.9 us  [exchange(): lax.all_to_all(values, 'slab', split_axis=0, concat_axis=0, tiled=True)]
    ppermute x6 -> x4, starting transfers between devices: 3.57 us -> 1.67 us  [the longest x2 1.5 us: everyone(): far = lax.ppermute(values, 'dp', [(i, i ^ 2) for i in range(4)])]
    pallas_call x1, Pallas kernels: 13.4 us -> 11.8 us  [activate(): pl.pallas_call(activate_body, in_specs=[VM, HBM, HBM, VM, VM], out_specs=...]
    unnamed x20 -> x22, local copies, waits for them, and re-layouts: 3.5 us -> 2.05 us
  transfers between devices with their start and end apart: 9 -> 8, of which waited for: 6 -> 6; matrix products, arithmetic and copies ran while one was open for 0% -> 0% of each run, Pallas kernels for 20% -> 16%
where the time goes in v2:
time: 109 us; the launch traced here: 108 us
  Pallas kernels  51.1 us (47%)
  waiting for transfers between devices  28.6 us (26%)
  starting transfers between devices  25.6 us (23%)
  local copies, waits for them, and re-layouts  2.05 us (2%)
    all_to_all x4, waiting for transfers between devices, exchange(): lax.all_to_all(values, 'slab', split_axis=0, concat_axis=0, tiled=True)  25.7 us
    all_to_all x4, starting transfers between devices, exchange(): lax.all_to_all(values, 'slab', split_axis=0, concat_axis=0, tiled=True)  23.9 us
    pallas_call x1, Pallas kernels, activate(): pl.pallas_call(activate_body, in_specs=[VM, HBM, HBM, VM, VM], out_specs=...  11.8 us
    pallas_call x2, Pallas kernels, linear(): pl.pallas_call(body, in_specs=[HBM, VM] + [pl.BlockSpec(memory_space=pltp...  11.6 us
    pallas_call x1, Pallas kernels, mix_backward(): pl.pallas_call(mix_backward_body, in_specs=[VM, HBM, VM, VM, VM], out_spe...  6.19 us
    pallas_call x1, Pallas kernels, weight_gradient(): pl.pallas_call(weight_body, in_specs=[VM] * 5, out_specs=HBM, out_shape=j...  6 us
    pallas_call x1, Pallas kernels, finish(): pl.pallas_call(finish_body, in_specs=[VM, HBM, VM, VM], out_specs=HBM, ou...  5.25 us
    pallas_call x1, Pallas kernels, mix_forward(): pl.pallas_call(mix_forward_body, in_specs=[VM, HBM, VM, VM, VM], out_spec...  5.17 us
  transfers between devices with their start and end apart: 8, of which 6 were waited for; matrix products, arithmetic and copies ran while one was open for 0% of the time, Pallas kernels for 16%

profile of v2, /device:TPU:0, one launch (start us, length us, event | category | flops | bytes accessed | tf_op | source)
XLA Modules:
  0.0 108.4 jit_solution(3784372879343976766)
XLA Ops:
  0.7 1.0 copy-done
  1.7 0.9 copy-done.2
  2.6 5.1 %analyse.1 = bf16[32,48,128]{2,1,0:T(8,128)(2,1)} custom-call(bf16[4096,512]{1,0:T(8,128)(2,1)} %bitcast.14, bf16[256,512]{1,0:T(8,128)(2,1)S(1)} %copy-done.2, bf16[1024,256]{1,0:T(8,128)(2,1)S(1)} %copy-done), custom_call_target="tpu_custom_call" | custom-call | tf_op jit(solution)/shard_map/analyse/pallas_call | solution.py:142
  7.7 10.9 %all-to-all-start = ((bf16[32,48,128]{2,1,0:T(8,128)(2,1)}), bf16[32,48,128]{2,1,0:T(8,128)(2,1)S(1)}, u32[]{:S(2)}, u32[]{:S(2)}) async-start(bf16[32,48,128]{2,1,0:T(8,128)(2,1)} %analyse.1), calls=%async_computation | async-start | bytes 786432 | tf_op jit(solution)/shard_map/all_to_all | solution.py:542
  18.7 6.1 %linear.2.lin = bf16[4096,512]{1,0:T(8,128)(2,1)} custom-call(bf16[4096,512]{1,0:T(8,128)(2,1)} %bitcast.15, bf16[32,32]{1,0:T(8,128)(2,1)S(1)} %copy-done.9, f32[32]{0:T(128)S(1)} %copy-done.10), custom_call_target="tpu_custom_call" | custom-call | tf_op jit(solution)/shard_map/linear/pallas_call | solution.py:453
  24.8 6.0 %all-to-all-done.got = bf16[32,48,128]{2,1,0:T(8,128)(2,1)S(1)} async-done(((bf16[32,48,128]{2,1,0:T(8,128)(2,1)}), bf16[32,48,128]{2,1,0:T(8,128)(2,1)S(1)}, u32[]{:S(2)}, u32[]{:S(2)}) %all-to-all-start) | async-done | bytes 393248 | tf_op jit(solution)/shard_map/all_to_all | solution.py:542
  30.8 5.2 %mix_forward.1 = (bf16[32,48,128]{2,1,0:T(8,128)(2,1)}, bf16[3,32,512]{2,1,0:T(8,128)(2,1)S(1)}) custom-call(bf16[32,48,128]{2,1,0:T(8,128)(2,1)S(1)} %all-to-all-done.got, bf16[3,8192,64]{2,1,0:T(8,128)(2,1)} %bitcast.12, bf16[128,512]{1,0:T(8,128)(2,1)S(1)} %copy-done.5, bf16[2,64,512]{2,1,0:T(8,128)(2,1)S(1)} %copy-done.6, bf16[128,512]{1,0:T(8,128)(2,1)S(1)} %copy-done.7), custom_call_target="tpu_custom_call" | custom-call | tf_op jit(solution)/shard_map/mix_forward/pallas_call | solution.py:236
  36.0 0.8 collective-permute-start
  36.8 4.5 %all-to-all-start.1 = ((bf16[32,48,128]{2,1,0:T(8,128)(2,1)}), bf16[32,48,128]{2,1,0:T(8,128)(2,1)S(1)}, u32[]{:S(2)}, u32[]{:S(2)}) async-start(bf16[32,48,128]{2,1,0:T(8,128)(2,1)} %get-tuple-element.20), calls=%async_computation.1 | async-start | bytes 786432 | tf_op jit(solution)/shard_map/all_to_all | solution.py:542
  41.3 0.1 collective-permute-start.1
  41.4 1.4 %collective-permute-done.1.refs_1_ = bf16[2,3,32,512]{3,2,1,0:T(8,128)(2,1)S(1)} collective-permute-done((bf16[2,3,32,512]{3,2,1,0:T(8,128)(2,1)S(1)}, bf16[2,3,32,512]{3,2,1,0:T(8,128)(2,1)S(1)}, u32[]{:S(2)}, u32[]{:S(2)}) %collective-permute-start.1) | collective-permute-done | bytes 196640 | tf_op jit(solution)/shard_map/ppermute | solution.py:548
  42.8 10.0 %all-to-all-done.1.got = bf16[32,48,128]{2,1,0:T(8,128)(2,1)S(1)} async-done(((bf16[32,48,128]{2,1,0:T(8,128)(2,1)}), bf16[32,48,128]{2,1,0:T(8,128)(2,1)S(1)}, u32[]{:S(2)}, u32[]{:S(2)}) %all-to-all-start.1) | async-done | bytes 393248 | tf_op jit(solution)/shard_map/all_to_all | solution.py:542
  52.9 11.8 %activate.1 = (bf16[4096,512]{1,0:T(8,128)(2,1)}, bf16[4096,512]{1,0:T(8,128)(2,1)}, bf16[32,48,128]{2,1,0:T(8,128)(2,1)}) custom-call(bf16[32,48,128]{2,1,0:T(8,128)(2,1)S(1)} %all-to-all-done.1.got, bf16[4096,512]{1,0:T(8,128)(2,1)} %linear.2.lin, bf16[4096,512]{1,0:T(8,128)(2,1)} %bitcast.17, bf16[256,512]{1,0:T(8,128)(2,1)S(1)} %copy-done.3, ...), custom_call_target="tpu_custom_call" | custom-call | tf_op jit(solution)/shard_map/activate/pallas_call | solution.py:367
  64.6 4.1 %all-to-all-start.2 = ((bf16[32,48,128]{2,1,0:T(8,128)(2,1)}), bf16[32,48,128]{2,1,0:T(8,128)(2,1)S(1)}, u32[]{:S(2)}, u32[]{:S(2)}) async-start(bf16[32,48,128]{2,1,0:T(8,128)(2,1)} %get-tuple-element.25), calls=%async_computation.2 | async-start | bytes 786432 | tf_op jit(solution)/shard_map/all_to_all | solution.py:542
  68.8 5.5 %linear.3.lin = bf16[4096,512]{1,0:T(8,128)(2,1)} custom-call(bf16[4096,512]{1,0:T(8,128)(2,1)} %get-tuple-element.26.v, bf16[32,32]{1,0:T(8,128)(2,1)S(1)} %copy-done.9), custom_call_target="tpu_custom_call" | custom-call | tf_op jit(solution)/shard_map/linear/pallas_call | solution.py:453
  74.3 5.8 %all-to-all-done.2.got = bf16[32,48,128]{2,1,0:T(8,128)(2,1)S(1)} async-done(((bf16[32,48,128]{2,1,0:T(8,128)(2,1)}), bf16[32,48,128]{2,1,0:T(8,128)(2,1)S(1)}, u32[]{:S(2)}, u32[]{:S(2)}) %all-to-all-start.2) | async-done | bytes 393248 | tf_op jit(solution)/shard_map/all_to_all | solution.py:542
  80.0 6.2 %mix_backward.1 = (bf16[32,48,128]{2,1,0:T(8,128)(2,1)}, bf16[3,32,512]{2,1,0:T(8,128)(2,1)S(1)}) custom-call(bf16[32,48,128]{2,1,0:T(8,128)(2,1)S(1)} %all-to-all-done.2.got, bf16[3,8192,64]{2,1,0:T(8,128)(2,1)} %bitcast.13, bf16[128,512]{1,0:T(8,128)(2,1)S(1)} %copy-done.5, bf16[512,128]{1,0:T(8,128)(2,1)S(1)} %copy-done.4, bf16[128,256]{1,0:T(8,128)(2,1)S(1)} %copy-done.8), custom_call_target="tpu_custom_call" | custom-call | tf_op jit(solution)/shard_map/mix_backward/pallas_call | solution.py:290
  86.2 0.7 collective-permute-start.2
  87.0 4.5 %all-to-all-start.3 = ((bf16[32,48,128]{2,1,0:T(8,128)(2,1)}), bf16[32,48,128]{2,1,0:T(8,128)(2,1)S(1)}, u32[]{:S(2)}, u32[]{:S(2)}) async-start(bf16[32,48,128]{2,1,0:T(8,128)(2,1)} %get-tuple-element.28), calls=%async_computation.3 | async-start | bytes 786432 | tf_op jit(solution)/shard_map/all_to_all | solution.py:542
  91.5 0.1 collective-permute-start.3
  91.6 1.4 %collective-permute-done.3.refs_3_ = bf16[2,3,32,512]{3,2,1,0:T(8,128)(2,1)S(1)} collective-permute-done((bf16[2,3,32,512]{3,2,1,0:T(8,128)(2,1)S(1)}, bf16[2,3,32,512]{3,2,1,0:T(8,128)(2,1)S(1)}, u32[]{:S(2)}, u32[]{:S(2)}) %collective-permute-start.3) | collective-permute-done | bytes 196640 | tf_op jit(solution)/shard_map/ppermute | solution.py:548
  93.0 6.0 %weight_gradient.1 = f32[3,8192,64]{2,1,0:T(8,128)} custom-call(bf16[2,3,32,512]{3,2,1,0:T(8,128)(2,1)S(1)} %pad_maximum_fusion.refs_0_, bf16[2,3,32,512]{3,2,1,0:T(8,128)(2,1)S(1)} %collective-permute-done.1.refs_1_, bf16[2,3,32,512]{3,2,1,0:T(8,128)(2,1)S(1)} %pad_maximum_fusion.1.refs_2_, bf16[2,3,32,512]{3,2,1,0:T(8,128)(2,1)S(1)} %collective-permute-done.3.refs_3_, ...), custom_call_target="tpu_custom_call" | custom-call | tf_op jit(solution)/shard_map/weight_gradient/pallas_call | solution.py:529
  99.1 3.9 %all-to-all-done.3.got = bf16[32,48,128]{2,1,0:T(8,128)(2,1)S(1)} async-done(((bf16[32,48,128]{2,1,0:T(8,128)(2,1)}), bf16[32,48,128]{2,1,0:T(8,128)(2,1)S(1)}, u32[]{:S(2)}, u32[]{:S(2)}) %all-to-all-start.3) | async-done | bytes 393248 | tf_op jit(solution)/shard_map/all_to_all | solution.py:542
  103.0 5.3 %finish.1 = bf16[4096,512]{1,0:T(8,128)(2,1)} custom-call(bf16[32,48,128]{2,1,0:T(8,128)(2,1)S(1)} %all-to-all-done.3.got, bf16[4096,512]{1,0:T(8,128)(2,1)} %linear.3.lin, bf16[256,512]{1,0:T(8,128)(2,1)S(1)} %copy-done.3, bf16[1024,256]{1,0:T(8,128)(2,1)S(1)} %copy-done.1), custom_call_target="tpu_custom_call" | custom-call | tf_op jit(solution)/shard_map/finish/pallas_call | solution.py:401
  (24 shorter events, 0.1 us)
Async XLA Ops:
  0.6 18.0 %copy-start.10 = (f32[32]{0:T(128)S(1)}, f32[32]{0:T(128)}, u32[]{:S(2)}) copy-start(f32[32]{0:T(128)} %bias.1) | copy-start | bytes 388
  0.6 1.0 copy-start
  1.7 0.9 copy-start.2
  2.6 16.0 %copy-start.9 = (bf16[32,32]{1,0:T(8,128)(2,1)S(1)}, bf16[32,32]{1,0:T(8,128)(2,1)}, u32[]{:S(2)}) copy-start(bf16[32,32]{1,0:T(8,128)(2,1)} %m.1) | copy-start | bytes 6148
  7.7 23.1 %all-to-all-start = ((bf16[32,48,128]{2,1,0:T(8,128)(2,1)}), bf16[32,48,128]{2,1,0:T(8,128)(2,1)S(1)}, u32[]{:S(2)}, u32[]{:S(2)}) async-start(bf16[32,48,128]{2,1,0:T(8,128)(2,1)} %analyse.1), calls=%async_computation | async-start | bytes 786432 | tf_op jit(solution)/shard_map/all_to_all | solution.py:542
  18.7 12.2 %copy-start.5 = (bf16[128,512]{1,0:T(8,128)(2,1)S(1)}, bf16[128,512]{1,0:T(8,128)(2,1)}, u32[]{:S(2)}) copy-start(bf16[128,512]{1,0:T(8,128)(2,1)} %constant.16.clone.ana_out) | copy-start | bytes 393220
  18.7 12.2 %copy-start.6 = (bf16[2,64,512]{2,1,0:T(8,128)(2,1)S(1)}, bf16[2,64,512]{2,1,0:T(8,128)(2,1)}, u32[]{:S(2)}) copy-start(bf16[2,64,512]{2,1,0:T(8,128)(2,1)} %constant.19.clone.spread) | copy-start | bytes 393220
  18.7 12.2 %copy-start.7 = (bf16[128,512]{1,0:T(8,128)(2,1)S(1)}, bf16[128,512]{1,0:T(8,128)(2,1)}, u32[]{:S(2)}) copy-start(bf16[128,512]{1,0:T(8,128)(2,1)} %constant.17.clone.fwd_out) | copy-start | bytes 393220
  24.8 28.1 %copy-start.1 = (bf16[1024,256]{1,0:T(8,128)(2,1)S(1)}, bf16[1024,256]{1,0:T(8,128)(2,1)}, u32[]{:S(2)}) copy-start(bf16[1024,256]{1,0:T(8,128)(2,1)} %constant.15.clone.middle) | copy-start | bytes 1572868
  24.8 28.1 %copy-start.3 = (bf16[256,512]{1,0:T(8,128)(2,1)S(1)}, bf16[256,512]{1,0:T(8,128)(2,1)}, u32[]{:S(2)}) copy-start(bf16[256,512]{1,0:T(8,128)(2,1)} %constant.14.clone.depth) | copy-start | bytes 786436
  36.0 5.2 %collective-permute-start = (bf16[3,32,512]{2,1,0:T(8,128)(2,1)S(1)}, bf16[3,32,512]{2,1,0:T(8,128)(2,1)S(1)}, u32[]{:S(2)}, u32[]{:S(2)}) collective-permute-start(bf16[3,32,512]{2,1,0:T(8,128)(2,1)S(1)} %get-tuple-element.21), channel_id=1, source_target_pairs={{0,2},{1,3},{2,0},{3,1},{4,6},{5,7},{6,4},{7,5},{8,10},{9,11},{10,... | collective-permute-start | bytes 294920 | tf_op jit(solution)/shard_map/ppermute | solution.py:546
  36.8 16.1 %all-to-all-start.1 = ((bf16[32,48,128]{2,1,0:T(8,128)(2,1)}), bf16[32,48,128]{2,1,0:T(8,128)(2,1)S(1)}, u32[]{:S(2)}, u32[]{:S(2)}) async-start(bf16[32,48,128]{2,1,0:T(8,128)(2,1)} %get-tuple-element.20), calls=%async_computation.1 | async-start | bytes 786432 | tf_op jit(solution)/shard_map/all_to_all | solution.py:542
  41.3 1.5 %collective-permute-start.1 = (bf16[2,3,32,512]{3,2,1,0:T(8,128)(2,1)S(1)}, bf16[2,3,32,512]{3,2,1,0:T(8,128)(2,1)S(1)}, u32[]{:S(2)}, u32[]{:S(2)}) collective-permute-start(bf16[2,3,32,512]{3,2,1,0:T(8,128)(2,1)S(1)} %pad_maximum_fusion.refs_0_), channel_id=1, source_target_pairs={{0,1},{1,0},{2,3},{3,2},{4,5},{5,4},{6,7},{7,6},{8,9},{9,8},{10,11... | collective-permute-start | bytes 589832 | tf_op jit(solution)/shard_map/ppermute | solution.py:548
  64.6 15.4 %all-to-all-start.2 = ((bf16[32,48,128]{2,1,0:T(8,128)(2,1)}), bf16[32,48,128]{2,1,0:T(8,128)(2,1)S(1)}, u32[]{:S(2)}, u32[]{:S(2)}) async-start(bf16[32,48,128]{2,1,0:T(8,128)(2,1)} %get-tuple-element.25), calls=%async_computation.2 | async-start | bytes 786432 | tf_op jit(solution)/shard_map/all_to_all | solution.py:542
  68.7 11.3 %copy-start.4 = (bf16[512,128]{1,0:T(8,128)(2,1)S(1)}, bf16[512,128]{1,0:T(8,128)(2,1)}, u32[]{:S(2)}) copy-start(bf16[512,128]{1,0:T(8,128)(2,1)} %constant.20.clone.fold.refs_4_) | copy-start | bytes 393220
  68.7 11.3 %copy-start.8 = (bf16[128,256]{1,0:T(8,128)(2,1)S(1)}, bf16[128,256]{1,0:T(8,128)(2,1)}, u32[]{:S(2)}) copy-start(bf16[128,256]{1,0:T(8,128)(2,1)} %constant.18.clone.bwd_out) | copy-start | bytes 196612
  86.2 5.2 %collective-permute-start.2 = (bf16[3,32,512]{2,1,0:T(8,128)(2,1)S(1)}, bf16[3,32,512]{2,1,0:T(8,128)(2,1)S(1)}, u32[]{:S(2)}, u32[]{:S(2)}) collective-permute-start(bf16[3,32,512]{2,1,0:T(8,128)(2,1)S(1)} %get-tuple-element.31), channel_id=1, source_target_pairs={{0,2},{1,3},{2,0},{3,1},{4,6},{5,7},{6,4},{7,5},{8,10},{9,11},{10,... | collective-permute-start | bytes 294920 | tf_op jit(solution)/shard_map/ppermute | solution.py:546
  87.0 16.0 %all-to-all-start.3 = ((bf16[32,48,128]{2,1,0:T(8,128)(2,1)}), bf16[32,48,128]{2,1,0:T(8,128)(2,1)S(1)}, u32[]{:S(2)}, u32[]{:S(2)}) async-start(bf16[32,48,128]{2,1,0:T(8,128)(2,1)} %get-tuple-element.28), calls=%async_computation.3 | async-start | bytes 786432 | tf_op jit(solution)/shard_map/all_to_all | solution.py:542
  91.5 1.5 %collective-permute-start.3 = (bf16[2,3,32,512]{3,2,1,0:T(8,128)(2,1)S(1)}, bf16[2,3,32,512]{3,2,1,0:T(8,128)(2,1)S(1)}, u32[]{:S(2)}, u32[]{:S(2)}) collective-permute-start(bf16[2,3,32,512]{3,2,1,0:T(8,128)(2,1)S(1)} %pad_maximum_fusion.1.refs_2_), channel_id=1, source_target_pairs={{0,1},{1,0},{2,3},{3,2},{4,5},{5,4},{6,7},{7,6},{8,9},{9,8},{10,11... | collective-permute-start | bytes 589832 | tf_op jit(solution)/shard_map/ppermute | solution.py:548

commit v3 on v2

--- a/solution.py
+++ b/solution.py
@@ -8,6 +8,7 @@
 from jax.experimental import pallas as pl
 from jax.experimental.pallas import tpu as pltpu
 from jax.sharding import PartitionSpec as P
+
 
 X = 64
 Y = 64
@@ -75,7 +76,7 @@
         fold[1, :, o, 64 + o] = 1.0
     fold = fold.reshape(512, 128)
     t = dict(
-        depth=depth, middle=middle, ana_out=ana_out, fwd_out=fwd_out * SCALE, bwd_out=bwd_out,
+        depth=depth, middle=middle, ana_out=ana_out, fwd_out=fwd_out * (SCALE / 2.0), bwd_out=bwd_out,
         spread=spread, fold=fold,
     )
     return {k: jnp.asarray(v, BF) for k, v in t.items()}
@@ -118,18 +119,27 @@
     return pltpu.make_async_copy(src.at[at], dst.at[at], sem.at[k])
 
 
-def analyse_body(v, depth, middle, out, have, first, work, sem):
+def analyse_body(v, depth_h, middle_h, out, have, first, work, depth, middle, sem, more):
+    tables_in = [
+        pltpu.make_async_copy(depth_h, depth, more.at[0]),
+        pltpu.make_async_copy(middle_h, middle, more.at[1]),
+    ]
+    tables_in[0].start()
     for k in range(8):
         chunk_copy(v, have, sem, k).start()
+    tables_in[1].start()
+    tables_in[0].wait()
     table = owner_table(depth)
-    for k in range(8):
-        chunk_copy(v, have, sem, k).wait()
-        analyse_rows(have[k * 512 : k * 512 + 512, :], k, table, first)
+    for half in range(2):
+        for k in range(half * 4, half * 4 + 4):
+            chunk_copy(v, have, sem, k).wait()
+        part = dot_t(table, have[half * 2048 : half * 2048 + 2048, :]).astype(BF)
+        for k in range(4):
+            at = half * 384 + k * 96
+            first[at : at + 96, 0:512] = part[:96, k * 512 : k * 512 + 512]
+            first[at : at + 96, 512:1024] = part[96:, k * 512 : k * 512 + 512]
+    tables_in[1].wait()
     by_owner(first, middle, out, work)
-
-
-def whole(shape):
-    return pl.BlockSpec(shape, lambda i: (0,) * len(shape))
 
 
 HBM = pl.BlockSpec(memory_space=pltpu.HBM)
@@ -141,15 +151,16 @@
 def analyse(values, t):
     return pl.pallas_call(
         analyse_body,
-        in_specs=[HBM, VM, VM],
+        in_specs=[HBM, HBM, HBM],
         out_specs=VM,
         out_shape=SENT,
         scratch_shapes=[
             pltpu.VMEM((4096, ZT), BF), pltpu.VMEM((768, 1024), BF),
-            pltpu.VMEM((NQ, 512, 128), F32), pltpu.SemaphoreType.DMA((8,)),
+            pltpu.VMEM((NQ, 512, 128), F32), pltpu.VMEM((256, ZT), BF), pltpu.VMEM((1024, 256), BF),
+            pltpu.SemaphoreType.DMA((8,)), pltpu.SemaphoreType.DMA((2,)),
         ],
         name="analyse",
-        compiler_params=pltpu.CompilerParams(vmem_limit_bytes=52 << 20),
+        compiler_params=pltpu.CompilerParams(vmem_limit_bytes=60 << 20),
     )(values, t["depth"], t["middle"])
 
 
@@ -254,7 +265,7 @@
     for q in range(NQ):
         weight_copy(w, have, sem, q).start()
     channel_order(perm)
-    rows = spectrum_rows(got, ana_out, perm, SCALE)
+    rows = spectrum_rows(got, ana_out, perm, SCALE / 2.0)
     srow[...] = rows
     for q in range(NQ):
         spec[q] = rows[q * 32 : q * 32 + 32].astype(BF)
@@ -321,7 +332,6 @@
 
 
 ROOT = math.sqrt(2.0 / math.pi)
-CHUNK = 512
 
 
 def activate_body(
@@ -331,31 +341,42 @@
     for k in range(8):
         chunk_copy(lin, lin_v, sems.at[0], k).start()
         chunk_copy(cot, cot_v, sems.at[1], k).start()
+    grad_v[0:512, :] = jnp.zeros((512, ZT), BF)
     unpack(got, have, turned, middle, tall)
-
-    def step(k, carry):
-        chunk_copy(lin, lin_v, sems.at[0], k).wait()
-        chunk_copy(cot, cot_v, sems.at[1], k).wait()
-        for j in range(512 // CHUNK):
-            at = pl.ds(pl.multiple_of(k * 512 + j * CHUNK, CHUNK), CHUNK)
-            v = dot(tall[at, :], depth[...]) + lin_v[at, :].astype(F32)
-            square = v * v
-            half = 0.5 + 0.5 * jnp.tanh(v * (ROOT + (ROOT * 0.044715) * square))
-            value = v * half
-            slope = half + (value - value * half) * (2.0 * ROOT + (6.0 * ROOT * 0.044715) * square)
+    table = owner_table(depth)
+
+    def grad_copy(k):
+        at = pl.ds(k * 512, 512)
+        return pltpu.make_async_copy(grad_v.at[pl.ds(k * 512 + 512, 512)], grad.at[at], sems.at[3, k])
+
+    def step(i, carry):
+        base = pl.multiple_of(i * 1024, 1024)
+        for u in range(2):
+            chunk_copy(lin, lin_v, sems.at[0], i * 2 + u).wait()
+            chunk_copy(cot, cot_v, sems.at[1], i * 2 + u).wait()
+        for u in range(2):
+            rows = grad_v[pl.ds(base + u * 512, 512), :]
+            slot = jnp.maximum(i * 2 + u - 1, 0)
+            analyse_rows(rows, slot, table, first)
+            at = pl.ds(base + u * 512, 512)
+            w = dot(tall[at, :], depth[...]) + lin_v[at, :].astype(F32)
+            square = w * w
+            t = jnp.tanh(w * (2.0 * ROOT + (8.0 * ROOT * 0.044715) * square))
+            one = 1.0 + t
+            value = w * one
+            slope = one + value * (1.0 - t) * (2.0 * ROOT + (24.0 * ROOT * 0.044715) * square)
             act_v[at, :] = value.astype(BF)
-            grad_v[at, :] = (cot_v[at, :].astype(F32) * slope).astype(BF)
-        chunk_copy(act_v, act, sems.at[2], k).start()
-        chunk_copy(grad_v, grad, sems.at[3], k).start()
-        rows = grad_v[pl.ds(pl.multiple_of(k * 512, 512), 512), :]
-        analyse_rows(rows, k, owner_table(depth), first)
+            grad_v[pl.ds(base + u * 512 + 512, 512), :] = cot_v[at, :] * slope.astype(BF)
+            chunk_copy(act_v, act, sems.at[2], i * 2 + u).start()
+            grad_copy(i * 2 + u).start()
         return carry
 
-    lax.fori_loop(0, 8, step, 0)
+    lax.fori_loop(0, 4, step, 0)
+    analyse_rows(grad_v[4096:4608, :], 7, table, first)
     by_owner(first, middle, out, work)
     for k in range(8):
         chunk_copy(act_v, act, sems.at[2], k).wait()
-        chunk_copy(grad_v, grad, sems.at[3], k).wait()
+        grad_copy(k).wait()
 
 
 SYNTH_SCRATCH = [
@@ -369,7 +390,8 @@
         in_specs=[VM, HBM, HBM, VM, VM],
         out_specs=[HBM, HBM, VM],
         out_shape=[GRID_ROWS, GRID_ROWS, SENT],
-        scratch_shapes=[pltpu.VMEM((4096, ZT), BF)] * 4
+        scratch_shapes=[pltpu.VMEM((4096, ZT), BF)] * 3
+        + [pltpu.VMEM((4608, ZT), BF)]
         + SYNTH_SCRATCH
         + [
             pltpu.VMEM((768, 1024), BF), pltpu.VMEM((NQ, 512, 128), F32),
@@ -423,7 +445,7 @@
     tall = dot(pick, wide.astype(BF))
     row = lax.broadcasted_iota(jnp.int32, (512, 512), 0) % 16
     col = lax.broadcasted_iota(jnp.int32, (512, 512), 1) % 16
-    kron[...] = jnp.where(row == col, tall, 0.0).astype(BF)
+    kron[...] = jnp.where(row == col, tall * 0.5, 0.0).astype(BF)
     for x in range(2):
         for k in range(4):
             chunk_copy(v, have, sems.at[0], x * 4 + k).wait()
@@ -435,7 +457,7 @@
             for c in range(C):
                 one = result[c * 16 : c * 16 + 16]
                 if bias is not None:
-                    one = one + bias[c]
+                    one = one + 0.5 * bias[c]
                 done[c, g * 16 : g * 16 + 16, :] = one.astype(BF)
         for k in range(4):
             chunk_copy(made, out, sems.at[1], x * 4 + k).start()
@@ -549,7 +571,7 @@
     return both, near
 
 
-def per_device(field, cotangent, spectral_weight, point_weight, bias_term):
+def layer(field, cotangent, spectral_weight, point_weight, bias_term):
     t = tables()
     rows = field.reshape(4096, ZT)
     weights = spectral_weight.reshape(NQ, 8192, 64)
@@ -583,7 +605,7 @@
         P(),
     )
     return jax.shard_map(
-        per_device,
+        layer,
         mesh=mesh,
         in_specs=placed,
         out_specs=(

time: 109 us -> 106 us (0.972)
  local copies, waits for them, and re-layouts: 2.05 us -> 0.06 us
    unnamed x22 -> x18, local copies, waits for them, and re-layouts: 2.05 us -> 0.06 us
  transfers between devices with their start and end apart: 8 -> 8, of which waited for: 6 -> 6; matrix products, arithmetic and copies ran while one was open for 0% -> 0% of each run, Pallas kernels for 16% -> 17%
where the time goes in v3:
time: 106 us; the launch traced here: 105 us
  Pallas kernels  50.1 us (47%)
  waiting for transfers between devices  28.6 us (27%)
  starting transfers between devices  25.6 us (24%)
    all_to_all x4, waiting for transfers between devices, exchange(): lax.all_to_all(values, 'slab', split_axis=0, concat_axis=0, tiled=True)  25.7 us
    all_to_all x4, starting transfers between devices, exchange(): lax.all_to_all(values, 'slab', split_axis=0, concat_axis=0, tiled=True)  23.9 us
    pallas_call x2, Pallas kernels, linear(): pl.pallas_call(body, in_specs=[HBM, VM] + [pl.BlockSpec(memory_space=pltp...  11.6 us
    pallas_call x1, Pallas kernels, activate(): pl.pallas_call(activate_body, in_specs=[VM, HBM, HBM, VM, VM], out_specs=...  10.7 us
    pallas_call x1, Pallas kernels, mix_backward(): pl.pallas_call(mix_backward_body, in_specs=[VM, HBM, VM, VM, VM], out_spe...  6.2 us
    pallas_call x1, Pallas kernels, weight_gradient(): pl.pallas_call(weight_body, in_specs=[VM] * 5, out_specs=HBM, out_shape=j...  6.01 us
    pallas_call x1, Pallas kernels, finish(): pl.pallas_call(finish_body, in_specs=[VM, HBM, VM, VM], out_specs=HBM, ou...  5.25 us
    pallas_call x1, Pallas kernels, mix_forward(): pl.pallas_call(mix_forward_body, in_specs=[VM, HBM, VM, VM, VM], out_spec...  5.17 us
  transfers between devices with their start and end apart: 8, of which 6 were waited for; matrix products, arithmetic and copies ran while one was open for 0% of the time, Pallas kernels for 17%

profile of v3, /device:TPU:0, one launch (start us, length us, event | category | flops | bytes accessed | tf_op | source)
XLA Modules:
  0.0 105.4 jit_solution(10951688451814748043)
XLA Ops:
  0.7 5.2 %analyse.1 = bf16[32,48,128]{2,1,0:T(8,128)(2,1)} custom-call(bf16[4096,512]{1,0:T(8,128)(2,1)} %bitcast.14, bf16[256,512]{1,0:T(8,128)(2,1)} %constant.14.clone.depth_h.depth, bf16[1024,256]{1,0:T(8,128)(2,1)} %constant.15.clone.middle_h.middle), custom_call_target="tpu_custom_call" | custom-call | tf_op jit(solution)/shard_map/analyse/pallas_call | solution.py:152
  5.8 10.9 %all-to-all-start = ((bf16[32,48,128]{2,1,0:T(8,128)(2,1)}), bf16[32,48,128]{2,1,0:T(8,128)(2,1)S(1)}, u32[]{:S(2)}, u32[]{:S(2)}) async-start(bf16[32,48,128]{2,1,0:T(8,128)(2,1)} %analyse.1), calls=%async_computation | async-start | bytes 786432 | tf_op jit(solution)/shard_map/all_to_all | solution.py:564
  16.8 0.0 copy-start.3
  16.8 0.0 copy-start.5
  16.8 6.1 %linear.2.lin = bf16[4096,512]{1,0:T(8,128)(2,1)} custom-call(bf16[4096,512]{1,0:T(8,128)(2,1)} %bitcast.15, bf16[32,32]{1,0:T(8,128)(2,1)S(1)} %copy-done.7, f32[32]{0:T(128)S(1)} %copy-done.8), custom_call_target="tpu_custom_call" | custom-call | tf_op jit(solution)/shard_map/linear/pallas_call | solution.py:475
  22.9 6.0 %all-to-all-done.got = bf16[32,48,128]{2,1,0:T(8,128)(2,1)S(1)} async-done(((bf16[32,48,128]{2,1,0:T(8,128)(2,1)}), bf16[32,48,128]{2,1,0:T(8,128)(2,1)S(1)}, u32[]{:S(2)}, u32[]{:S(2)}) %all-to-all-start) | async-done | bytes 393248 | tf_op jit(solution)/shard_map/all_to_all | solution.py:564
  28.9 5.2 %mix_forward.1 = (bf16[32,48,128]{2,1,0:T(8,128)(2,1)}, bf16[3,32,512]{2,1,0:T(8,128)(2,1)S(1)}) custom-call(bf16[32,48,128]{2,1,0:T(8,128)(2,1)S(1)} %all-to-all-done.got, bf16[3,8192,64]{2,1,0:T(8,128)(2,1)} %bitcast.12, bf16[128,512]{1,0:T(8,128)(2,1)S(1)} %copy-done.3, bf16[2,64,512]{2,1,0:T(8,128)(2,1)S(1)} %copy-done.4, bf16[128,512]{1,0:T(8,128)(2,1)S(1)} %copy-done.5), custom_call_target="tpu_custom_call" | custom-call | tf_op jit(solution)/shard_map/mix_forward/pallas_call | solution.py:247
  34.1 0.8 collective-permute-start
  34.9 4.5 %all-to-all-start.1 = ((bf16[32,48,128]{2,1,0:T(8,128)(2,1)}), bf16[32,48,128]{2,1,0:T(8,128)(2,1)S(1)}, u32[]{:S(2)}, u32[]{:S(2)}) async-start(bf16[32,48,128]{2,1,0:T(8,128)(2,1)} %get-tuple-element.20), calls=%async_computation.1 | async-start | bytes 786432 | tf_op jit(solution)/shard_map/all_to_all | solution.py:564
  39.4 0.1 collective-permute-start.1
  39.5 1.4 %collective-permute-done.1.refs_1_ = bf16[2,3,32,512]{3,2,1,0:T(8,128)(2,1)S(1)} collective-permute-done((bf16[2,3,32,512]{3,2,1,0:T(8,128)(2,1)S(1)}, bf16[2,3,32,512]{3,2,1,0:T(8,128)(2,1)S(1)}, u32[]{:S(2)}, u32[]{:S(2)}) %collective-permute-start.1) | collective-permute-done | bytes 196640 | tf_op jit(solution)/shard_map/ppermute | solution.py:570
  40.9 10.0 %all-to-all-done.1.got = bf16[32,48,128]{2,1,0:T(8,128)(2,1)S(1)} async-done(((bf16[32,48,128]{2,1,0:T(8,128)(2,1)}), bf16[32,48,128]{2,1,0:T(8,128)(2,1)S(1)}, u32[]{:S(2)}, u32[]{:S(2)}) %all-to-all-start.1) | async-done | bytes 393248 | tf_op jit(solution)/shard_map/all_to_all | solution.py:564
  51.0 10.7 %activate.1 = (bf16[4096,512]{1,0:T(8,128)(2,1)}, bf16[4096,512]{1,0:T(8,128)(2,1)}, bf16[32,48,128]{2,1,0:T(8,128)(2,1)}) custom-call(bf16[32,48,128]{2,1,0:T(8,128)(2,1)S(1)} %all-to-all-done.1.got, bf16[4096,512]{1,0:T(8,128)(2,1)} %linear.2.lin, bf16[4096,512]{1,0:T(8,128)(2,1)} %bitcast.17, bf16[256,512]{1,0:T(8,128)(2,1)S(1)} %copy-done.1, ...), custom_call_target="tpu_custom_call" | custom-call | tf_op jit(solution)/shard_map/activate/pallas_call | solution.py:388
  61.7 4.1 %all-to-all-start.2 = ((bf16[32,48,128]{2,1,0:T(8,128)(2,1)}), bf16[32,48,128]{2,1,0:T(8,128)(2,1)S(1)}, u32[]{:S(2)}, u32[]{:S(2)}) async-start(bf16[32,48,128]{2,1,0:T(8,128)(2,1)} %get-tuple-element.25), calls=%async_computation.2 | async-start | bytes 786432 | tf_op jit(solution)/shard_map/all_to_all | solution.py:564
  65.8 5.5 %linear.3.lin = bf16[4096,512]{1,0:T(8,128)(2,1)} custom-call(bf16[4096,512]{1,0:T(8,128)(2,1)} %get-tuple-element.26.v, bf16[32,32]{1,0:T(8,128)(2,1)S(1)} %copy-done.7), custom_call_target="tpu_custom_call" | custom-call | tf_op jit(solution)/shard_map/linear/pallas_call | solution.py:475
  71.3 5.8 %all-to-all-done.2.got = bf16[32,48,128]{2,1,0:T(8,128)(2,1)S(1)} async-done(((bf16[32,48,128]{2,1,0:T(8,128)(2,1)}), bf16[32,48,128]{2,1,0:T(8,128)(2,1)S(1)}, u32[]{:S(2)}, u32[]{:S(2)}) %all-to-all-start.2) | async-done | bytes 393248 | tf_op jit(solution)/shard_map/all_to_all | solution.py:564
  77.1 6.2 %mix_backward.1 = (bf16[32,48,128]{2,1,0:T(8,128)(2,1)}, bf16[3,32,512]{2,1,0:T(8,128)(2,1)S(1)}) custom-call(bf16[32,48,128]{2,1,0:T(8,128)(2,1)S(1)} %all-to-all-done.2.got, bf16[3,8192,64]{2,1,0:T(8,128)(2,1)} %bitcast.13, bf16[128,512]{1,0:T(8,128)(2,1)S(1)} %copy-done.3, bf16[512,128]{1,0:T(8,128)(2,1)S(1)} %copy-done.2, bf16[128,256]{1,0:T(8,128)(2,1)S(1)} %copy-done.6), custom_call_target="tpu_custom_call" | custom-call | tf_op jit(solution)/shard_map/mix_backward/pallas_call | solution.py:301
  83.3 0.7 collective-permute-start.2
  84.0 4.5 %all-to-all-start.3 = ((bf16[32,48,128]{2,1,0:T(8,128)(2,1)}), bf16[32,48,128]{2,1,0:T(8,128)(2,1)S(1)}, u32[]{:S(2)}, u32[]{:S(2)}) async-start(bf16[32,48,128]{2,1,0:T(8,128)(2,1)} %get-tuple-element.28), calls=%async_computation.3 | async-start | bytes 786432 | tf_op jit(solution)/shard_map/all_to_all | solution.py:564
  88.6 0.1 collective-permute-start.3
  88.6 1.4 %collective-permute-done.3.refs_3_ = bf16[2,3,32,512]{3,2,1,0:T(8,128)(2,1)S(1)} collective-permute-done((bf16[2,3,32,512]{3,2,1,0:T(8,128)(2,1)S(1)}, bf16[2,3,32,512]{3,2,1,0:T(8,128)(2,1)S(1)}, u32[]{:S(2)}, u32[]{:S(2)}) %collective-permute-start.3) | collective-permute-done | bytes 196640 | tf_op jit(solution)/shard_map/ppermute | solution.py:570
  90.1 6.0 %weight_gradient.1 = f32[3,8192,64]{2,1,0:T(8,128)} custom-call(bf16[2,3,32,512]{3,2,1,0:T(8,128)(2,1)S(1)} %pad_maximum_fusion.refs_0_, bf16[2,3,32,512]{3,2,1,0:T(8,128)(2,1)S(1)} %collective-permute-done.1.refs_1_, bf16[2,3,32,512]{3,2,1,0:T(8,128)(2,1)S(1)} %pad_maximum_fusion.1.refs_2_, bf16[2,3,32,512]{3,2,1,0:T(8,128)(2,1)S(1)} %collective-permute-done.3.refs_3_, ...), custom_call_target="tpu_custom_call" | custom-call | tf_op jit(solution)/shard_map/weight_gradient/pallas_call | solution.py:551
  96.1 3.9 %all-to-all-done.3.got = bf16[32,48,128]{2,1,0:T(8,128)(2,1)S(1)} async-done(((bf16[32,48,128]{2,1,0:T(8,128)(2,1)}), bf16[32,48,128]{2,1,0:T(8,128)(2,1)S(1)}, u32[]{:S(2)}, u32[]{:S(2)}) %all-to-all-start.3) | async-done | bytes 393248 | tf_op jit(solution)/shard_map/all_to_all | solution.py:564
  100.0 5.3 %finish.1 = bf16[4096,512]{1,0:T(8,128)(2,1)} custom-call(bf16[32,48,128]{2,1,0:T(8,128)(2,1)S(1)} %all-to-all-done.3.got, bf16[4096,512]{1,0:T(8,128)(2,1)} %linear.3.lin, bf16[256,512]{1,0:T(8,128)(2,1)S(1)} %copy-done.1, bf16[1024,256]{1,0:T(8,128)(2,1)S(1)} %copy-done), custom_call_target="tpu_custom_call" | custom-call | tf_op jit(solution)/shard_map/finish/pallas_call | solution.py:423
  (20 shorter events, 0.1 us)
Async XLA Ops:
  0.6 16.1 %copy-start.7 = (bf16[32,32]{1,0:T(8,128)(2,1)S(1)}, bf16[32,32]{1,0:T(8,128)(2,1)}, u32[]{:S(2)}) copy-start(bf16[32,32]{1,0:T(8,128)(2,1)} %m.1) | copy-start | bytes 6148
  0.6 16.1 %copy-start.8 = (f32[32]{0:T(128)S(1)}, f32[32]{0:T(128)}, u32[]{:S(2)}) copy-start(f32[32]{0:T(128)} %bias.1) | copy-start | bytes 388
  5.8 23.1 %all-to-all-start = ((bf16[32,48,128]{2,1,0:T(8,128)(2,1)}), bf16[32,48,128]{2,1,0:T(8,128)(2,1)S(1)}, u32[]{:S(2)}, u32[]{:S(2)}) async-start(bf16[32,48,128]{2,1,0:T(8,128)(2,1)} %analyse.1), calls=%async_computation | async-start | bytes 786432 | tf_op jit(solution)/shard_map/all_to_all | solution.py:564
  16.8 12.2 %copy-start.3 = (bf16[128,512]{1,0:T(8,128)(2,1)S(1)}, bf16[128,512]{1,0:T(8,128)(2,1)}, u32[]{:S(2)}) copy-start(bf16[128,512]{1,0:T(8,128)(2,1)} %constant.16.clone.ana_out) | copy-start | bytes 393220
  16.8 12.2 %copy-start.4 = (bf16[2,64,512]{2,1,0:T(8,128)(2,1)S(1)}, bf16[2,64,512]{2,1,0:T(8,128)(2,1)}, u32[]{:S(2)}) copy-start(bf16[2,64,512]{2,1,0:T(8,128)(2,1)} %constant.19.clone.spread) | copy-start | bytes 393220
  16.8 12.2 %copy-start.5 = (bf16[128,512]{1,0:T(8,128)(2,1)S(1)}, bf16[128,512]{1,0:T(8,128)(2,1)}, u32[]{:S(2)}) copy-start(bf16[128,512]{1,0:T(8,128)(2,1)} %constant.17.clone.fwd_out) | copy-start | bytes 393220
  22.9 28.1 %copy-start = (bf16[1024,256]{1,0:T(8,128)(2,1)S(1)}, bf16[1024,256]{1,0:T(8,128)(2,1)}, u32[]{:S(2)}) copy-start(bf16[1024,256]{1,0:T(8,128)(2,1)} %constant.15.clone.middle_h.middle) | copy-start | bytes 1572868
  22.9 28.1 %copy-start.1 = (bf16[256,512]{1,0:T(8,128)(2,1)S(1)}, bf16[256,512]{1,0:T(8,128)(2,1)}, u32[]{:S(2)}) copy-start(bf16[256,512]{1,0:T(8,128)(2,1)} %constant.14.clone.depth_h.depth) | copy-start | bytes 786436
  34.1 5.3 %collective-permute-start = (bf16[3,32,512]{2,1,0:T(8,128)(2,1)S(1)}, bf16[3,32,512]{2,1,0:T(8,128)(2,1)S(1)}, u32[]{:S(2)}, u32[]{:S(2)}) collective-permute-start(bf16[3,32,512]{2,1,0:T(8,128)(2,1)S(1)} %get-tuple-element.21), channel_id=1, source_target_pairs={{0,2},{1,3},{2,0},{3,1},{4,6},{5,7},{6,4},{7,5},{8,10},{9,11},{10,... | collective-permute-start | bytes 294920 | tf_op jit(solution)/shard_map/ppermute | solution.py:568
  34.9 16.1 %all-to-all-start.1 = ((bf16[32,48,128]{2,1,0:T(8,128)(2,1)}), bf16[32,48,128]{2,1,0:T(8,128)(2,1)S(1)}, u32[]{:S(2)}, u32[]{:S(2)}) async-start(bf16[32,48,128]{2,1,0:T(8,128)(2,1)} %get-tuple-element.20), calls=%async_computation.1 | async-start | bytes 786432 | tf_op jit(solution)/shard_map/all_to_all | solution.py:564
  39.4 1.5 %collective-permute-start.1 = (bf16[2,3,32,512]{3,2,1,0:T(8,128)(2,1)S(1)}, bf16[2,3,32,512]{3,2,1,0:T(8,128)(2,1)S(1)}, u32[]{:S(2)}, u32[]{:S(2)}) collective-permute-start(bf16[2,3,32,512]{3,2,1,0:T(8,128)(2,1)S(1)} %pad_maximum_fusion.refs_0_), channel_id=1, source_target_pairs={{0,1},{1,0},{2,3},{3,2},{4,5},{5,4},{6,7},{7,6},{8,9},{9,8},{10,11... | collective-permute-start | bytes 589832 | tf_op jit(solution)/shard_map/ppermute | solution.py:570
  61.7 15.4 %all-to-all-start.2 = ((bf16[32,48,128]{2,1,0:T(8,128)(2,1)}), bf16[32,48,128]{2,1,0:T(8,128)(2,1)S(1)}, u32[]{:S(2)}, u32[]{:S(2)}) async-start(bf16[32,48,128]{2,1,0:T(8,128)(2,1)} %get-tuple-element.25), calls=%async_computation.2 | async-start | bytes 786432 | tf_op jit(solution)/shard_map/all_to_all | solution.py:564
  65.8 11.3 %copy-start.2 = (bf16[512,128]{1,0:T(8,128)(2,1)S(1)}, bf16[512,128]{1,0:T(8,128)(2,1)}, u32[]{:S(2)}) copy-start(bf16[512,128]{1,0:T(8,128)(2,1)} %constant.20.clone.fold.refs_4_) | copy-start | bytes 393220
  65.8 11.3 %copy-start.6 = (bf16[128,256]{1,0:T(8,128)(2,1)S(1)}, bf16[128,256]{1,0:T(8,128)(2,1)}, u32[]{:S(2)}) copy-start(bf16[128,256]{1,0:T(8,128)(2,1)} %constant.18.clone.bwd_out) | copy-start | bytes 196612
  83.3 5.2 %collective-permute-start.2 = (bf16[3,32,512]{2,1,0:T(8,128)(2,1)S(1)}, bf16[3,32,512]{2,1,0:T(8,128)(2,1)S(1)}, u32[]{:S(2)}, u32[]{:S(2)}) collective-permute-start(bf16[3,32,512]{2,1,0:T(8,128)(2,1)S(1)} %get-tuple-element.31), channel_id=1, source_target_pairs={{0,2},{1,3},{2,0},{3,1},{4,6},{5,7},{6,4},{7,5},{8,10},{9,11},{10,... | collective-permute-start | bytes 294920 | tf_op jit(solution)/shard_map/ppermute | solution.py:568
  84.0 16.0 %all-to-all-start.3 = ((bf16[32,48,128]{2,1,0:T(8,128)(2,1)}), bf16[32,48,128]{2,1,0:T(8,128)(2,1)S(1)}, u32[]{:S(2)}, u32[]{:S(2)}) async-start(bf16[32,48,128]{2,1,0:T(8,128)(2,1)} %get-tuple-element.28), calls=%async_computation.3 | async-start | bytes 786432 | tf_op jit(solution)/shard_map/all_to_all | solution.py:564
  88.6 1.5 %collective-permute-start.3 = (bf16[2,3,32,512]{3,2,1,0:T(8,128)(2,1)S(1)}, bf16[2,3,32,512]{3,2,1,0:T(8,128)(2,1)S(1)}, u32[]{:S(2)}, u32[]{:S(2)}) collective-permute-start(bf16[2,3,32,512]{3,2,1,0:T(8,128)(2,1)S(1)} %pad_maximum_fusion.1.refs_2_), channel_id=1, source_target_pairs={{0,1},{1,0},{2,3},{3,2},{4,5},{5,4},{6,7},{7,6},{8,9},{9,8},{10,11... | collective-permute-start | bytes 589832 | tf_op jit(solution)/shard_map/ppermute | solution.py:570

commit v4 on v3

--- a/solution.py
+++ b/solution.py
@@ -564,8 +564,11 @@
     return lax.all_to_all(values, "slab", split_axis=0, concat_axis=0, tiled=True)
 
 
-def everyone(values):
-    far = lax.ppermute(values, "dp", [(i, i ^ 2) for i in range(4)])
+def far_chip(values):
+    return lax.ppermute(values, "dp", [(i, i ^ 2) for i in range(4)])
+
+
+def everyone(values, far):
     both = jnp.stack([values, far])
     near = lax.ppermute(both, "dp", [(i, i ^ 1) for i in range(4)])
     return both, near
@@ -580,15 +583,18 @@
     sent, lin = lax.optimization_barrier((sent, lin))
     back, spec = mix_forward(sent, weights, t)
     got = exchange(back)
-    specs = everyone(spec)
-    got, specs = lax.optimization_barrier((got, specs))
+    got, spec = lax.optimization_barrier((got, spec))
+    far = far_chip(spec)
     act, grad_pre, out = activate(got, lin, cotangent.reshape(4096, ZT), t)
+    out, spec, far = lax.optimization_barrier((out, spec, far))
     sent = exchange(out)
     lin = linear(grad_pre, point_weight, None, True)
     sent, lin = lax.optimization_barrier((sent, lin))
     back, grad_spec = mix_backward(sent, weights, t)
+    far_grad = far_chip(grad_spec)
     got = exchange(back)
-    grads = everyone(grad_spec)
+    specs = everyone(spec, far)
+    grads = everyone(grad_spec, far_grad)
     weight_grad = weight_gradient(specs, grads, t).reshape(NQ, MX, MY, C, 2 * C)
     got, weight_grad = lax.optimization_barrier((got, weight_grad))
     total = finish(got, lin, t)

time: 106 us -> 106 us (level); the launches traced: 105 us -> 104 us
  blocking collectives: 0 us -> 15.3 us
  waiting for transfers between devices: 28.6 us -> 17.2 us
  starting transfers between devices: 25.6 us -> 21.2 us
    all_to_all x0 -> x1, blocking collectives: none -> 15.3 us  [exchange(): lax.all_to_all(values, 'slab', split_axis=0, concat_axis=0, tiled=True)]
    all_to_all x4 -> x3, waiting for transfers between devices: 25.7 us -> 11.8 us  [exchange(): lax.all_to_all(values, 'slab', split_axis=0, concat_axis=0, tiled=True)]
    all_to_all x4 -> x3, starting transfers between devices: 23.9 us -> 19.3 us  [exchange(): lax.all_to_all(values, 'slab', split_axis=0, concat_axis=0, tiled=True)]
    ppermute x2, waiting for transfers between devices: 0.01 us -> 4.06 us  [far_chip(): return lax.ppermute(values, 'dp', [(i, i ^ 2) for i in range(4)])]
    ppermute x2, waiting for transfers between devices: 2.86 us -> 1.42 us  [everyone(): near = lax.ppermute(both, 'dp', [(i, i ^ 1) for i in range(4)])]
  transfers between devices with their start and end apart: 8 -> 7, of which waited for: 6 -> 4; matrix products, arithmetic and copies ran while one was open for 0% -> 0% of each run, Pallas kernels for 17% -> 27%
where the time goes in v4:
time: 106 us; the launch traced here: 104 us
  Pallas kernels  49.3 us (47%)
  starting transfers between devices  21.2 us (20%)
  waiting for transfers between devices  17.2 us (16%)
  blocking collectives  15.3 us (14%)
    all_to_all x3, starting transfers between devices, exchange(): lax.all_to_all(values, 'slab', split_axis=0, concat_axis=0, tiled=True)  19.3 us
    all_to_all x1, blocking collectives, exchange(): lax.all_to_all(values, 'slab', split_axis=0, concat_axis=0, tiled=True)  15.3 us
    all_to_all x3, waiting for transfers between devices, exchange(): lax.all_to_all(values, 'slab', split_axis=0, concat_axis=0, tiled=True)  11.8 us
    pallas_call x2, Pallas kernels, linear(): pl.pallas_call(body, in_specs=[HBM, VM] + [pl.BlockSpec(memory_space=pltp...  11.6 us
    pallas_call x1, Pallas kernels, activate(): pl.pallas_call(activate_body, in_specs=[VM, HBM, HBM, VM, VM], out_specs=...  10.7 us
    pallas_call x1, Pallas kernels, mix_backward(): pl.pallas_call(mix_backward_body, in_specs=[VM, HBM, VM, VM, VM], out_spe...  6.2 us
    pallas_call x1, Pallas kernels, weight_gradient(): pl.pallas_call(weight_body, in_specs=[VM] * 5, out_specs=HBM, out_shape=j...  6.01 us
    pallas_call x1, Pallas kernels, finish(): pl.pallas_call(finish_body, in_specs=[VM, HBM, VM, VM], out_specs=HBM, ou...  5.26 us
  transfers between devices with their start and end apart: 7, of which 4 were waited for; matrix products, arithmetic and copies ran while one was open for 0% of the time, Pallas kernels for 27%

profile of v4, /device:TPU:0, one launch (start us, length us, event | category | flops | bytes accessed | tf_op | source)
XLA Modules:
  0.0 104.2 jit_solution(771532933249680961)
XLA Ops:
  0.7 5.2 %analyse.1 = bf16[32,48,128]{2,1,0:T(8,128)(2,1)} custom-call(bf16[4096,512]{1,0:T(8,128)(2,1)} %bitcast.14, bf16[256,512]{1,0:T(8,128)(2,1)} %constant.14.clone.depth_h.depth, bf16[1024,256]{1,0:T(8,128)(2,1)} %constant.15.clone.middle_h.middle), custom_call_target="tpu_custom_call" | custom-call | tf_op jit(solution)/shard_map/analyse/pallas_call | solution.py:152
  5.8 10.9 %all-to-all-start = ((bf16[32,48,128]{2,1,0:T(8,128)(2,1)}), bf16[32,48,128]{2,1,0:T(8,128)(2,1)S(1)}, u32[]{:S(2)}, u32[]{:S(2)}) async-start(bf16[32,48,128]{2,1,0:T(8,128)(2,1)} %analyse.1), calls=%async_computation | async-start | bytes 786432 | tf_op jit(solution)/shard_map/all_to_all | solution.py:564
  16.8 0.0 copy-start.3
  16.8 0.0 copy-start.5
  16.8 6.1 %linear.2.lin = bf16[4096,512]{1,0:T(8,128)(2,1)} custom-call(bf16[4096,512]{1,0:T(8,128)(2,1)} %bitcast.15, bf16[32,32]{1,0:T(8,128)(2,1)S(1)} %copy-done.7, f32[32]{0:T(128)S(1)} %copy-done.8), custom_call_target="tpu_custom_call" | custom-call | tf_op jit(solution)/shard_map/linear/pallas_call | solution.py:475
  22.9 0.0 copy-start.1
  22.9 6.0 %all-to-all-done.got = bf16[32,48,128]{2,1,0:T(8,128)(2,1)S(1)} async-done(((bf16[32,48,128]{2,1,0:T(8,128)(2,1)}), bf16[32,48,128]{2,1,0:T(8,128)(2,1)S(1)}, u32[]{:S(2)}, u32[]{:S(2)}) %all-to-all-start) | async-done | bytes 393248 | tf_op jit(solution)/shard_map/all_to_all | solution.py:564
  28.9 4.4 %mix_forward.1 = (bf16[32,48,128]{2,1,0:T(8,128)(2,1)S(1)}, bf16[3,32,512]{2,1,0:T(8,128)(2,1)S(1)}) custom-call(bf16[32,48,128]{2,1,0:T(8,128)(2,1)S(1)} %all-to-all-done.got, bf16[3,8192,64]{2,1,0:T(8,128)(2,1)} %bitcast.12, bf16[128,512]{1,0:T(8,128)(2,1)S(1)} %copy-done.3, bf16[2,64,512]{2,1,0:T(8,128)(2,1)S(1)} %copy-done.4, bf16[128,512]{1,0:T(8,128)(2,1)S(1)} %copy-done.5), custom_call_target="tpu_custom_call" | custom-call | tf_op jit(solution)/shard_map/mix_forward/pallas_call | solution.py:247
  33.4 15.3 %all_to_all.20.got = bf16[32,48,128]{2,1,0:T(8,128)(2,1)S(1)} all-to-all(bf16[32,48,128]{2,1,0:T(8,128)(2,1)S(1)} %get-tuple-element.22), channel_id=1, replica_groups=mesh['slab'=32,'dp'=4] {'slab'}, dimensions={0} | all-to-all | bytes 786432 | tf_op jit(solution)/shard_map/all_to_all | solution.py:564
  48.7 0.7 collective-permute-start
  49.4 10.7 %activate.1 = (bf16[4096,512]{1,0:T(8,128)(2,1)}, bf16[4096,512]{1,0:T(8,128)(2,1)}, bf16[32,48,128]{2,1,0:T(8,128)(2,1)}) custom-call(bf16[32,48,128]{2,1,0:T(8,128)(2,1)S(1)} %all_to_all.20.got, bf16[4096,512]{1,0:T(8,128)(2,1)} %linear.2.lin, bf16[4096,512]{1,0:T(8,128)(2,1)} %bitcast.17, bf16[256,512]{1,0:T(8,128)(2,1)S(1)} %copy-done.1, ...), custom_call_target="tpu_custom_call" | custom-call | tf_op jit(solution)/shard_map/activate/pallas_call | solution.py:388
  60.0 4.5 %all-to-all-start.2 = ((bf16[32,48,128]{2,1,0:T(8,128)(2,1)}), bf16[32,48,128]{2,1,0:T(8,128)(2,1)S(1)}, u32[]{:S(2)}, u32[]{:S(2)}) async-start(bf16[32,48,128]{2,1,0:T(8,128)(2,1)} %get-tuple-element.29), calls=%async_computation.2 | async-start | bytes 786432 | tf_op jit(solution)/shard_map/all_to_all | solution.py:564
  64.5 0.0 copy-start.6
  64.5 5.5 %linear.3.lin = bf16[4096,512]{1,0:T(8,128)(2,1)} custom-call(bf16[4096,512]{1,0:T(8,128)(2,1)} %get-tuple-element.30.v, bf16[32,32]{1,0:T(8,128)(2,1)S(1)} %copy-done.7), custom_call_target="tpu_custom_call" | custom-call | tf_op jit(solution)/shard_map/linear/pallas_call | solution.py:475
  70.1 5.7 %all-to-all-done.2.got = bf16[32,48,128]{2,1,0:T(8,128)(2,1)S(1)} async-done(((bf16[32,48,128]{2,1,0:T(8,128)(2,1)}), bf16[32,48,128]{2,1,0:T(8,128)(2,1)S(1)}, u32[]{:S(2)}, u32[]{:S(2)}) %all-to-all-start.2) | async-done | bytes 393248 | tf_op jit(solution)/shard_map/all_to_all | solution.py:564
  75.8 6.2 %mix_backward.1 = (bf16[32,48,128]{2,1,0:T(8,128)(2,1)}, bf16[3,32,512]{2,1,0:T(8,128)(2,1)S(1)}) custom-call(bf16[32,48,128]{2,1,0:T(8,128)(2,1)S(1)} %all-to-all-done.2.got, bf16[3,8192,64]{2,1,0:T(8,128)(2,1)} %bitcast.13, bf16[128,512]{1,0:T(8,128)(2,1)S(1)} %copy-done.3, bf16[512,128]{1,0:T(8,128)(2,1)S(1)} %copy-done.2, bf16[128,256]{1,0:T(8,128)(2,1)S(1)} %copy-done.6), custom_call_target="tpu_custom_call" | custom-call | tf_op jit(solution)/shard_map/mix_backward/pallas_call | solution.py:301
  82.0 3.9 %all-to-all-start.3 = ((bf16[32,48,128]{2,1,0:T(8,128)(2,1)}), bf16[32,48,128]{2,1,0:T(8,128)(2,1)S(1)}, u32[]{:S(2)}, u32[]{:S(2)}) async-start(bf16[32,48,128]{2,1,0:T(8,128)(2,1)} %get-tuple-element.32), calls=%async_computation.3 | async-start | bytes 786432 | tf_op jit(solution)/shard_map/all_to_all | solution.py:564
  85.9 1.0 %collective-permute-start.2 = (bf16[3,32,512]{2,1,0:T(8,128)(2,1)S(1)}, bf16[3,32,512]{2,1,0:T(8,128)(2,1)S(1)}, u32[]{:S(2)}, u32[]{:S(2)}) collective-permute-start(bf16[3,32,512]{2,1,0:T(8,128)(2,1)S(1)} %get-tuple-element.35), channel_id=1, source_target_pairs={{0,2},{1,3},{2,0},{3,1},{4,6},{5,7},{6,4},{7,5},{8,10},{9,11},{10,... | collective-permute-start | bytes 294920 | tf_op jit(solution)/shard_map/ppermute | solution.py:568
  87.0 0.1 collective-permute-start.1
  87.1 4.1 %collective-permute-done.2 = bf16[3,32,512]{2,1,0:T(8,128)(2,1)S(1)} collective-permute-done((bf16[3,32,512]{2,1,0:T(8,128)(2,1)S(1)}, bf16[3,32,512]{2,1,0:T(8,128)(2,1)S(1)}, u32[]{:S(2)}, u32[]{:S(2)}) %collective-permute-start.2) | collective-permute-done | bytes 98336 | tf_op jit(solution)/shard_map/ppermute | solution.py:568
  91.2 0.1 collective-permute-start.3
  91.3 1.4 %collective-permute-done.3.refs_3_ = bf16[2,3,32,512]{3,2,1,0:T(8,128)(2,1)S(1)} collective-permute-done((bf16[2,3,32,512]{3,2,1,0:T(8,128)(2,1)S(1)}, bf16[2,3,32,512]{3,2,1,0:T(8,128)(2,1)S(1)}, u32[]{:S(2)}, u32[]{:S(2)}) %collective-permute-start.3) | collective-permute-done | bytes 196640 | tf_op jit(solution)/shard_map/ppermute | solution.py:573
  92.7 6.0 %weight_gradient.1 = f32[3,8192,64]{2,1,0:T(8,128)} custom-call(bf16[2,3,32,512]{3,2,1,0:T(8,128)(2,1)S(1)} %pad_maximum_fusion.refs_0_, bf16[2,3,32,512]{3,2,1,0:T(8,128)(2,1)S(1)} %collective-permute-done.1.refs_1_, bf16[2,3,32,512]{3,2,1,0:T(8,128)(2,1)S(1)} %pad_maximum_fusion.1.refs_2_, bf16[2,3,32,512]{3,2,1,0:T(8,128)(2,1)S(1)} %collective-permute-done.3.refs_3_, ...), custom_call_target="tpu_custom_call" | custom-call | tf_op jit(solution)/shard_map/weight_gradient/pallas_call | solution.py:551
  98.7 5.3 %finish.1 = bf16[4096,512]{1,0:T(8,128)(2,1)} custom-call(bf16[32,48,128]{2,1,0:T(8,128)(2,1)S(1)} %all-to-all-done.3.got, bf16[4096,512]{1,0:T(8,128)(2,1)} %linear.3.lin, bf16[256,512]{1,0:T(8,128)(2,1)S(1)} %copy-done.1, bf16[1024,256]{1,0:T(8,128)(2,1)S(1)} %copy-done), custom_call_target="tpu_custom_call" | custom-call | tf_op jit(solution)/shard_map/finish/pallas_call | solution.py:423
  (19 shorter events, 0.1 us)
Async XLA Ops:
  0.6 16.1 %copy-start.7 = (bf16[32,32]{1,0:T(8,128)(2,1)S(1)}, bf16[32,32]{1,0:T(8,128)(2,1)}, u32[]{:S(2)}) copy-start(bf16[32,32]{1,0:T(8,128)(2,1)} %m.1) | copy-start | bytes 6148
  0.6 16.1 %copy-start.8 = (f32[32]{0:T(128)S(1)}, f32[32]{0:T(128)}, u32[]{:S(2)}) copy-start(f32[32]{0:T(128)} %bias.1) | copy-start | bytes 388
  5.8 23.1 %all-to-all-start = ((bf16[32,48,128]{2,1,0:T(8,128)(2,1)}), bf16[32,48,128]{2,1,0:T(8,128)(2,1)S(1)}, u32[]{:S(2)}, u32[]{:S(2)}) async-start(bf16[32,48,128]{2,1,0:T(8,128)(2,1)} %analyse.1), calls=%async_computation | async-start | bytes 786432 | tf_op jit(solution)/shard_map/all_to_all | solution.py:564
  16.8 12.2 %copy-start.3 = (bf16[128,512]{1,0:T(8,128)(2,1)S(1)}, bf16[128,512]{1,0:T(8,128)(2,1)}, u32[]{:S(2)}) copy-start(bf16[128,512]{1,0:T(8,128)(2,1)} %constant.16.clone.ana_out) | copy-start | bytes 393220
  16.8 12.2 %copy-start.4 = (bf16[2,64,512]{2,1,0:T(8,128)(2,1)S(1)}, bf16[2,64,512]{2,1,0:T(8,128)(2,1)}, u32[]{:S(2)}) copy-start(bf16[2,64,512]{2,1,0:T(8,128)(2,1)} %constant.19.clone.spread) | copy-start | bytes 393220
  16.8 12.2 %copy-start.5 = (bf16[128,512]{1,0:T(8,128)(2,1)S(1)}, bf16[128,512]{1,0:T(8,128)(2,1)}, u32[]{:S(2)}) copy-start(bf16[128,512]{1,0:T(8,128)(2,1)} %constant.17.clone.fwd_out) | copy-start | bytes 393220
  22.9 26.5 %copy-start = (bf16[1024,256]{1,0:T(8,128)(2,1)S(1)}, bf16[1024,256]{1,0:T(8,128)(2,1)}, u32[]{:S(2)}) copy-start(bf16[1024,256]{1,0:T(8,128)(2,1)} %constant.15.clone.middle_h.middle) | copy-start | bytes 1572868
  22.9 26.4 %copy-start.1 = (bf16[256,512]{1,0:T(8,128)(2,1)S(1)}, bf16[256,512]{1,0:T(8,128)(2,1)}, u32[]{:S(2)}) copy-start(bf16[256,512]{1,0:T(8,128)(2,1)} %constant.14.clone.depth_h.depth) | copy-start | bytes 786436
  48.7 11.4 %collective-permute-start = (bf16[3,32,512]{2,1,0:T(8,128)(2,1)S(1)}, bf16[3,32,512]{2,1,0:T(8,128)(2,1)S(1)}, u32[]{:S(2)}, u32[]{:S(2)}) collective-permute-start(bf16[3,32,512]{2,1,0:T(8,128)(2,1)S(1)} %get-tuple-element.33), channel_id=1, source_target_pairs={{0,2},{1,3},{2,0},{3,1},{4,6},{5,7},{6,4},{7,5},{8,10},{9,11},{10,... | collective-permute-start | bytes 294920 | tf_op jit(solution)/shard_map/ppermute | solution.py:568
  60.0 15.8 %all-to-all-start.2 = ((bf16[32,48,128]{2,1,0:T(8,128)(2,1)}), bf16[32,48,128]{2,1,0:T(8,128)(2,1)S(1)}, u32[]{:S(2)}, u32[]{:S(2)}) async-start(bf16[32,48,128]{2,1,0:T(8,128)(2,1)} %get-tuple-element.29), calls=%async_computation.2 | async-start | bytes 786432 | tf_op jit(solution)/shard_map/all_to_all | solution.py:564
  64.5 11.3 %copy-start.2 = (bf16[512,128]{1,0:T(8,128)(2,1)S(1)}, bf16[512,128]{1,0:T(8,128)(2,1)}, u32[]{:S(2)}) copy-start(bf16[512,128]{1,0:T(8,128)(2,1)} %constant.20.clone.fold.refs_4_) | copy-start | bytes 393220
  64.5 11.3 %copy-start.6 = (bf16[128,256]{1,0:T(8,128)(2,1)S(1)}, bf16[128,256]{1,0:T(8,128)(2,1)}, u32[]{:S(2)}) copy-start(bf16[128,256]{1,0:T(8,128)(2,1)} %constant.18.clone.bwd_out) | copy-start | bytes 196612
  82.0 16.7 %all-to-all-start.3 = ((bf16[32,48,128]{2,1,0:T(8,128)(2,1)}), bf16[32,48,128]{2,1,0:T(8,128)(2,1)S(1)}, u32[]{:S(2)}, u32[]{:S(2)}) async-start(bf16[32,48,128]{2,1,0:T(8,128)(2,1)} %get-tuple-element.32), calls=%async_computation.3 | async-start | bytes 786432 | tf_op jit(solution)/shard_map/all_to_all | solution.py:564
  85.9 5.2 %collective-permute-start.2 = (bf16[3,32,512]{2,1,0:T(8,128)(2,1)S(1)}, bf16[3,32,512]{2,1,0:T(8,128)(2,1)S(1)}, u32[]{:S(2)}, u32[]{:S(2)}) collective-permute-start(bf16[3,32,512]{2,1,0:T(8,128)(2,1)S(1)} %get-tuple-element.35), channel_id=1, source_target_pairs={{0,2},{1,3},{2,0},{3,1},{4,6},{5,7},{6,4},{7,5},{8,10},{9,11},{10,... | collective-permute-start | bytes 294920 | tf_op jit(solution)/shard_map/ppermute | solution.py:568
  87.0 4.3 %collective-permute-start.1 = (bf16[2,3,32,512]{3,2,1,0:T(8,128)(2,1)S(1)}, bf16[2,3,32,512]{3,2,1,0:T(8,128)(2,1)S(1)}, u32[]{:S(2)}, u32[]{:S(2)}) collective-permute-start(bf16[2,3,32,512]{3,2,1,0:T(8,128)(2,1)S(1)} %pad_maximum_fusion.refs_0_), channel_id=1, source_target_pairs={{0,1},{1,0},{2,3},{3,2},{4,5},{5,4},{6,7},{7,6},{8,9},{9,8},{10,11... | collective-permute-start | bytes 589832 | tf_op jit(solution)/shard_map/ppermute | solution.py:573
  91.2 1.5 %collective-permute-start.3 = (bf16[2,3,32,512]{3,2,1,0:T(8,128)(2,1)S(1)}, bf16[2,3,32,512]{3,2,1,0:T(8,128)(2,1)S(1)}, u32[]{:S(2)}, u32[]{:S(2)}) collective-permute-start(bf16[2,3,32,512]{3,2,1,0:T(8,128)(2,1)S(1)} %pad_maximum_fusion.1.refs_2_), channel_id=1, source_target_pairs={{0,1},{1,0},{2,3},{3,2},{4,5},{5,4},{6,7},{7,6},{8,9},{9,8},{10,11... | collective-permute-start | bytes 589832 | tf_op jit(solution)/shard_map/ppermute | solution.py:573

commit v5 on v4

--- a/solution.py
+++ b/solution.py
@@ -408,13 +408,15 @@
     unpack(got, have, turned, middle, tall)
 
     def step(k, carry):
-        chunk_copy(lin, lin_v, sems.at[0], k).wait()
-        at = pl.ds(pl.multiple_of(k * 512, 512), 512)
+        for u in range(2):
+            chunk_copy(lin, lin_v, sems.at[0], k * 2 + u).wait()
+        at = pl.ds(pl.multiple_of(k * 1024, 1024), 1024)
         out_v[at, :] = (dot(tall[at, :], depth[...]) + lin_v[at, :].astype(F32)).astype(BF)
-        chunk_copy(out_v, out, sems.at[1], k).start()
+        for u in range(2):
+            chunk_copy(out_v, out, sems.at[1], k * 2 + u).start()
         return carry
 
-    lax.fori_loop(0, 8, step, 0)
+    lax.fori_loop(0, 4, step, 0)
     for k in range(8):
         chunk_copy(out_v, out, sems.at[1], k).wait()
 

time: 106 us -> 106 us (level)
  no operation moved by 1% of the time
where the time goes in v5:
time: 106 us; the launch traced here: 104 us
  Pallas kernels  49 us (46%)
  starting transfers between devices  21.2 us (20%)
  waiting for transfers between devices  17.2 us (16%)
  blocking collectives  15.3 us (14%)
    all_to_all x3, starting transfers between devices, exchange(): lax.all_to_all(values, 'slab', split_axis=0, concat_axis=0, tiled=True)  19.3 us
    all_to_all x1, blocking collectives, exchange(): lax.all_to_all(values, 'slab', split_axis=0, concat_axis=0, tiled=True)  15.3 us
    all_to_all x3, waiting for transfers between devices, exchange(): lax.all_to_all(values, 'slab', split_axis=0, concat_axis=0, tiled=True)  11.8 us
    pallas_call x2, Pallas kernels, linear(): pl.pallas_call(body, in_specs=[HBM, VM] + [pl.BlockSpec(memory_space=pltp...  11.6 us
    pallas_call x1, Pallas kernels, activate(): pl.pallas_call(activate_body, in_specs=[VM, HBM, HBM, VM, VM], out_specs=...  10.7 us
    pallas_call x1, Pallas kernels, mix_backward(): pl.pallas_call(mix_backward_body, in_specs=[VM, HBM, VM, VM, VM], out_spe...  6.2 us
    pallas_call x1, Pallas kernels, weight_gradient(): pl.pallas_call(weight_body, in_specs=[VM] * 5, out_specs=HBM, out_shape=j...  6.01 us
    pallas_call x1, Pallas kernels, analyse(): pl.pallas_call(analyse_body, in_specs=[HBM, HBM, HBM], out_specs=VM, out_...  5.17 us
  transfers between devices with their start and end apart: 7, of which 4 were waited for; matrix products, arithmetic and copies ran while one was open for 0% of the time, Pallas kernels for 27%

profile of v5, /device:TPU:0, one launch (start us, length us, event | category | flops | bytes accessed | tf_op | source)
XLA Modules:
  0.0 103.8 jit_solution(10390542657393953656)
XLA Ops:
  0.7 5.2 %analyse.1 = bf16[32,48,128]{2,1,0:T(8,128)(2,1)} custom-call(bf16[4096,512]{1,0:T(8,128)(2,1)} %bitcast.14, bf16[256,512]{1,0:T(8,128)(2,1)} %constant.14.clone.depth_h.depth, bf16[1024,256]{1,0:T(8,128)(2,1)} %constant.15.clone.middle_h.middle), custom_call_target="tpu_custom_call" | custom-call | tf_op jit(solution)/shard_map/analyse/pallas_call | solution.py:152
  5.8 10.9 %all-to-all-start = ((bf16[32,48,128]{2,1,0:T(8,128)(2,1)}), bf16[32,48,128]{2,1,0:T(8,128)(2,1)S(1)}, u32[]{:S(2)}, u32[]{:S(2)}) async-start(bf16[32,48,128]{2,1,0:T(8,128)(2,1)} %analyse.1), calls=%async_computation | async-start | bytes 786432 | tf_op jit(solution)/shard_map/all_to_all | solution.py:566
  16.8 0.0 copy-start.3
  16.8 0.0 copy-start.5
  16.8 6.1 %linear.2.lin = bf16[4096,512]{1,0:T(8,128)(2,1)} custom-call(bf16[4096,512]{1,0:T(8,128)(2,1)} %bitcast.15, bf16[32,32]{1,0:T(8,128)(2,1)S(1)} %copy-done.7, f32[32]{0:T(128)S(1)} %copy-done.8), custom_call_target="tpu_custom_call" | custom-call | tf_op jit(solution)/shard_map/linear/pallas_call | solution.py:477
  22.9 0.0 copy-start.1
  22.9 6.0 %all-to-all-done.got = bf16[32,48,128]{2,1,0:T(8,128)(2,1)S(1)} async-done(((bf16[32,48,128]{2,1,0:T(8,128)(2,1)}), bf16[32,48,128]{2,1,0:T(8,128)(2,1)S(1)}, u32[]{:S(2)}, u32[]{:S(2)}) %all-to-all-start) | async-done | bytes 393248 | tf_op jit(solution)/shard_map/all_to_all | solution.py:566
  28.9 4.4 %mix_forward.1 = (bf16[32,48,128]{2,1,0:T(8,128)(2,1)S(1)}, bf16[3,32,512]{2,1,0:T(8,128)(2,1)S(1)}) custom-call(bf16[32,48,128]{2,1,0:T(8,128)(2,1)S(1)} %all-to-all-done.got, bf16[3,8192,64]{2,1,0:T(8,128)(2,1)} %bitcast.12, bf16[128,512]{1,0:T(8,128)(2,1)S(1)} %copy-done.3, bf16[2,64,512]{2,1,0:T(8,128)(2,1)S(1)} %copy-done.4, bf16[128,512]{1,0:T(8,128)(2,1)S(1)} %copy-done.5), custom_call_target="tpu_custom_call" | custom-call | tf_op jit(solution)/shard_map/mix_forward/pallas_call | solution.py:247
  33.4 15.3 %all_to_all.20.got = bf16[32,48,128]{2,1,0:T(8,128)(2,1)S(1)} all-to-all(bf16[32,48,128]{2,1,0:T(8,128)(2,1)S(1)} %get-tuple-element.22), channel_id=1, replica_groups=mesh['slab'=32,'dp'=4] {'slab'}, dimensions={0} | all-to-all | bytes 786432 | tf_op jit(solution)/shard_map/all_to_all | solution.py:566
  48.7 0.7 collective-permute-start
  49.4 10.7 %activate.1 = (bf16[4096,512]{1,0:T(8,128)(2,1)}, bf16[4096,512]{1,0:T(8,128)(2,1)}, bf16[32,48,128]{2,1,0:T(8,128)(2,1)}) custom-call(bf16[32,48,128]{2,1,0:T(8,128)(2,1)S(1)} %all_to_all.20.got, bf16[4096,512]{1,0:T(8,128)(2,1)} %linear.2.lin, bf16[4096,512]{1,0:T(8,128)(2,1)} %bitcast.17, bf16[256,512]{1,0:T(8,128)(2,1)S(1)} %copy-done.1, ...), custom_call_target="tpu_custom_call" | custom-call | tf_op jit(solution)/shard_map/activate/pallas_call | solution.py:388
  60.0 4.5 %all-to-all-start.2 = ((bf16[32,48,128]{2,1,0:T(8,128)(2,1)}), bf16[32,48,128]{2,1,0:T(8,128)(2,1)S(1)}, u32[]{:S(2)}, u32[]{:S(2)}) async-start(bf16[32,48,128]{2,1,0:T(8,128)(2,1)} %get-tuple-element.29), calls=%async_computation.2 | async-start | bytes 786432 | tf_op jit(solution)/shard_map/all_to_all | solution.py:566
  64.5 0.0 copy-start.6
  64.5 5.5 %linear.3.lin = bf16[4096,512]{1,0:T(8,128)(2,1)} custom-call(bf16[4096,512]{1,0:T(8,128)(2,1)} %get-tuple-element.30.v, bf16[32,32]{1,0:T(8,128)(2,1)S(1)} %copy-done.7), custom_call_target="tpu_custom_call" | custom-call | tf_op jit(solution)/shard_map/linear/pallas_call | solution.py:477
  70.1 5.7 %all-to-all-done.2.got = bf16[32,48,128]{2,1,0:T(8,128)(2,1)S(1)} async-done(((bf16[32,48,128]{2,1,0:T(8,128)(2,1)}), bf16[32,48,128]{2,1,0:T(8,128)(2,1)S(1)}, u32[]{:S(2)}, u32[]{:S(2)}) %all-to-all-start.2) | async-done | bytes 393248 | tf_op jit(solution)/shard_map/all_to_all | solution.py:566
  75.8 6.2 %mix_backward.1 = (bf16[32,48,128]{2,1,0:T(8,128)(2,1)}, bf16[3,32,512]{2,1,0:T(8,128)(2,1)S(1)}) custom-call(bf16[32,48,128]{2,1,0:T(8,128)(2,1)S(1)} %all-to-all-done.2.got, bf16[3,8192,64]{2,1,0:T(8,128)(2,1)} %bitcast.13, bf16[128,512]{1,0:T(8,128)(2,1)S(1)} %copy-done.3, bf16[512,128]{1,0:T(8,128)(2,1)S(1)} %copy-done.2, bf16[128,256]{1,0:T(8,128)(2,1)S(1)} %copy-done.6), custom_call_target="tpu_custom_call" | custom-call | tf_op jit(solution)/shard_map/mix_backward/pallas_call | solution.py:301
  82.0 3.9 %all-to-all-start.3 = ((bf16[32,48,128]{2,1,0:T(8,128)(2,1)}), bf16[32,48,128]{2,1,0:T(8,128)(2,1)S(1)}, u32[]{:S(2)}, u32[]{:S(2)}) async-start(bf16[32,48,128]{2,1,0:T(8,128)(2,1)} %get-tuple-element.32), calls=%async_computation.3 | async-start | bytes 786432 | tf_op jit(solution)/shard_map/all_to_all | solution.py:566
  85.9 1.0 %collective-permute-start.2 = (bf16[3,32,512]{2,1,0:T(8,128)(2,1)S(1)}, bf16[3,32,512]{2,1,0:T(8,128)(2,1)S(1)}, u32[]{:S(2)}, u32[]{:S(2)}) collective-permute-start(bf16[3,32,512]{2,1,0:T(8,128)(2,1)S(1)} %get-tuple-element.35), channel_id=1, source_target_pairs={{0,2},{1,3},{2,0},{3,1},{4,6},{5,7},{6,4},{7,5},{8,10},{9,11},{10,... | collective-permute-start | bytes 294920 | tf_op jit(solution)/shard_map/ppermute | solution.py:570
  87.0 0.1 collective-permute-start.1
  87.1 4.1 %collective-permute-done.2 = bf16[3,32,512]{2,1,0:T(8,128)(2,1)S(1)} collective-permute-done((bf16[3,32,512]{2,1,0:T(8,128)(2,1)S(1)}, bf16[3,32,512]{2,1,0:T(8,128)(2,1)S(1)}, u32[]{:S(2)}, u32[]{:S(2)}) %collective-permute-start.2) | collective-permute-done | bytes 98336 | tf_op jit(solution)/shard_map/ppermute | solution.py:570
  91.2 0.1 collective-permute-start.3
  91.3 1.4 %collective-permute-done.3.refs_3_ = bf16[2,3,32,512]{3,2,1,0:T(8,128)(2,1)S(1)} collective-permute-done((bf16[2,3,32,512]{3,2,1,0:T(8,128)(2,1)S(1)}, bf16[2,3,32,512]{3,2,1,0:T(8,128)(2,1)S(1)}, u32[]{:S(2)}, u32[]{:S(2)}) %collective-permute-start.3) | collective-permute-done | bytes 196640 | tf_op jit(solution)/shard_map/ppermute | solution.py:575
  92.7 6.0 %weight_gradient.1 = f32[3,8192,64]{2,1,0:T(8,128)} custom-call(bf16[2,3,32,512]{3,2,1,0:T(8,128)(2,1)S(1)} %pad_maximum_fusion.refs_0_, bf16[2,3,32,512]{3,2,1,0:T(8,128)(2,1)S(1)} %collective-permute-done.1.refs_1_, bf16[2,3,32,512]{3,2,1,0:T(8,128)(2,1)S(1)} %pad_maximum_fusion.1.refs_2_, bf16[2,3,32,512]{3,2,1,0:T(8,128)(2,1)S(1)} %collective-permute-done.3.refs_3_, ...), custom_call_target="tpu_custom_call" | custom-call | tf_op jit(solution)/shard_map/weight_gradient/pallas_call | solution.py:553
  98.7 4.9 %finish.1 = bf16[4096,512]{1,0:T(8,128)(2,1)} custom-call(bf16[32,48,128]{2,1,0:T(8,128)(2,1)S(1)} %all-to-all-done.3.got, bf16[4096,512]{1,0:T(8,128)(2,1)} %linear.3.lin, bf16[256,512]{1,0:T(8,128)(2,1)S(1)} %copy-done.1, bf16[1024,256]{1,0:T(8,128)(2,1)S(1)} %copy-done), custom_call_target="tpu_custom_call" | custom-call | tf_op jit(solution)/shard_map/finish/pallas_call | solution.py:425
  (19 shorter events, 0.1 us)
Async XLA Ops:
  0.6 16.1 %copy-start.7 = (bf16[32,32]{1,0:T(8,128)(2,1)S(1)}, bf16[32,32]{1,0:T(8,128)(2,1)}, u32[]{:S(2)}) copy-start(bf16[32,32]{1,0:T(8,128)(2,1)} %m.1) | copy-start | bytes 6148
  0.6 16.1 %copy-start.8 = (f32[32]{0:T(128)S(1)}, f32[32]{0:T(128)}, u32[]{:S(2)}) copy-start(f32[32]{0:T(128)} %bias.1) | copy-start | bytes 388
  5.8 23.1 %all-to-all-start = ((bf16[32,48,128]{2,1,0:T(8,128)(2,1)}), bf16[32,48,128]{2,1,0:T(8,128)(2,1)S(1)}, u32[]{:S(2)}, u32[]{:S(2)}) async-start(bf16[32,48,128]{2,1,0:T(8,128)(2,1)} %analyse.1), calls=%async_computation | async-start | bytes 786432 | tf_op jit(solution)/shard_map/all_to_all | solution.py:566
  16.8 12.2 %copy-start.3 = (bf16[128,512]{1,0:T(8,128)(2,1)S(1)}, bf16[128,512]{1,0:T(8,128)(2,1)}, u32[]{:S(2)}) copy-start(bf16[128,512]{1,0:T(8,128)(2,1)} %constant.16.clone.ana_out) | copy-start | bytes 393220
  16.8 12.2 %copy-start.4 = (bf16[2,64,512]{2,1,0:T(8,128)(2,1)S(1)}, bf16[2,64,512]{2,1,0:T(8,128)(2,1)}, u32[]{:S(2)}) copy-start(bf16[2,64,512]{2,1,0:T(8,128)(2,1)} %constant.19.clone.spread) | copy-start | bytes 393220
  16.8 12.2 %copy-start.5 = (bf16[128,512]{1,0:T(8,128)(2,1)S(1)}, bf16[128,512]{1,0:T(8,128)(2,1)}, u32[]{:S(2)}) copy-start(bf16[128,512]{1,0:T(8,128)(2,1)} %constant.17.clone.fwd_out) | copy-start | bytes 393220
  22.9 26.5 %copy-start = (bf16[1024,256]{1,0:T(8,128)(2,1)S(1)}, bf16[1024,256]{1,0:T(8,128)(2,1)}, u32[]{:S(2)}) copy-start(bf16[1024,256]{1,0:T(8,128)(2,1)} %constant.15.clone.middle_h.middle) | copy-start | bytes 1572868
  22.9 26.4 %copy-start.1 = (bf16[256,512]{1,0:T(8,128)(2,1)S(1)}, bf16[256,512]{1,0:T(8,128)(2,1)}, u32[]{:S(2)}) copy-start(bf16[256,512]{1,0:T(8,128)(2,1)} %constant.14.clone.depth_h.depth) | copy-start | bytes 786436
  48.7 11.4 %collective-permute-start = (bf16[3,32,512]{2,1,0:T(8,128)(2,1)S(1)}, bf16[3,32,512]{2,1,0:T(8,128)(2,1)S(1)}, u32[]{:S(2)}, u32[]{:S(2)}) collective-permute-start(bf16[3,32,512]{2,1,0:T(8,128)(2,1)S(1)} %get-tuple-element.33), channel_id=1, source_target_pairs={{0,2},{1,3},{2,0},{3,1},{4,6},{5,7},{6,4},{7,5},{8,10},{9,11},{10,... | collective-permute-start | bytes 294920 | tf_op jit(solution)/shard_map/ppermute | solution.py:570
  60.0 15.8 %all-to-all-start.2 = ((bf16[32,48,128]{2,1,0:T(8,128)(2,1)}), bf16[32,48,128]{2,1,0:T(8,128)(2,1)S(1)}, u32[]{:S(2)}, u32[]{:S(2)}) async-start(bf16[32,48,128]{2,1,0:T(8,128)(2,1)} %get-tuple-element.29), calls=%async_computation.2 | async-start | bytes 786432 | tf_op jit(solution)/shard_map/all_to_all | solution.py:566
  64.5 11.3 %copy-start.2 = (bf16[512,128]{1,0:T(8,128)(2,1)S(1)}, bf16[512,128]{1,0:T(8,128)(2,1)}, u32[]{:S(2)}) copy-start(bf16[512,128]{1,0:T(8,128)(2,1)} %constant.20.clone.fold.refs_4_) | copy-start | bytes 393220
  64.5 11.3 %copy-start.6 = (bf16[128,256]{1,0:T(8,128)(2,1)S(1)}, bf16[128,256]{1,0:T(8,128)(2,1)}, u32[]{:S(2)}) copy-start(bf16[128,256]{1,0:T(8,128)(2,1)} %constant.18.clone.bwd_out) | copy-start | bytes 196612
  82.0 16.7 %all-to-all-start.3 = ((bf16[32,48,128]{2,1,0:T(8,128)(2,1)}), bf16[32,48,128]{2,1,0:T(8,128)(2,1)S(1)}, u32[]{:S(2)}, u32[]{:S(2)}) async-start(bf16[32,48,128]{2,1,0:T(8,128)(2,1)} %get-tuple-element.32), calls=%async_computation.3 | async-start | bytes 786432 | tf_op jit(solution)/shard_map/all_to_all | solution.py:566
  85.9 5.2 %collective-permute-start.2 = (bf16[3,32,512]{2,1,0:T(8,128)(2,1)S(1)}, bf16[3,32,512]{2,1,0:T(8,128)(2,1)S(1)}, u32[]{:S(2)}, u32[]{:S(2)}) collective-permute-start(bf16[3,32,512]{2,1,0:T(8,128)(2,1)S(1)} %get-tuple-element.35), channel_id=1, source_target_pairs={{0,2},{1,3},{2,0},{3,1},{4,6},{5,7},{6,4},{7,5},{8,10},{9,11},{10,... | collective-permute-start | bytes 294920 | tf_op jit(solution)/shard_map/ppermute | solution.py:570
  87.0 4.3 %collective-permute-start.1 = (bf16[2,3,32,512]{3,2,1,0:T(8,128)(2,1)S(1)}, bf16[2,3,32,512]{3,2,1,0:T(8,128)(2,1)S(1)}, u32[]{:S(2)}, u32[]{:S(2)}) collective-permute-start(bf16[2,3,32,512]{3,2,1,0:T(8,128)(2,1)S(1)} %pad_maximum_fusion.refs_0_), channel_id=1, source_target_pairs={{0,1},{1,0},{2,3},{3,2},{4,5},{5,4},{6,7},{7,6},{8,9},{9,8},{10,11... | collective-permute-start | bytes 589832 | tf_op jit(solution)/shard_map/ppermute | solution.py:575
  91.2 1.5 %collective-permute-start.3 = (bf16[2,3,32,512]{3,2,1,0:T(8,128)(2,1)S(1)}, bf16[2,3,32,512]{3,2,1,0:T(8,128)(2,1)S(1)}, u32[]{:S(2)}, u32[]{:S(2)}) collective-permute-start(bf16[2,3,32,512]{3,2,1,0:T(8,128)(2,1)S(1)} %pad_maximum_fusion.1.refs_2_), channel_id=1, source_target_pairs={{0,1},{1,0},{2,3},{3,2},{4,5},{5,4},{6,7},{7,6},{8,9},{9,8},{10,11... | collective-permute-start | bytes 589832 | tf_op jit(solution)/shard_map/ppermute | solution.py:575
